TPU v7x, 256 devices: a whole 4x4x8 slice. The times are simulated.
256 devices in a mesh: seq: 32 (over x, y, core), tensor: 8 (over z).
Axes of the slice: x: 4, y: 4, z: 8, core: 2. Of those that a mesh axis runs over, the one named last changes fastest.
Arguments:
- tokens: bfloat16 [16384, 4096], P('seq', 'tensor'), may hold values from -6 to 6
- norm_gain: float32 [4096], replicated, may hold values from 0.1 to 1.9
- w_query: bfloat16 [4096, 4096], P('seq', 'tensor'), may hold values from -0.09375 to 0.09375
- w_key: bfloat16 [4096, 4096], P('seq', 'tensor'), may hold values from -0.09375 to 0.09375
- w_value: bfloat16 [4096, 4096], P('seq', 'tensor'), may hold values from -0.09375 to 0.09375
- out_gain: float32 [4096], P('tensor'), may hold values from 0.1 to 1.9
- carried: float32 [32, 128, 128], P('tensor'), may hold values from -384 to 384
Outputs:
- attended: bfloat16 [16384, 4096], P('seq', 'tensor')
- final_state: float32 [32, 128, 128], P('tensor')
All inputs are finite; a program needn't handle non-finite values.
Results may differ from a plain program's by a relative error of at most 0.009.
Values may be sent and summed in bfloat16 or wider, within the bound.
No kernel may reach another device: no remote copies, remote signals or barrier semaphores. Data moves between devices by JAX's collectives and lax.ppermute only.
A program may use at most 64 MiB of HBM per device.

v0:
```python
import jax
import jax.numpy as jnp
from jax import lax
from jax.sharding import PartitionSpec as P

BLOCK = 512


def add_rows(normed, pieces):
    return tuple((jnp.dot(normed, piece, preferred_element_type=jnp.float32) for piece in pieces))


def shards(tokens, norm_gain, w_query, w_key, w_value, out_gain, carried):
    whole = lax.all_gather(tokens, "tensor", axis=1, tiled=True)
    xf = whole.astype(jnp.float32)
    normed = (xf * lax.rsqrt(jnp.mean(xf * xf, axis=1, keepdims=True) + 1e-05) * norm_gain).astype(
        jnp.bfloat16
    )
    rows = normed.shape[0]
    width = w_query.shape[1]
    size = carried.shape[1]
    heads = width // size
    qsum, ksum, vsum = add_rows(
        normed,
        (
            lax.all_gather(w_query, "seq", axis=0, tiled=True),
            lax.all_gather(w_key, "seq", axis=0, tiled=True),
            lax.all_gather(w_value, "seq", axis=0, tiled=True),
        ),
    )
    blocks = rows // BLOCK
    query = qsum.astype(jnp.bfloat16).reshape(blocks, BLOCK, heads, size)
    key = ksum.astype(jnp.bfloat16).reshape(blocks, BLOCK, heads, size)
    value = vsum.astype(jnp.bfloat16).reshape(blocks, BLOCK, heads, size)
    block_state = jnp.einsum("nthd,nthe->nhde", key, value, preferred_element_type=jnp.float32)
    local_total = jnp.sum(block_state, axis=0)
    zero_state = jnp.zeros_like(local_total)
    mine = lax.axis_index("seq")
    piece = lax.all_gather(
        local_total[None].astype(jnp.bfloat16), "seq", axis=0, tiled=True
    ).astype(jnp.float32)
    where = jnp.arange(piece.shape[0], dtype=jnp.int32)
    keep = (where < mine).astype(jnp.float32)
    before = zero_state + jnp.sum(keep[:, None, None, None] * piece, axis=0)
    total = zero_state + jnp.sum(piece, axis=0)
    start_state = carried + before
    running = jnp.cumsum(block_state, axis=0) - block_state
    priors = start_state[None] + running
    inter = jnp.einsum(
        "nthd,nhde->nthe", query.astype(jnp.float32), priors, precision=lax.Precision.HIGHEST
    )
    causal = jnp.tril(jnp.ones((BLOCK, BLOCK), jnp.float32))
    scores = jnp.einsum("nthd,nshd->nhts", query, key, preferred_element_type=jnp.float32)
    weights = (scores * causal).astype(jnp.bfloat16)
    intra = jnp.einsum("nhts,nshe->nthe", weights, value, preferred_element_type=jnp.float32)
    raw = inter + intra
    normal = (
        raw
        * lax.rsqrt(jnp.mean(raw * raw, axis=3, keepdims=True) + 1e-06)
        * out_gain.reshape(heads, size)
    )
    attended = normal.astype(jnp.bfloat16).reshape(rows, width)
    return (attended, carried + total)


def solution(mesh):
    return jax.shard_map(
        shards,
        mesh=mesh,
        in_specs=(
            P("seq", "tensor"),
            P(),
            P("seq", "tensor"),
            P("seq", "tensor"),
            P("seq", "tensor"),
            P("tensor"),
            P("tensor", None, None),
        ),
        out_specs=(P("seq", "tensor"), P("tensor", None, None)),
        check_vma=False,
    )
```

profile of v0, /device:TPU:1, one launch (start us, length us, event | category | flops | bytes accessed | tf_op | source)
XLA Modules:
  0.0 293.1 jit_solution(6839959478735101237)
XLA Ops:
  7.2 0.0 copy-start.4
  7.2 0.0 all-gather.7.cloned.1.call-start
  7.2 0.7 all-gather.7.cloned.1.call-update
  7.9 0.0 all-gather.9.cloned.1.call-start
  8.0 0.7 all-gather.9.cloned.1.call-update
  8.7 0.0 all-gather.11.cloned.1.call-start
  8.7 0.7 all-gather.11.cloned.1.call-update
  9.4 0.0 all-gather.13.cloned.1.call-start
  9.4 0.5 all-gather.13.cloned.1.call-update
  10.0 0.0 all-gather.15.cloned.1.call-start
  10.0 58.4 %all-gather.7.cloned.1.call-done = bf16[512,4096]{1,0:T(8,128)(2,1)} async-done(((bf16[512,512]{1,0:T(8,128)(2,1)}), bf16[512,4096]{1,0:T(8,128)(2,1)}) %all-gather.7.cloned.1.call-update) | async-done | bytes 4194320 | tf_op jit(solution)/shard_map/all_gather | solution.py:14
  68.5 3.1 %fusion = f32[512]{0:T(512)S(1)} fusion(bf16[512,4096]{1,0:T(8,128)(2,1)} %all-gather.7.cloned.1.call-done), kind=kLoop, calls=%fused_computation.4 | loop fusion | flops 6290944 | bytes 4196352 | tf_op jit(solution)/shard_map/reduce_sum | solution.py:16
  71.5 49.6 %all-gather.9.cloned.1.call-done = bf16[4096,512]{1,0:T(8,128)(2,1)} async-done(((bf16[128,512]{1,0:T(8,128)(2,1)}), bf16[4096,512]{1,0:T(8,128)(2,1)}) %all-gather.9.cloned.1.call-update) | async-done | bytes 4194320 | tf_op jit(solution)/shard_map/all_gather | solution.py:27
  121.2 0.0 copy-done.4
  121.2 5.9 %convolution_convert_fusion.2 = bf16[512,512]{0,1:T(8,128)(2,1)S(1)} fusion(bf16[4096,512]{1,0:T(8,128)(2,1)} %all-gather.9.cloned.1.call-done, bf16[512,4096]{1,0:T(8,128)(2,1)} %all-gather.7.cloned.1.call-done, f32[4096]{0:T(1024)S(1)} %copy-done.4, f32[512]{0:T(512)S(1)} %add_rsqrt_fusion.1), kind=kOutput, calls=%fused_computation.14 | convolution fusion | flops 2156134400 | bytes 8931328 | tf_op jit(solution)/shard_map/dot_general | solution.py:10
  127.1 47.2 %all-gather.11.cloned.1.call-done = bf16[4096,512]{1,0:T(8,128)(2,1)} async-done(((bf16[128,512]{1,0:T(8,128)(2,1)}), bf16[4096,512]{1,0:T(8,128)(2,1)}) %all-gather.11.cloned.1.call-update) | async-done | bytes 4194320 | tf_op jit(solution)/shard_map/all_gather | solution.py:28
  174.3 5.9 %convolution_convert_fusion.1 = bf16[512,512]{0,1:T(8,128)(2,1)S(1)} fusion(bf16[4096,512]{1,0:T(8,128)(2,1)} %all-gather.11.cloned.1.call-done, bf16[512,4096]{1,0:T(8,128)(2,1)} %all-gather.7.cloned.1.call-done, f32[4096]{0:T(1024)S(1)} %copy-done.4, f32[512]{0:T(512)S(1)} %add_rsqrt_fusion.1), kind=kOutput, calls=%fused_computation.13 | convolution fusion | flops 2156134400 | bytes 8931328 | tf_op jit(solution)/shard_map/dot_general | solution.py:10
  180.2 1.0 fusion.13
  181.3 0.0 all-gather.15.cloned.1.call-update
  181.3 0.1 fusion.6
  181.4 45.8 %all-gather.13.cloned.1.call-done = bf16[4096,512]{1,0:T(8,128)(2,1)} async-done(((bf16[128,512]{1,0:T(8,128)(2,1)}), bf16[4096,512]{1,0:T(8,128)(2,1)}) %all-gather.13.cloned.1.call-update) | async-done | bytes 4194320 | tf_op jit(solution)/shard_map/all_gather | solution.py:26
  227.2 6.7 %convolution_convert_fusion = bf16[512,512]{0,1:T(8,128)(2,1)} fusion(bf16[4096,512]{1,0:T(8,128)(2,1)} %all-gather.13.cloned.1.call-done, bf16[512,4096]{1,0:T(8,128)(2,1)} %all-gather.7.cloned.1.call-done, f32[4096]{0:T(1024)S(1)} %copy-done.4, f32[512]{0:T(512)S(1)} %add_rsqrt_fusion.1), kind=kOutput, calls=%fused_computation.12 | convolution fusion | flops 2156134400 | bytes 8931328 | tf_op jit(solution)/shard_map/dot_general | solution.py:10
  234.0 0.0 copy-start.1
  234.0 2.5 fusion.4
  236.5 0.0 copy-start
  236.5 0.0 copy-start.2
  236.5 0.0 copy-start.3
  236.5 43.7 %all-gather.15.cloned.1.call-done = bf16[128,128,128]{2,1,0:T(8,128)(2,1)} async-done(((bf16[4,128,128]{2,1,0:T(8,128)(2,1)}), bf16[128,128,128]{2,1,0:T(8,128)(2,1)}) %all-gather.15.cloned.1.call-update) | async-done | bytes 4194320 | tf_op jit(solution)/shard_map/all_gather | solution.py:39
  280.2 3.6 %convert_reduce_fusion = (f32[4,128,128]{2,1,0:T(8,128)S(1)}, f32[4,128,128]{2,1,0:T(8,128)S(1)}) fusion(bf16[32,4,128,128]{3,2,1,0:T(8,128)(2,1)} %bitcast.20, f32[32]{0:T(128)S(1)} %compare_convert_fusion), kind=kLoop, calls=%fused_computation | loop fusion | flops 8257536 | bytes 4718720 | tf_op jit(solution)/shard_map/reduce_sum | solution.py:45
  283.8 0.0 copy-done.1
  283.8 0.0 copy-done
  283.9 0.0 copy-done.2
  283.9 0.7 multiply_reduce_fusion
  284.6 0.0 copy-done.3
  284.6 0.2 multiply_convert_fusion.1
  284.8 1.0 copy.16
  285.8 0.7 add.52
  (3 shorter events, 0.0 us)
Async XLA Ops:
  7.2 114.0 %copy-start.4 = (f32[4096]{0:T(1024)S(1)}, f32[4096]{0:T(1024)}, u32[]{:S(2)}) copy-start(f32[4096]{0:T(1024)} %param.8) | copy-start | bytes 49156
  7.2 61.3 %all-gather.7.cloned.1.call-start = ((), (), s32[]{:S(2)}) async-start(), calls=%async_computation | async-start | bytes 4718592 | tf_op jit(solution)/shard_map/all_gather | solution.py:14
  7.9 113.2 %all-gather.9.cloned.1.call-start = ((), (), s32[]{:S(2)}) async-start(), calls=%async_computation.1 | async-start | bytes 4325376 | tf_op jit(solution)/shard_map/all_gather | solution.py:27
  8.7 165.6 %all-gather.11.cloned.1.call-start = ((), (), s32[]{:S(2)}) async-start(), calls=%async_computation.2 | async-start | bytes 4325376 | tf_op jit(solution)/shard_map/all_gather | solution.py:28
  9.4 217.8 %all-gather.13.cloned.1.call-start = ((), (), s32[]{:S(2)}) async-start(), calls=%async_computation.3 | async-start | bytes 4325376 | tf_op jit(solution)/shard_map/all_gather | solution.py:26
  10.0 270.2 %all-gather.15.cloned.1.call-start = ((), (), s32[]{:S(2)}) async-start(), calls=%async_computation.4 | async-start | bytes 4325376 | tf_op jit(solution)/shard_map/all_gather | solution.py:39
  234.0 49.9 %copy-start.1 = (f32[4,128,128]{2,1,0:T(8,128)S(1)}, f32[4,128,128]{2,1,0:T(8,128)}, u32[]{:S(2)}) copy-start(f32[4,128,128]{2,1,0:T(8,128)} %param.13) | copy-start | bytes 786436
  236.5 47.4 %copy-start = (bf16[512,512]{0,1:T(8,128)(2,1)S(1)}, bf16[512,512]{0,1:T(8,128)(2,1)}, u32[]{:S(2)}) copy-start(bf16[512,512]{0,1:T(8,128)(2,1)} %convolution_convert_fusion) | copy-start | bytes 1572868
  236.5 47.4 %copy-start.2 = (f32[4,128,128]{2,1,0:T(8,128)S(1)}, f32[4,128,128]{2,1,0:T(8,128)}, u32[]{:S(2)}) copy-start(f32[4,128,128]{2,1,0:T(8,128)} %get-tuple-element.9) | copy-start | bytes 786436
  236.5 48.1 %copy-start.3 = (f32[512]{0:T(512)S(1)}, f32[512]{0:T(512)}, u32[]{:S(2)}) copy-start(f32[512]{0:T(512)} %param.12) | copy-start | bytes 6148
Sparse Core Ops, SparseCore 0:
  9.8 58.6 all-gather.6
  71.0 50.0 all-gather.8
  123.7 50.5 all-gather.10
  176.7 50.5 all-gather.12
  229.6 50.5 all-gather.14
where the time goes:
time: 293 us
  waiting for transfers between devices  247 us (84%)
  matrix products  22.9 us (8%)
  between operations  13.9 us (5%)
  other arithmetic  7.74 us (3%)
    all_gather x1, waiting for transfers between devices, shards(): whole = lax.all_gather(tokens, 'tensor', axis=1, tiled=True)  58.4 us
    all_gather x1, waiting for transfers between devices, shards(): lax.all_gather(w_key, 'seq', axis=0, tiled=True)  49.6 us
    all_gather x1, waiting for transfers between devices, shards(): lax.all_gather(w_value, 'seq', axis=0, tiled=True)  47.2 us
    all_gather x1, waiting for transfers between devices, shards(): lax.all_gather(w_query, 'seq', axis=0, tiled=True)  45.8 us
    all_gather x1, waiting for transfers between devices, shards(): lax.all_gather(local_total[None].astype(jnp.bfloat16), 'seq', axis=0, til...  43.7 us
    dot_general x3, matrix products, add_rows(): jnp.dot(normed, piece, preferred_element_type=jnp.float32)  18.6 us
  transfers between devices with their start and end apart: 5, of which 5 were waited for; matrix products, arithmetic and copies ran while one was open for 9% of the time, Pallas kernels for 0%

commit v1 on v0

v1 whole, which is shorter than its diff:
```python
import functools

import jax
import jax.numpy as jnp
from jax import lax
from jax.experimental import pallas as pl
from jax.experimental.pallas import tpu as pltpu
from jax.sharding import PartitionSpec as P

NX, NY, NC, NZ = 4, 4, 2, 8
BOTH = ("seq", "tensor")
BF, F32 = jnp.bfloat16, jnp.float32
OFFSETS = (0, 1, -1, 2)


def place(x, y, c, z):
    return (((x % NX) * NY + y % NY) * NC + c % NC) * NZ + z % NZ


def move(a, f):
    pairs = [
        (place(x, y, c, z), place(*f(x, y, c, z)))
        for x in range(NX)
        for y in range(NY)
        for c in range(NC)
        for z in range(NZ)
    ]
    return lax.ppermute(a, BOTH, pairs)


def swap(a):
    return move(a, lambda x, y, c, z: (x, y, c + 1, z))


def along_z(a):
    return move(a, lambda x, y, c, z: (x, y, c, z + (1 if c == 0 else -1)))


def first(a, k):
    return move(a, lambda x, y, c, z: (x + k, y, c, z) if c == 0 else (x, y + k, c, z))


def second(a, k):
    return move(a, lambda x, y, c, z: (x, y + k, c, z) if c == 0 else (x + k, y, c, z))


def by_x(a, k):
    return move(a, lambda x, y, c, z: (x + k, y, c, z))


def by_y(a, k):
    return move(a, lambda x, y, c, z: (x, y + k, c, z))


def gather_plane(a):
    stack = jnp.stack([a, first(a, 1), first(a, -1), first(a, 2)])
    right = second(stack, 1)
    left = second(stack, -1)
    far_a = second(right[:2], 1)
    far_b = second(left[2:], -1)
    return stack, right, left, far_a, far_b


def slots(parts):
    out = []
    for part, j, lo in ((0, 0, 0), (1, 1, 0), (2, 2, 0), (3, 3, 0), (4, 3, 2)):
        for n in range(parts[part].shape[0]):
            out.append((part, n, lo + n, j))
    return out


def row_block(c, x, y, i, j):
    d, e = OFFSETS[i], OFFSETS[j]
    qx = jnp.where(c == 0, x - d, x - e)
    qy = jnp.where(c == 0, y - e, y - d)
    return lax.rem(qx + NX, NX) * NY + lax.rem(qy + NY, NY)


def load_tokens(pos, pieces, x_s, sem):
    z, c = pos[2], pos[3]
    sign = 1 - 2 * c
    shifts = [0] + [-k for k in range(1, 5)] + [k for k in range(1, 4)]
    copies = []
    for piece, k in zip(pieces, shifts):
        at = lax.rem(z + sign * k + 2 * NZ, NZ)
        copies.append(
            pltpu.make_async_copy(piece, x_s.at[:, pl.ds(pl.multiple_of(at * 512, 512), 512)], sem)
        )
    return copies


def load_weights(pos, mine, other, w_s, sems):
    x, y, c = pos[0], pos[1], pos[3]
    groups = []
    for which, parts in enumerate((mine, other)):
        owner = c if which == 0 else 1 - c
        copies = []
        for part, n, i, j in slots(parts):
            q = row_block(owner, x, y, i, j)
            copies.append(
                pltpu.make_async_copy(
                    parts[part].at[n],
                    w_s.at[owner, pl.ds(pl.multiple_of(q * 256, 256), 256), :],
                    sems.at[which],
                )
            )
        groups.append(copies)
    return groups


def kv_kernel(pos, *refs):
    pieces, mine, other = refs[:8], refs[8:13], refs[13:18]
    kv_ref, r_ref, s_ref, x_s, w_s, sem_x, sem_w = refs[18:]
    loads = load_tokens(pos, pieces, x_s, sem_x)
    for cp in loads:
        cp.start()
    groups = load_weights(pos, mine, other, w_s, sem_w)
    for group in groups:
        for cp in group:
            cp.start()
    for cp in loads:
        cp.wait()
    total = jnp.zeros((512, 128), F32)
    for b in range(32):
        xb = x_s[:, b * 128 : (b + 1) * 128].astype(F32)
        total = total + xb * xb
    r = lax.rsqrt(jnp.sum(total, axis=1, keepdims=True) * (1.0 / 4096) + 1e-05)
    r_ref[...] = jnp.broadcast_to(r, (512, 128))
    for group in groups:
        for cp in group:
            cp.wait()

    @pl.loop(0, 4)
    def _(i):
        lanes = pl.ds(pl.multiple_of((i % 2) * 256, 256), 256)
        got = jnp.dot(x_s[...], w_s[i // 2, :, lanes], preferred_element_type=F32)
        kv_ref[i // 2, :, lanes] = (got * r_ref[:, :1]).astype(BF)

    @pl.loop(0, 4)
    def _(h):
        lanes = pl.ds(pl.multiple_of(h * 128, 128), 128)
        s_ref[h] = lax.dot_general(
            kv_ref[0, :, lanes],
            kv_ref[1, :, lanes],
            (((0,), (0,)), ((), ())),
            preferred_element_type=F32,
        )


def split_dot(q, m):
    hi = m.astype(BF)
    lo = (m - hi.astype(F32)).astype(BF)
    return jnp.dot(q, hi, preferred_element_type=F32) + jnp.dot(q, lo, preferred_element_type=F32)


def q_kernel(pos, *refs):
    pieces, mine, other = refs[:8], refs[8:13], refs[13:18]
    kv_ref, r_ref, carried_ref, q_ref, raw_ref, x_s, w_s, sem_x, sem_w = refs[18:]
    loads = load_tokens(pos, pieces, x_s, sem_x)
    for cp in loads:
        cp.start()
    groups = load_weights(pos, mine, other, w_s, sem_w)
    for group in groups:
        for cp in group:
            cp.start()
    for cp in loads:
        cp.wait()
    for group in groups:
        for cp in group:
            cp.wait()
    row = lax.broadcasted_iota(jnp.int32, (512, 512), 0)
    col = lax.broadcasted_iota(jnp.int32, (512, 512), 1)

    @pl.loop(0, 2)
    def _(h):
        got = jnp.dot(x_s[...], w_s[h], preferred_element_type=F32)
        q_ref[:, pl.ds(pl.multiple_of(h * 256, 256), 256)] = (got * r_ref[:, :1]).astype(BF)

    @pl.loop(0, 4)
    def _(h):
        lanes = pl.ds(pl.multiple_of(h * 128, 128), 128)
        q = q_ref[:, lanes]
        scores = lax.dot_general(
            q, kv_ref[0, :, lanes], (((1,), (1,)), ((), ())), preferred_element_type=F32
        )
        weights = jnp.where(col <= row, scores, 0.0).astype(BF)
        intra = jnp.dot(weights, kv_ref[1, :, lanes], preferred_element_type=F32)
        raw_ref[:, lanes] = intra + split_dot(q, carried_ref[h])


def out_kernel(q_ref, raw_ref, before_ref, gain_ref, out_ref):
    for h in range(4):
        lanes = slice(h * 128, (h + 1) * 128)
        raw = raw_ref[:, lanes] + split_dot(q_ref[:, lanes], before_ref[h])
        scale = lax.rsqrt(jnp.mean(raw * raw, axis=1, keepdims=True) + 1e-06)
        out_ref[:, lanes] = (raw * scale * gain_ref[:, lanes]).astype(BF)


SMEM = pl.BlockSpec(memory_space=pltpu.SMEM)
ANY = pl.BlockSpec(memory_space=pl.ANY)
VMEM = pl.BlockSpec(memory_space=pltpu.VMEM)
LIMIT = pltpu.CompilerParams(vmem_limit_bytes=40 << 20)


def shards(tokens, norm_gain, w_query, w_key, w_value, out_gain, carried):
    s = lax.axis_index("seq").astype(jnp.int32)
    z = lax.axis_index("tensor").astype(jnp.int32)
    c = s % 2
    y = (s // 2) % NY
    x = s // (2 * NY)
    pos = jnp.stack([x, y, z, c])
    even = c == 0

    sib = swap(tokens)
    own_chain, sib_chain = [tokens], [sib]
    for k in range(3):
        own_chain.append(along_z(own_chain[-1]))
        sib_chain.append(along_z(sib_chain[-1]))
    own_chain.append(along_z(own_chain[-1]))
    pieces = own_chain + [swap(b) for b in sib_chain[1:]]

    g = lax.dynamic_slice(norm_gain, (s * 128,), (128,))[:, None]
    scaled = lambda w: (w.astype(F32) * g).astype(BF)
    wq, wk, wv = scaled(w_query), scaled(w_key), scaled(w_value)
    pick = lambda a, b: jnp.where(even, a, b)
    mine = jnp.concatenate([pick(wk, wv), pick(wq[:, :256], wq[:, 256:])], 1)
    give = jnp.concatenate([pick(wv, wk), pick(wq[:, 256:], wq[:, :256])], 1)
    got = swap(give)
    chip = jnp.concatenate([pick(mine, got), pick(got, mine)], 0)
    kv = gather_plane(chip[:, :512])
    qq = gather_plane(chip[:, 512:])
    kv_other = [swap(a) for a in kv]
    qq_other = [swap(a) for a in qq]

    flops = 2 * 512 * 4096 * 1024
    kv_rows, r, state = pl.pallas_call(
        kv_kernel,
        name="kv",
        out_shape=(
            jax.ShapeDtypeStruct((2, 512, 512), BF),
            jax.ShapeDtypeStruct((512, 128), F32),
            jax.ShapeDtypeStruct((4, 128, 128), F32),
        ),
        in_specs=[SMEM] + [ANY] * 18,
        out_specs=(VMEM,) * 3,
        scratch_shapes=[
            pltpu.VMEM((512, 4096), BF),
            pltpu.VMEM((2, 4096, 512), BF),
            pltpu.SemaphoreType.DMA,
            pltpu.SemaphoreType.DMA((2,)),
        ],
        compiler_params=LIMIT,
        cost_estimate=pl.CostEstimate(flops=flops, bytes_accessed=13 << 20, transcendentals=0),
    )(pos, *pieces, *kv, *kv_other)

    query, raw = pl.pallas_call(
        q_kernel,
        name="q",
        out_shape=(
            jax.ShapeDtypeStruct((512, 512), BF),
            jax.ShapeDtypeStruct((512, 512), F32),
        ),
        in_specs=[SMEM] + [ANY] * 18 + [VMEM] * 3,
        out_specs=(VMEM,) * 2,
        scratch_shapes=[
            pltpu.VMEM((512, 4096), BF),
            pltpu.VMEM((2, 4096, 256), BF),
            pltpu.SemaphoreType.DMA,
            pltpu.SemaphoreType.DMA((2,)),
        ],
        compiler_params=LIMIT,
        cost_estimate=pl.CostEstimate(flops=flops, bytes_accessed=10 << 20, transcendentals=0),
    )(pos, *pieces, *qq, *qq_other, kv_rows, r, carried)

    low, high = state[:2], state[2:]
    part = pick(low, high)
    from_sib = swap(pick(high, low).astype(BF)).astype(F32)
    chip_state = part + from_sib

    def across(a, go, at):
        sent = a.astype(BF)
        near = [go(sent, 1), go(sent, -1), go(sent, 2)]
        b, f, o = [n.astype(F32) for n in near]
        total = (lax.reduce_precision(a, 8, 7) + o) + (b + f)
        before = jnp.where(at >= 1, b, 0.0)
        before = before + jnp.where(at >= 2, o, 0.0) + jnp.where(at == 3, f, 0.0)
        return before, total

    before_y, row_total = across(chip_state, by_y, y)
    before_x, total = across(row_total, by_x, x)
    before = before_x + before_y
    mine_before = before + jnp.where(even, 0.0, from_sib)
    give_before = before + jnp.where(even, part, 0.0)
    both = swap(jnp.stack([give_before, total]))
    order = lambda a, b: jnp.concatenate([pick(a, b), pick(b, a)], 0)
    before_all = order(mine_before, both[0])
    total_all = order(total, both[1])

    attended = pl.pallas_call(
        out_kernel,
        name="out",
        out_shape=jax.ShapeDtypeStruct((512, 512), BF),
        in_specs=[VMEM] * 4,
        out_specs=VMEM,
        compiler_params=LIMIT,
        cost_estimate=pl.CostEstimate(flops=1 << 28, bytes_accessed=2 << 20, transcendentals=0),
    )(query, raw, before_all, out_gain.reshape(1, 512))
    return attended, carried + total_all


def solution(mesh):
    return jax.shard_map(
        shards,
        mesh=mesh,
        in_specs=(
            P("seq", "tensor"),
            P(),
            P("seq", "tensor"),
            P("seq", "tensor"),
            P("seq", "tensor"),
            P("tensor"),
            P("tensor", None, None),
        ),
        out_specs=(P("seq", "tensor"), P("tensor", None, None)),
        check_vma=False,
    )
```

time: 293 us -> 148 us (0.51)
  waiting for transfers between devices: 247 us -> 27.5 us
  starting transfers between devices: 0.19 us -> 69.1 us
  matrix products: 22.9 us -> 0 us
  local copies, waits for them, and re-layouts: 1.03 us -> 23.3 us
  Pallas kernels: 0 us -> 20.6 us
  between operations: 13.9 us -> 1.03 us
    all_gather x5 -> x0, waiting for transfers between devices: 245 us -> none  [the longest x1 58.4 us: shards(): whole = lax.all_gather(tokens, 'tensor', axis=1, tiled=True)]
    ppermute x0 -> x44, starting transfers between devices: none -> 69.1 us  [move(): return lax.ppermute(a, BOTH, pairs)]
    ppermute x0 -> x44, waiting for transfers between devices: none -> 27.5 us  [move(): return lax.ppermute(a, BOTH, pairs)]
    dot_general x6 -> x0, matrix products: 22.9 us -> none  [the longest x3 18.6 us: add_rows(): jnp.dot(normed, piece, preferred_element_type=jnp.float32)]
    pallas_call x0 -> x3, Pallas kernels: none -> 20.6 us  [the longest x1 9.82 us: shards(): pl.pallas_call(kv_kernel, name='kv', out_shape=(jax.ShapeDtypeStruct((2,...]
    unnamed x11 -> x76, local copies, waits for them, and re-layouts: 1.03 us -> 20.4 us
    reduce_sum x2 -> x0, other arithmetic: 6.72 us -> none  [the longest x1 3.64 us: shards(): total = zero_state + jnp.sum(piece, axis=0)]
  transfers between devices with their start and end apart: 5 -> 44, of which waited for: 5 -> 15; matrix products, arithmetic and copies ran while one was open for 9% -> 4% of each run, Pallas kernels for 0% -> 13%
where the time goes in v1:
time: 148 us; the launch traced here: 147 us
  starting transfers between devices  69.1 us (47%)
  waiting for transfers between devices  27.5 us (19%)
  local copies, waits for them, and re-layouts  23.3 us (16%)
  Pallas kernels  20.6 us (14%)
  other arithmetic  5.19 us (4%)
    ppermute x44, starting transfers between devices, move(): return lax.ppermute(a, BOTH, pairs)  69.1 us
    ppermute x44, waiting for transfers between devices, move(): return lax.ppermute(a, BOTH, pairs)  27.5 us
    unnamed x76, local copies, waits for them, and re-layouts  20.4 us
    pallas_call x1, Pallas kernels, shards(): pl.pallas_call(kv_kernel, name='kv', out_shape=(jax.ShapeDtypeStruct((2,...  9.82 us
    pallas_call x1, Pallas kernels, shards(): pl.pallas_call(q_kernel, name='q', out_shape=(jax.ShapeDtypeStruct((512,...  9.35 us
  transfers between devices with their start and end apart: 44, of which 15 were waited for; matrix products, arithmetic and copies ran while one was open for 4% of the time, Pallas kernels for 13%

profile of v1, /device:TPU:1, one launch (start us, length us, event | category | flops | bytes accessed | tf_op | source)
XLA Modules:
  0.0 146.7 jit_solution(6846681312689899212)
XLA Ops:
  1.4 1.0 multiply_convert_fusion
  2.5 0.9 copy-done.36
  3.5 3.3 %collective-permute-start.11 = (bf16[128,768]{1,0:T(8,128)(2,1)S(1)}, bf16[128,768]{1,0:T(8,128)(2,1)S(1)}, u32[]{:S(2)}, u32[]{:S(2)}) collective-permute-start(bf16[128,768]{1,0:T(8,128)(2,1)S(1)} %pad_maximum_fusion.6), channel_id=1, source_target_pairs={{0,8},{1,9},{2,10},{3,11},{4,12},{5,13},{6,14},{7,15},{8,0},{9,1},... | collective-permute-start | bytes 589832 | tf_op jit(solution)/shard_map/ppermute | solution.py:28
  6.9 1.1 collective-permute-done.11
  8.0 1.1 collective-permute-start.25
  10.1 3.5 %collective-permute-done.25 = bf16[256,512]{1,0:T(8,128)(2,1)S(1)} collective-permute-done((bf16[256,512]{1,0:T(8,128)(2,1)S(1)}, bf16[256,512]{1,0:T(8,128)(2,1)S(1)}, u32[]{:S(2)}, u32[]{:S(2)}) %collective-permute-start.25) | collective-permute-done | bytes 262176 | tf_op jit(solution)/shard_map/ppermute | solution.py:28
  13.6 2.5 %collective-permute-done.26 = bf16[256,512]{1,0:T(8,128)(2,1)S(1)} collective-permute-done((bf16[256,512]{1,0:T(8,128)(2,1)S(1)}, bf16[256,512]{1,0:T(8,128)(2,1)S(1)}, u32[]{:S(2)}, u32[]{:S(2)}) %collective-permute-start.26) | collective-permute-done | bytes 262176 | tf_op jit(solution)/shard_map/ppermute | solution.py:28
  16.2 2.8 %collective-permute-done.24 = bf16[256,512]{1,0:T(8,128)(2,1)S(1)} collective-permute-done((bf16[256,512]{1,0:T(8,128)(2,1)S(1)}, bf16[256,512]{1,0:T(8,128)(2,1)S(1)}, u32[]{:S(2)}, u32[]{:S(2)}) %collective-permute-start.24) | collective-permute-done | bytes 262176 | tf_op jit(solution)/shard_map/ppermute | solution.py:28
  19.1 1.0 collective-permute-start.27
  20.1 1.8 %collective-permute-start.28 = (bf16[4,256,512]{2,1,0:T(8,128)(2,1)S(1)}, bf16[4,256,512]{2,1,0:T(8,128)(2,1)}, u32[]{:S(2)}, u32[]{:S(2)}) collective-permute-start(bf16[4,256,512]{2,1,0:T(8,128)(2,1)S(1)} %pad_maximum_fusion.refs_8_), channel_id=1, source_target_pairs={{0,48},{1,49},{2,50},{3,51},{4,52},{5,53},{6,54},{7,55},{8,200},{9... | collective-permute-start | bytes 3145736 | tf_op jit(solution)/shard_map/ppermute | solution.py:28
  22.0 5.7 %collective-permute-start = (bf16[512,512]{1,0:T(8,128)(2,1)S(1)}, bf16[512,512]{1,0:T(8,128)(2,1)S(1)}, u32[]{:S(2)}, u32[]{:S(2)}) collective-permute-start(bf16[512,512]{1,0:T(8,128)(2,1)S(1)} %copy-done.4), channel_id=1, source_target_pairs={{0,1},{1,2},{2,3},{3,4},{4,5},{5,6},{6,7},{7,0},{8,15},{9,8},{10,9... | collective-permute-start | bytes 1572872 | tf_op jit(solution)/shard_map/ppermute | solution.py:28
  27.6 1.1 collective-permute-done.12
  28.7 2.7 %collective-permute-start.31 = (bf16[4,256,512]{2,1,0:T(8,128)(2,1)S(1)}, bf16[4,256,512]{2,1,0:T(8,128)(2,1)S(1)}, u32[]{:S(2)}, u32[]{:S(2)}) collective-permute-start(bf16[4,256,512]{2,1,0:T(8,128)(2,1)S(1)} %pad_maximum_fusion.refs_8_), channel_id=1, source_target_pairs={{0,8},{1,9},{2,10},{3,11},{4,12},{5,13},{6,14},{7,15},{8,0},{9,1},... | collective-permute-start | bytes 3145736 | tf_op jit(solution)/shard_map/ppermute | solution.py:28
  31.4 2.3 %collective-permute-done.refs_1_ = bf16[512,512]{1,0:T(8,128)(2,1)S(1)} collective-permute-done((bf16[512,512]{1,0:T(8,128)(2,1)S(1)}, bf16[512,512]{1,0:T(8,128)(2,1)S(1)}, u32[]{:S(2)}, u32[]{:S(2)}) %collective-permute-start) | collective-permute-done | bytes 524320 | tf_op jit(solution)/shard_map/ppermute | solution.py:28
  33.7 3.4 %collective-permute-start.1 = (bf16[512,512]{1,0:T(8,128)(2,1)S(1)}, bf16[512,512]{1,0:T(8,128)(2,1)S(1)}, u32[]{:S(2)}, u32[]{:S(2)}) collective-permute-start(bf16[512,512]{1,0:T(8,128)(2,1)S(1)} %collective-permute-done.refs_1_), channel_id=1, source_target_pairs={{0,1},{1,2},{2,3},{3,4},{4,5},{5,6},{6,7},{7,0},{8,15},{9,8},{10,9... | collective-permute-start | bytes 1572872 | tf_op jit(solution)/shard_map/ppermute | solution.py:28
  37.7 2.2 %collective-permute-start.13 = (bf16[256,256]{1,0:T(8,128)(2,1)S(1)}, bf16[256,256]{1,0:T(8,128)(2,1)S(1)}, u32[]{:S(2)}, u32[]{:S(2)}) collective-permute-start(bf16[256,256]{1,0:T(8,128)(2,1)S(1)} %pad_maximum_fusion.7), channel_id=1, source_target_pairs={{0,192},{1,193},{2,194},{3,195},{4,196},{5,197},{6,198},{7,199},{8... | collective-permute-start | bytes 393224 | tf_op jit(solution)/shard_map/ppermute | solution.py:28
  40.0 1.1 slice.55
  41.1 2.2 %collective-permute-done.1.refs_2_ = bf16[512,512]{1,0:T(8,128)(2,1)S(1)} collective-permute-done((bf16[512,512]{1,0:T(8,128)(2,1)S(1)}, bf16[512,512]{1,0:T(8,128)(2,1)S(1)}, u32[]{:S(2)}, u32[]{:S(2)}) %collective-permute-start.1) | collective-permute-done | bytes 524320 | tf_op jit(solution)/shard_map/ppermute | solution.py:28
  43.3 3.1 %collective-permute-start.2 = (bf16[512,512]{1,0:T(8,128)(2,1)S(1)}, bf16[512,512]{1,0:T(8,128)(2,1)S(1)}, u32[]{:S(2)}, u32[]{:S(2)}) collective-permute-start(bf16[512,512]{1,0:T(8,128)(2,1)S(1)} %collective-permute-done.1.refs_2_), channel_id=1, source_target_pairs={{0,1},{1,2},{2,3},{3,4},{4,5},{5,6},{6,7},{7,0},{8,15},{9,8},{10,9... | collective-permute-start | bytes 1572872 | tf_op jit(solution)/shard_map/ppermute | solution.py:28
  46.4 0.8 copy-done.10
  47.2 1.7 %collective-permute-done.5 = bf16[512,512]{1,0:T(8,128)(2,1)S(1)} collective-permute-done((bf16[512,512]{1,0:T(8,128)(2,1)S(1)}, bf16[512,512]{1,0:T(8,128)(2,1)S(1)}, u32[]{:S(2)}, u32[]{:S(2)}) %collective-permute-start.5) | collective-permute-done | bytes 524320 | tf_op jit(solution)/shard_map/ppermute | solution.py:28
  48.9 3.1 %collective-permute-start.7 = (bf16[512,512]{1,0:T(8,128)(2,1)S(1)}, bf16[512,512]{1,0:T(8,128)(2,1)S(1)}, u32[]{:S(2)}, u32[]{:S(2)}) collective-permute-start(bf16[512,512]{1,0:T(8,128)(2,1)S(1)} %collective-permute-done.5), channel_id=1, source_target_pairs={{0,1},{1,2},{2,3},{3,4},{4,5},{5,6},{6,7},{7,0},{8,15},{9,8},{10,9... | collective-permute-start | bytes 1572872 | tf_op jit(solution)/shard_map/ppermute | solution.py:28
  52.0 0.9 collective-permute-start.6
  53.3 1.0 copy-done.2
  54.2 2.5 %collective-permute-start.30 = (bf16[2,256,512]{2,1,0:T(8,128)(2,1)S(1)}, bf16[2,256,512]{2,1,0:T(8,128)(2,1)}, u32[]{:S(2)}, u32[]{:S(2)}) collective-permute-start(bf16[2,256,512]{2,1,0:T(8,128)(2,1)S(1)} %slice.55), channel_id=1, source_target_pairs={{0,48},{1,49},{2,50},{3,51},{4,52},{5,53},{6,54},{7,55},{8,200},{9... | collective-permute-start | bytes 1572872 | tf_op jit(solution)/shard_map/ppermute | solution.py:28
  56.7 1.8 %collective-permute-start.32 = (bf16[4,256,512]{2,1,0:T(8,128)(2,1)S(1)}, bf16[4,256,512]{2,1,0:T(8,128)(2,1)}, u32[]{:S(2)}, u32[]{:S(2)}) collective-permute-start(bf16[4,256,512]{2,1,0:T(8,128)(2,1)S(1)} %collective-permute-done.27.refs_9_), channel_id=1, source_target_pairs={{0,8},{1,9},{2,10},{3,11},{4,12},{5,13},{6,14},{7,15},{8,0},{9,1},... | collective-permute-start | bytes 3145736 | tf_op jit(solution)/shard_map/ppermute | solution.py:28
  58.5 1.6 %collective-permute-done.7 = bf16[512,512]{1,0:T(8,128)(2,1)S(1)} collective-permute-done((bf16[512,512]{1,0:T(8,128)(2,1)S(1)}, bf16[512,512]{1,0:T(8,128)(2,1)S(1)}, u32[]{:S(2)}, u32[]{:S(2)}) %collective-permute-start.7) | collective-permute-done | bytes 524320 | tf_op jit(solution)/shard_map/ppermute | solution.py:28
  60.1 3.4 %collective-permute-start.3 = (bf16[512,512]{1,0:T(8,128)(2,1)S(1)}, bf16[512,512]{1,0:T(8,128)(2,1)S(1)}, u32[]{:S(2)}, u32[]{:S(2)}) collective-permute-start(bf16[512,512]{1,0:T(8,128)(2,1)S(1)} %collective-permute-done.2.refs_3_), channel_id=1, source_target_pairs={{0,1},{1,2},{2,3},{3,4},{4,5},{5,6},{6,7},{7,0},{8,15},{9,8},{10,9... | collective-permute-start | bytes 1572872 | tf_op jit(solution)/shard_map/ppermute | solution.py:28
  64.3 0.8 copy-done.16
  65.8 3.8 %collective-permute-done.3.refs_4_ = bf16[512,512]{1,0:T(8,128)(2,1)S(1)} collective-permute-done((bf16[512,512]{1,0:T(8,128)(2,1)S(1)}, bf16[512,512]{1,0:T(8,128)(2,1)S(1)}, u32[]{:S(2)}, u32[]{:S(2)}) %collective-permute-start.3) | collective-permute-done | bytes 524320 | tf_op jit(solution)/shard_map/ppermute | solution.py:28
  70.5 4.8 %collective-permute-start.34 = (bf16[2,256,512]{2,1,0:T(8,128)(2,1)S(1)}, bf16[2,256,512]{2,1,0:T(8,128)(2,1)}, u32[]{:S(2)}, u32[]{:S(2)}) collective-permute-start(bf16[2,256,512]{2,1,0:T(8,128)(2,1)S(1)} %collective-permute-done.29.refs_11_), channel_id=1, source_target_pairs={{0,8},{1,9},{2,10},{3,11},{4,12},{5,13},{6,14},{7,15},{8,0},{9,1},... | collective-permute-start | bytes 1572872 | tf_op jit(solution)/shard_map/ppermute | solution.py:28
  76.1 4.1 %collective-permute-start.35 = (bf16[2,256,512]{2,1,0:T(8,128)(2,1)}, bf16[2,256,512]{2,1,0:T(8,128)(2,1)}, u32[]{:S(2)}, u32[]{:S(2)}) collective-permute-start(bf16[2,256,512]{2,1,0:T(8,128)(2,1)} %collective-permute-done.30.refs_12_), channel_id=1, source_target_pairs={{0,8},{1,9},{2,10},{3,11},{4,12},{5,13},{6,14},{7,15},{8,0},{9,1},... | collective-permute-start | bytes 1572872 | tf_op jit(solution)/shard_map/ppermute | solution.py:28
  80.2 0.9 copy-done.22
  81.2 1.0 pad_maximum_fusion.1.refs_8_
  82.7 2.6 %collective-permute-start.16 = (bf16[4,256,256]{2,1,0:T(8,128)(2,1)S(1)}, bf16[4,256,256]{2,1,0:T(8,128)(2,1)}, u32[]{:S(2)}, u32[]{:S(2)}) collective-permute-start(bf16[4,256,256]{2,1,0:T(8,128)(2,1)S(1)} %pad_maximum_fusion.1.refs_8_), channel_id=1, source_target_pairs={{0,48},{1,49},{2,50},{3,51},{4,52},{5,53},{6,54},{7,55},{8,200},{9... | collective-permute-start | bytes 1572872 | tf_op jit(solution)/shard_map/ppermute | solution.py:28
  85.3 1.0 copy-done.5
  86.3 1.0 copy-done.8
  87.4 1.0 copy-done.11
  88.4 1.0 copy-done.14
  89.5 1.0 copy-done.17
  90.5 1.0 copy-done.20
  91.5 1.0 copy-done.23
  92.6 1.0 copy-done.26
  93.6 9.8 %kv.1 = (bf16[2,512,512]{2,1,0:T(8,128)(2,1)S(1)}, f32[512,128]{1,0:T(8,128)S(1)}, f32[4,128,128]{2,1,0:T(8,128)S(1)}) custom-call(s32[4]{0:T(128)S(1)} %pad_add_fusion.pos, bf16[512,512]{1,0:T(8,128)(2,1)S(1)} %copy-done.5, bf16[512,512]{1,0:T(8,128)(2,1)S(1)} %copy-done.8, bf16[512,512]{1,0:T(8,128)(2,1)S(1)} %copy-done.11, ...), custom_call_target="tpu_custom_call" | custom-call | flops 4294967296 | bytes 13631488 | tf_op jit(solution)/shard_map/kv/pallas_call | solution.py:236
  104.2 0.9 collective-permute-start.36
  105.1 0.9 collective-permute-done.36
  106.0 1.4 collective-permute-start.37
  107.7 2.3 %collective-permute-start.39 = (bf16[2,128,128]{2,1,0:T(8,128)(2,1)S(1)}, bf16[2,128,128]{2,1,0:T(8,128)(2,1)S(1)}, u32[]{:S(2)}, u32[]{:S(2)}) collective-permute-start(bf16[2,128,128]{2,1,0:T(8,128)(2,1)S(1)} %get-tuple-element.14), channel_id=1, source_target_pairs={{0,48},{1,49},{2,50},{3,51},{4,52},{5,53},{6,54},{7,55},{8,56},{9,... | collective-permute-start | bytes 196616 | tf_op jit(solution)/shard_map/ppermute | solution.py:28
  110.2 1.1 collective-permute-start.19
  111.2 1.0 slice.53
  112.3 2.4 %collective-permute-start.18 = (bf16[2,256,256]{2,1,0:T(8,128)(2,1)S(1)}, bf16[2,256,256]{2,1,0:T(8,128)(2,1)}, u32[]{:S(2)}, u32[]{:S(2)}) collective-permute-start(bf16[2,256,256]{2,1,0:T(8,128)(2,1)S(1)} %slice.53), channel_id=1, source_target_pairs={{0,48},{1,49},{2,50},{3,51},{4,52},{5,53},{6,54},{7,55},{8,200},{9... | collective-permute-start | bytes 786440 | tf_op jit(solution)/shard_map/ppermute | solution.py:28
  114.6 0.9 collective-permute-start.20
  116.9 1.1 collective-permute-done.18.refs_12_
  118.0 2.2 %collective-permute-start.41 = (bf16[2,128,128]{2,1,0:T(8,128)(2,1)}, bf16[2,128,128]{2,1,0:T(8,128)(2,1)}, u32[]{:S(2)}, u32[]{:S(2)}) collective-permute-start(bf16[2,128,128]{2,1,0:T(8,128)(2,1)} %fusion.13), channel_id=1, source_target_pairs={{0,128},{1,129},{2,130},{3,131},{4,132},{5,133},{6,134},{7,135},{8... | collective-permute-start | bytes 196616 | tf_op jit(solution)/shard_map/ppermute | solution.py:28
  120.2 1.3 collective-permute-done.40
  122.1 0.8 collective-permute-done.41
  122.9 3.1 %collective-permute-start.22 = (bf16[2,256,256]{2,1,0:T(8,128)(2,1)S(1)}, bf16[2,256,256]{2,1,0:T(8,128)(2,1)S(1)}, u32[]{:S(2)}, u32[]{:S(2)}) collective-permute-start(bf16[2,256,256]{2,1,0:T(8,128)(2,1)S(1)} %collective-permute-done.17.refs_11_), channel_id=1, source_target_pairs={{0,8},{1,9},{2,10},{3,11},{4,12},{5,13},{6,14},{7,15},{8,0},{9,1},... | collective-permute-start | bytes 786440 | tf_op jit(solution)/shard_map/ppermute | solution.py:28
  126.0 3.1 %collective-permute-start.23 = (bf16[2,256,256]{2,1,0:T(8,128)(2,1)}, bf16[2,256,256]{2,1,0:T(8,128)(2,1)S(1)}, u32[]{:S(2)}, u32[]{:S(2)}) collective-permute-start(bf16[2,256,256]{2,1,0:T(8,128)(2,1)} %collective-permute-done.18.refs_12_), channel_id=1, source_target_pairs={{0,8},{1,9},{2,10},{3,11},{4,12},{5,13},{6,14},{7,15},{8,0},{9,1},... | collective-permute-start | bytes 786440 | tf_op jit(solution)/shard_map/ppermute | solution.py:28
  129.1 1.2 add_bitcast_fusion
  131.2 1.0 copy-done.24
  132.2 1.2 copy-done.28
  133.5 0.9 copy-done.30
  134.4 9.3 %q.1 = (bf16[512,512]{1,0:T(8,128)(2,1)S(1)}, f32[512,512]{1,0:T(8,128)S(1)}) custom-call(s32[4]{0:T(128)S(1)} %pad_add_fusion.pos, bf16[512,512]{1,0:T(8,128)(2,1)S(1)} %copy-done.6, bf16[512,512]{1,0:T(8,128)(2,1)S(1)} %copy-done.9, bf16[512,512]{1,0:T(8,128)(2,1)S(1)} %copy-done.12, bf16[512,512]{1,0:T(8,128)(2,1)S(1)} %copy-done.15, ...), custom_call_target="tpu_custom_call" | custom-call | flops 4294967296 | bytes 10485760 | tf_op jit(solution)/shard_map/q/pallas_call | solution.py:256
  145.3 1.4 out.1
  (125 shorter events, 12.6 us)
Async XLA Ops:
  3.5 4.4 %collective-permute-start.11 = (bf16[128,768]{1,0:T(8,128)(2,1)S(1)}, bf16[128,768]{1,0:T(8,128)(2,1)S(1)}, u32[]{:S(2)}, u32[]{:S(2)}) collective-permute-start(bf16[128,768]{1,0:T(8,128)(2,1)S(1)} %pad_maximum_fusion.6), channel_id=1, source_target_pairs={{0,8},{1,9},{2,10},{3,11},{4,12},{5,13},{6,14},{7,15},{8,0},{9,1},... | collective-permute-start | bytes 589832 | tf_op jit(solution)/shard_map/ppermute | solution.py:28
  8.0 5.6 %collective-permute-start.25 = (bf16[256,512]{1,0:T(8,128)(2,1)S(1)}, bf16[256,512]{1,0:T(8,128)(2,1)S(1)}, u32[]{:S(2)}, u32[]{:S(2)}) collective-permute-start(bf16[256,512]{1,0:T(8,128)(2,1)S(1)} %pad_maximum_fusion.2), channel_id=1, source_target_pairs={{0,192},{1,193},{2,194},{3,195},{4,196},{5,197},{6,198},{7,199},{8... | collective-permute-start | bytes 786440 | tf_op jit(solution)/shard_map/ppermute | solution.py:28
  9.1 7.1 %collective-permute-start.26 = (bf16[256,512]{1,0:T(8,128)(2,1)S(1)}, bf16[256,512]{1,0:T(8,128)(2,1)S(1)}, u32[]{:S(2)}, u32[]{:S(2)}) collective-permute-start(bf16[256,512]{1,0:T(8,128)(2,1)S(1)} %pad_maximum_fusion.2), channel_id=1, source_target_pairs={{0,128},{1,129},{2,130},{3,131},{4,132},{5,133},{6,134},{7,135},{8... | collective-permute-start | bytes 786440 | tf_op jit(solution)/shard_map/ppermute | solution.py:28
  9.5 9.5 %collective-permute-start.24 = (bf16[256,512]{1,0:T(8,128)(2,1)S(1)}, bf16[256,512]{1,0:T(8,128)(2,1)S(1)}, u32[]{:S(2)}, u32[]{:S(2)}) collective-permute-start(bf16[256,512]{1,0:T(8,128)(2,1)S(1)} %pad_maximum_fusion.2), channel_id=1, source_target_pairs={{0,64},{1,65},{2,66},{3,67},{4,68},{5,69},{6,70},{7,71},{8,24},{9,... | collective-permute-start | bytes 786440 | tf_op jit(solution)/shard_map/ppermute | solution.py:28
  19.1 2.9 %copy-start.4 = (bf16[512,512]{1,0:T(8,128)(2,1)S(1)}, bf16[512,512]{1,0:T(8,128)(2,1)}, u32[]{:S(2)}) copy-start(bf16[512,512]{1,0:T(8,128)(2,1)} %refs_0_.3) | copy-start | bytes 1572868
  19.1 18.6 %collective-permute-start.27 = (bf16[4,256,512]{2,1,0:T(8,128)(2,1)S(1)}, bf16[4,256,512]{2,1,0:T(8,128)(2,1)S(1)}, u32[]{:S(2)}, u32[]{:S(2)}) collective-permute-start(bf16[4,256,512]{2,1,0:T(8,128)(2,1)S(1)} %pad_maximum_fusion.refs_8_), channel_id=1, source_target_pairs={{0,16},{1,17},{2,18},{3,19},{4,20},{5,21},{6,22},{7,23},{8,72},{9,... | collective-permute-start | bytes 3145736 | tf_op jit(solution)/shard_map/ppermute | solution.py:28
  20.1 19.8 %collective-permute-start.28 = (bf16[4,256,512]{2,1,0:T(8,128)(2,1)S(1)}, bf16[4,256,512]{2,1,0:T(8,128)(2,1)}, u32[]{:S(2)}, u32[]{:S(2)}) collective-permute-start(bf16[4,256,512]{2,1,0:T(8,128)(2,1)S(1)} %pad_maximum_fusion.refs_8_), channel_id=1, source_target_pairs={{0,48},{1,49},{2,50},{3,51},{4,52},{5,53},{6,54},{7,55},{8,200},{9... | collective-permute-start | bytes 3145736 | tf_op jit(solution)/shard_map/ppermute | solution.py:28
  21.9 6.8 %collective-permute-start.12 = (bf16[256,256]{1,0:T(8,128)(2,1)S(1)}, bf16[256,256]{1,0:T(8,128)(2,1)S(1)}, u32[]{:S(2)}, u32[]{:S(2)}) collective-permute-start(bf16[256,256]{1,0:T(8,128)(2,1)S(1)} %pad_maximum_fusion.7), channel_id=1, source_target_pairs={{0,64},{1,65},{2,66},{3,67},{4,68},{5,69},{6,70},{7,71},{8,24},{9,... | collective-permute-start | bytes 393224 | tf_op jit(solution)/shard_map/ppermute | solution.py:28
  22.0 11.8 %collective-permute-start = (bf16[512,512]{1,0:T(8,128)(2,1)S(1)}, bf16[512,512]{1,0:T(8,128)(2,1)S(1)}, u32[]{:S(2)}, u32[]{:S(2)}) collective-permute-start(bf16[512,512]{1,0:T(8,128)(2,1)S(1)} %copy-done.4), channel_id=1, source_target_pairs={{0,1},{1,2},{2,3},{3,4},{4,5},{5,6},{6,7},{7,0},{8,15},{9,8},{10,9... | collective-permute-start | bytes 1572872 | tf_op jit(solution)/shard_map/ppermute | solution.py:28
  27.6 9.5 %collective-permute-start.4 = (bf16[512,512]{1,0:T(8,128)(2,1)S(1)}, bf16[512,512]{1,0:T(8,128)(2,1)S(1)}, u32[]{:S(2)}, u32[]{:S(2)}) collective-permute-start(bf16[512,512]{1,0:T(8,128)(2,1)S(1)} %copy-done.4), channel_id=1, source_target_pairs={{0,8},{1,9},{2,10},{3,11},{4,12},{5,13},{6,14},{7,15},{8,0},{9,1},... | collective-permute-start | bytes 1572872 | tf_op jit(solution)/shard_map/ppermute | solution.py:28
  28.7 24.6 %collective-permute-start.31 = (bf16[4,256,512]{2,1,0:T(8,128)(2,1)S(1)}, bf16[4,256,512]{2,1,0:T(8,128)(2,1)S(1)}, u32[]{:S(2)}, u32[]{:S(2)}) collective-permute-start(bf16[4,256,512]{2,1,0:T(8,128)(2,1)S(1)} %pad_maximum_fusion.refs_8_), channel_id=1, source_target_pairs={{0,8},{1,9},{2,10},{3,11},{4,12},{5,13},{6,14},{7,15},{8,0},{9,1},... | collective-permute-start | bytes 3145736 | tf_op jit(solution)/shard_map/ppermute | solution.py:28
  33.7 7.3 %copy-start.7 = (bf16[512,512]{1,0:T(8,128)(2,1)}, bf16[512,512]{1,0:T(8,128)(2,1)S(1)}, u32[]{:S(2)}) copy-start(bf16[512,512]{1,0:T(8,128)(2,1)S(1)} %collective-permute-done.refs_1_) | copy-start | bytes 1572868
  33.7 9.5 %collective-permute-start.1 = (bf16[512,512]{1,0:T(8,128)(2,1)S(1)}, bf16[512,512]{1,0:T(8,128)(2,1)S(1)}, u32[]{:S(2)}, u32[]{:S(2)}) collective-permute-start(bf16[512,512]{1,0:T(8,128)(2,1)S(1)} %collective-permute-done.refs_1_), channel_id=1, source_target_pairs={{0,1},{1,2},{2,3},{3,4},{4,5},{5,6},{6,7},{7,0},{8,15},{9,8},{10,9... | collective-permute-start | bytes 1572872 | tf_op jit(solution)/shard_map/ppermute | solution.py:28
  37.1 11.7 %collective-permute-start.5 = (bf16[512,512]{1,0:T(8,128)(2,1)S(1)}, bf16[512,512]{1,0:T(8,128)(2,1)S(1)}, u32[]{:S(2)}, u32[]{:S(2)}) collective-permute-start(bf16[512,512]{1,0:T(8,128)(2,1)S(1)} %collective-permute-done.4), channel_id=1, source_target_pairs={{0,1},{1,2},{2,3},{3,4},{4,5},{5,6},{6,7},{7,0},{8,15},{9,8},{10,9... | collective-permute-start | bytes 1572872 | tf_op jit(solution)/shard_map/ppermute | solution.py:28
  37.7 14.3 %collective-permute-start.13 = (bf16[256,256]{1,0:T(8,128)(2,1)S(1)}, bf16[256,256]{1,0:T(8,128)(2,1)S(1)}, u32[]{:S(2)}, u32[]{:S(2)}) collective-permute-start(bf16[256,256]{1,0:T(8,128)(2,1)S(1)} %pad_maximum_fusion.7), channel_id=1, source_target_pairs={{0,192},{1,193},{2,194},{3,195},{4,196},{5,197},{6,198},{7,199},{8... | collective-permute-start | bytes 393224 | tf_op jit(solution)/shard_map/ppermute | solution.py:28
  39.9 13.0 %collective-permute-start.14 = (bf16[256,256]{1,0:T(8,128)(2,1)S(1)}, bf16[256,256]{1,0:T(8,128)(2,1)}, u32[]{:S(2)}, u32[]{:S(2)}) collective-permute-start(bf16[256,256]{1,0:T(8,128)(2,1)S(1)} %pad_maximum_fusion.7), channel_id=1, source_target_pairs={{0,128},{1,129},{2,130},{3,131},{4,132},{5,133},{6,134},{7,135},{8... | collective-permute-start | bytes 393224 | tf_op jit(solution)/shard_map/ppermute | solution.py:28
  43.3 13.4 %collective-permute-start.2 = (bf16[512,512]{1,0:T(8,128)(2,1)S(1)}, bf16[512,512]{1,0:T(8,128)(2,1)S(1)}, u32[]{:S(2)}, u32[]{:S(2)}) collective-permute-start(bf16[512,512]{1,0:T(8,128)(2,1)S(1)} %collective-permute-done.1.refs_2_), channel_id=1, source_target_pairs={{0,1},{1,2},{2,3},{3,4},{4,5},{5,6},{6,7},{7,0},{8,15},{9,8},{10,9... | collective-permute-start | bytes 1572872 | tf_op jit(solution)/shard_map/ppermute | solution.py:28
  48.9 11.2 %collective-permute-start.7 = (bf16[512,512]{1,0:T(8,128)(2,1)S(1)}, bf16[512,512]{1,0:T(8,128)(2,1)S(1)}, u32[]{:S(2)}, u32[]{:S(2)}) collective-permute-start(bf16[512,512]{1,0:T(8,128)(2,1)S(1)} %collective-permute-done.5), channel_id=1, source_target_pairs={{0,1},{1,2},{2,3},{3,4},{4,5},{5,6},{6,7},{7,0},{8,15},{9,8},{10,9... | collective-permute-start | bytes 1572872 | tf_op jit(solution)/shard_map/ppermute | solution.py:28
  52.0 12.3 %collective-permute-start.6 = (bf16[512,512]{1,0:T(8,128)(2,1)S(1)}, bf16[512,512]{1,0:T(8,128)(2,1)S(1)}, u32[]{:S(2)}, u32[]{:S(2)}) collective-permute-start(bf16[512,512]{1,0:T(8,128)(2,1)S(1)} %collective-permute-done.5), channel_id=1, source_target_pairs={{0,8},{1,9},{2,10},{3,11},{4,12},{5,13},{6,14},{7,15},{8,0},{9,1},... | collective-permute-start | bytes 1572872 | tf_op jit(solution)/shard_map/ppermute | solution.py:28
  52.9 12.3 %collective-permute-start.29 = (bf16[2,256,512]{2,1,0:T(8,128)(2,1)S(1)}, bf16[2,256,512]{2,1,0:T(8,128)(2,1)S(1)}, u32[]{:S(2)}, u32[]{:S(2)}) collective-permute-start(bf16[2,256,512]{2,1,0:T(8,128)(2,1)S(1)} %slice.54), channel_id=1, source_target_pairs={{0,16},{1,17},{2,18},{3,19},{4,20},{5,21},{6,22},{7,23},{8,72},{9,... | collective-permute-start | bytes 1572872 | tf_op jit(solution)/shard_map/ppermute | solution.py:28
  54.2 11.5 %collective-permute-start.30 = (bf16[2,256,512]{2,1,0:T(8,128)(2,1)S(1)}, bf16[2,256,512]{2,1,0:T(8,128)(2,1)}, u32[]{:S(2)}, u32[]{:S(2)}) collective-permute-start(bf16[2,256,512]{2,1,0:T(8,128)(2,1)S(1)} %slice.55), channel_id=1, source_target_pairs={{0,48},{1,49},{2,50},{3,51},{4,52},{5,53},{6,54},{7,55},{8,200},{9... | collective-permute-start | bytes 1572872 | tf_op jit(solution)/shard_map/ppermute | solution.py:28
  56.7 28.6 %collective-permute-start.32 = (bf16[4,256,512]{2,1,0:T(8,128)(2,1)S(1)}, bf16[4,256,512]{2,1,0:T(8,128)(2,1)}, u32[]{:S(2)}, u32[]{:S(2)}) collective-permute-start(bf16[4,256,512]{2,1,0:T(8,128)(2,1)S(1)} %collective-permute-done.27.refs_9_), channel_id=1, source_target_pairs={{0,8},{1,9},{2,10},{3,11},{4,12},{5,13},{6,14},{7,15},{8,0},{9,1},... | collective-permute-start | bytes 3145736 | tf_op jit(solution)/shard_map/ppermute | solution.py:28
  60.1 9.5 %collective-permute-start.3 = (bf16[512,512]{1,0:T(8,128)(2,1)S(1)}, bf16[512,512]{1,0:T(8,128)(2,1)S(1)}, u32[]{:S(2)}, u32[]{:S(2)}) collective-permute-start(bf16[512,512]{1,0:T(8,128)(2,1)S(1)} %collective-permute-done.2.refs_3_), channel_id=1, source_target_pairs={{0,1},{1,2},{2,3},{3,4},{4,5},{5,6},{6,7},{7,0},{8,15},{9,8},{10,9... | collective-permute-start | bytes 1572872 | tf_op jit(solution)/shard_map/ppermute | solution.py:28
  65.1 11.0 %collective-permute-start.9 = (bf16[512,512]{1,0:T(8,128)(2,1)S(1)}, bf16[512,512]{1,0:T(8,128)(2,1)}, u32[]{:S(2)}, u32[]{:S(2)}) collective-permute-start(bf16[512,512]{1,0:T(8,128)(2,1)S(1)} %collective-permute-done.7), channel_id=1, source_target_pairs={{0,1},{1,2},{2,3},{3,4},{4,5},{5,6},{6,7},{7,0},{8,15},{9,8},{10,9... | collective-permute-start | bytes 1572872 | tf_op jit(solution)/shard_map/ppermute | solution.py:28
  65.2 20.1 %collective-permute-start.33 = (bf16[4,256,512]{2,1,0:T(8,128)(2,1)}, bf16[4,256,512]{2,1,0:T(8,128)(2,1)}, u32[]{:S(2)}, u32[]{:S(2)}) collective-permute-start(bf16[4,256,512]{2,1,0:T(8,128)(2,1)} %collective-permute-done.28.refs_10_), channel_id=1, source_target_pairs={{0,8},{1,9},{2,10},{3,11},{4,12},{5,13},{6,14},{7,15},{8,0},{9,1},... | collective-permute-start | bytes 3145736 | tf_op jit(solution)/shard_map/ppermute | solution.py:28
  65.7 14.5 %collective-permute-start.8 = (bf16[512,512]{1,0:T(8,128)(2,1)S(1)}, bf16[512,512]{1,0:T(8,128)(2,1)S(1)}, u32[]{:S(2)}, u32[]{:S(2)}) collective-permute-start(bf16[512,512]{1,0:T(8,128)(2,1)S(1)} %collective-permute-done.7), channel_id=1, source_target_pairs={{0,8},{1,9},{2,10},{3,11},{4,12},{5,13},{6,14},{7,15},{8,0},{9,1},... | collective-permute-start | bytes 1572872 | tf_op jit(solution)/shard_map/ppermute | solution.py:28
  70.5 11.8 %collective-permute-start.34 = (bf16[2,256,512]{2,1,0:T(8,128)(2,1)S(1)}, bf16[2,256,512]{2,1,0:T(8,128)(2,1)}, u32[]{:S(2)}, u32[]{:S(2)}) collective-permute-start(bf16[2,256,512]{2,1,0:T(8,128)(2,1)S(1)} %collective-permute-done.29.refs_11_), channel_id=1, source_target_pairs={{0,8},{1,9},{2,10},{3,11},{4,12},{5,13},{6,14},{7,15},{8,0},{9,1},... | collective-permute-start | bytes 1572872 | tf_op jit(solution)/shard_map/ppermute | solution.py:28
  76.1 6.6 %collective-permute-start.35 = (bf16[2,256,512]{2,1,0:T(8,128)(2,1)}, bf16[2,256,512]{2,1,0:T(8,128)(2,1)}, u32[]{:S(2)}, u32[]{:S(2)}) collective-permute-start(bf16[2,256,512]{2,1,0:T(8,128)(2,1)} %collective-permute-done.30.refs_12_), channel_id=1, source_target_pairs={{0,8},{1,9},{2,10},{3,11},{4,12},{5,13},{6,14},{7,15},{8,0},{9,1},... | collective-permute-start | bytes 1572872 | tf_op jit(solution)/shard_map/ppermute | solution.py:28
  81.1 4.2 %collective-permute-start.10 = (bf16[512,512]{1,0:T(8,128)(2,1)}, bf16[512,512]{1,0:T(8,128)(2,1)}, u32[]{:S(2)}, u32[]{:S(2)}) collective-permute-start(bf16[512,512]{1,0:T(8,128)(2,1)} %collective-permute-done.9), channel_id=1, source_target_pairs={{0,8},{1,9},{2,10},{3,11},{4,12},{5,13},{6,14},{7,15},{8,0},{9,1},... | collective-permute-start | bytes 1572872 | tf_op jit(solution)/shard_map/ppermute | solution.py:28
  81.1 4.2 %copy-start.3 = (bf16[4,256,512]{2,1,0:T(8,128)(2,1)S(1)}, bf16[4,256,512]{2,1,0:T(8,128)(2,1)}, u32[]{:S(2)}) copy-start(bf16[4,256,512]{2,1,0:T(8,128)(2,1)} %copy-done.2) | copy-start | bytes 3145732
  82.2 27.8 %collective-permute-start.15 = (bf16[4,256,256]{2,1,0:T(8,128)(2,1)S(1)}, bf16[4,256,256]{2,1,0:T(8,128)(2,1)S(1)}, u32[]{:S(2)}, u32[]{:S(2)}) collective-permute-start(bf16[4,256,256]{2,1,0:T(8,128)(2,1)S(1)} %pad_maximum_fusion.1.refs_8_), channel_id=1, source_target_pairs={{0,16},{1,17},{2,18},{3,19},{4,20},{5,21},{6,22},{7,23},{8,72},{9,... | collective-permute-start | bytes 1572872 | tf_op jit(solution)/shard_map/ppermute | solution.py:28
  82.7 27.4 %collective-permute-start.16 = (bf16[4,256,256]{2,1,0:T(8,128)(2,1)S(1)}, bf16[4,256,256]{2,1,0:T(8,128)(2,1)}, u32[]{:S(2)}, u32[]{:S(2)}) collective-permute-start(bf16[4,256,256]{2,1,0:T(8,128)(2,1)S(1)} %pad_maximum_fusion.1.refs_8_), channel_id=1, source_target_pairs={{0,48},{1,49},{2,50},{3,51},{4,52},{5,53},{6,54},{7,55},{8,200},{9... | collective-permute-start | bytes 1572872 | tf_op jit(solution)/shard_map/ppermute | solution.py:28
  85.3 1.0 copy-start.5
  86.3 1.0 copy-start.8
  87.4 1.0 copy-start.11
  88.4 1.0 copy-start.14
  89.5 1.0 copy-start.17
  104.2 12.1 %copy-start.27 = (bf16[2,512,512]{2,1,0:T(8,128)(2,1)}, bf16[2,512,512]{2,1,0:T(8,128)(2,1)S(1)}, u32[]{:S(2)}) copy-start(bf16[2,512,512]{2,1,0:T(8,128)(2,1)S(1)} %get-tuple-element.7.refs_18_) | copy-start | bytes 3145732
  104.2 1.8 %collective-permute-start.36 = (bf16[2,128,128]{2,1,0:T(8,128)(2,1)S(1)}, bf16[2,128,128]{2,1,0:T(8,128)(2,1)S(1)}, u32[]{:S(2)}, u32[]{:S(2)}) collective-permute-start(bf16[2,128,128]{2,1,0:T(8,128)(2,1)S(1)} %select_convert_fusion), channel_id=1, source_target_pairs={{0,8},{1,9},{2,10},{3,11},{4,12},{5,13},{6,14},{7,15},{8,0},{9,1},... | collective-permute-start | bytes 196616 | tf_op jit(solution)/shard_map/ppermute | solution.py:28
  106.0 9.7 %copy-start.31 = (bf16[2,128,128]{2,1,0:T(8,128)(2,1)}, bf16[2,128,128]{2,1,0:T(8,128)(2,1)S(1)}, u32[]{:S(2)}) copy-start(bf16[2,128,128]{2,1,0:T(8,128)(2,1)S(1)} %collective-permute-done.36) | copy-start | bytes 196612
  106.0 24.5 %copy-start.21 = (bf16[512,512]{1,0:T(8,128)(2,1)S(1)}, bf16[512,512]{1,0:T(8,128)(2,1)}, u32[]{:S(2)}) copy-start(bf16[512,512]{1,0:T(8,128)(2,1)} %copy-done.19) | copy-start | bytes 1572868
  106.0 6.3 %collective-permute-start.37 = (bf16[2,128,128]{2,1,0:T(8,128)(2,1)S(1)}, bf16[2,128,128]{2,1,0:T(8,128)(2,1)S(1)}, u32[]{:S(2)}, u32[]{:S(2)}) collective-permute-start(bf16[2,128,128]{2,1,0:T(8,128)(2,1)S(1)} %get-tuple-element.14), channel_id=1, source_target_pairs={{0,32},{1,33},{2,34},{3,35},{4,36},{5,37},{6,38},{7,39},{8,40},{9,... | collective-permute-start | bytes 196616 | tf_op jit(solution)/shard_map/ppermute | solution.py:28
  107.3 7.3 %collective-permute-start.38 = (bf16[2,128,128]{2,1,0:T(8,128)(2,1)S(1)}, bf16[2,128,128]{2,1,0:T(8,128)(2,1)S(1)}, u32[]{:S(2)}, u32[]{:S(2)}) collective-permute-start(bf16[2,128,128]{2,1,0:T(8,128)(2,1)S(1)} %get-tuple-element.14), channel_id=1, source_target_pairs={{0,16},{1,17},{2,18},{3,19},{4,20},{5,21},{6,22},{7,23},{8,24},{9,... | collective-permute-start | bytes 196616 | tf_op jit(solution)/shard_map/ppermute | solution.py:28
  107.7 7.8 %collective-permute-start.39 = (bf16[2,128,128]{2,1,0:T(8,128)(2,1)S(1)}, bf16[2,128,128]{2,1,0:T(8,128)(2,1)S(1)}, u32[]{:S(2)}, u32[]{:S(2)}) collective-permute-start(bf16[2,128,128]{2,1,0:T(8,128)(2,1)S(1)} %get-tuple-element.14), channel_id=1, source_target_pairs={{0,48},{1,49},{2,50},{3,51},{4,52},{5,53},{6,54},{7,55},{8,56},{9,... | collective-permute-start | bytes 196616 | tf_op jit(solution)/shard_map/ppermute | solution.py:28
  110.0 20.4 %copy-start.18 = (bf16[512,512]{1,0:T(8,128)(2,1)S(1)}, bf16[512,512]{1,0:T(8,128)(2,1)}, u32[]{:S(2)}) copy-start(bf16[512,512]{1,0:T(8,128)(2,1)} %copy-done.16) | copy-start | bytes 1572868
  110.0 6.8 %collective-permute-start.17 = (bf16[2,256,256]{2,1,0:T(8,128)(2,1)S(1)}, bf16[2,256,256]{2,1,0:T(8,128)(2,1)S(1)}, u32[]{:S(2)}, u32[]{:S(2)}) collective-permute-start(bf16[2,256,256]{2,1,0:T(8,128)(2,1)S(1)} %slice.52), channel_id=1, source_target_pairs={{0,16},{1,17},{2,18},{3,19},{4,20},{5,21},{6,22},{7,23},{8,72},{9,... | collective-permute-start | bytes 786440 | tf_op jit(solution)/shard_map/ppermute | solution.py:28
  110.2 20.1 %collective-permute-start.19 = (bf16[4,256,256]{2,1,0:T(8,128)(2,1)S(1)}, bf16[4,256,256]{2,1,0:T(8,128)(2,1)}, u32[]{:S(2)}, u32[]{:S(2)}) collective-permute-start(bf16[4,256,256]{2,1,0:T(8,128)(2,1)S(1)} %pad_maximum_fusion.1.refs_8_), channel_id=1, source_target_pairs={{0,8},{1,9},{2,10},{3,11},{4,12},{5,13},{6,14},{7,15},{8,0},{9,1},... | collective-permute-start | bytes 1572872 | tf_op jit(solution)/shard_map/ppermute | solution.py:28
  111.2 19.2 %copy-start.15 = (bf16[512,512]{1,0:T(8,128)(2,1)S(1)}, bf16[512,512]{1,0:T(8,128)(2,1)}, u32[]{:S(2)}) copy-start(bf16[512,512]{1,0:T(8,128)(2,1)} %copy-done.13) | copy-start | bytes 1572868
  112.3 4.0 %copy-start.33 = (bf16[2,128,128]{2,1,0:T(8,128)(2,1)}, bf16[2,128,128]{2,1,0:T(8,128)(2,1)S(1)}, u32[]{:S(2)}) copy-start(bf16[2,128,128]{2,1,0:T(8,128)(2,1)S(1)} %collective-permute-done.37) | copy-start | bytes 196612
  112.3 5.7 %collective-permute-start.18 = (bf16[2,256,256]{2,1,0:T(8,128)(2,1)S(1)}, bf16[2,256,256]{2,1,0:T(8,128)(2,1)}, u32[]{:S(2)}, u32[]{:S(2)}) collective-permute-start(bf16[2,256,256]{2,1,0:T(8,128)(2,1)S(1)} %slice.53), channel_id=1, source_target_pairs={{0,48},{1,49},{2,50},{3,51},{4,52},{5,53},{6,54},{7,55},{8,200},{9... | collective-permute-start | bytes 786440 | tf_op jit(solution)/shard_map/ppermute | solution.py:28
  114.6 1.7 %copy-start.34 = (bf16[2,128,128]{2,1,0:T(8,128)(2,1)}, bf16[2,128,128]{2,1,0:T(8,128)(2,1)S(1)}, u32[]{:S(2)}) copy-start(bf16[2,128,128]{2,1,0:T(8,128)(2,1)S(1)} %collective-permute-done.38) | copy-start | bytes 196612
  114.6 15.8 %collective-permute-start.20 = (bf16[4,256,256]{2,1,0:T(8,128)(2,1)S(1)}, bf16[4,256,256]{2,1,0:T(8,128)(2,1)}, u32[]{:S(2)}, u32[]{:S(2)}) collective-permute-start(bf16[4,256,256]{2,1,0:T(8,128)(2,1)S(1)} %collective-permute-done.15.refs_9_), channel_id=1, source_target_pairs={{0,8},{1,9},{2,10},{3,11},{4,12},{5,13},{6,14},{7,15},{8,0},{9,1},... | collective-permute-start | bytes 1572872 | tf_op jit(solution)/shard_map/ppermute | solution.py:28
  115.5 14.9 %collective-permute-start.21 = (bf16[4,256,256]{2,1,0:T(8,128)(2,1)}, bf16[4,256,256]{2,1,0:T(8,128)(2,1)}, u32[]{:S(2)}, u32[]{:S(2)}) collective-permute-start(bf16[4,256,256]{2,1,0:T(8,128)(2,1)} %collective-permute-done.16.refs_10_), channel_id=1, source_target_pairs={{0,8},{1,9},{2,10},{3,11},{4,12},{5,13},{6,14},{7,15},{8,0},{9,1},... | collective-permute-start | bytes 1572872 | tf_op jit(solution)/shard_map/ppermute | solution.py:28
  115.6 14.9 %copy-start.12 = (bf16[512,512]{1,0:T(8,128)(2,1)S(1)}, bf16[512,512]{1,0:T(8,128)(2,1)}, u32[]{:S(2)}) copy-start(bf16[512,512]{1,0:T(8,128)(2,1)} %copy-done.10) | copy-start | bytes 1572868
  116.9 4.6 %collective-permute-start.40 = (bf16[2,128,128]{2,1,0:T(8,128)(2,1)}, bf16[2,128,128]{2,1,0:T(8,128)(2,1)}, u32[]{:S(2)}, u32[]{:S(2)}) collective-permute-start(bf16[2,128,128]{2,1,0:T(8,128)(2,1)} %fusion.13), channel_id=1, source_target_pairs={{0,64},{1,65},{2,66},{3,67},{4,68},{5,69},{6,70},{7,71},{8,72},{9,... | collective-permute-start | bytes 196616 | tf_op jit(solution)/shard_map/ppermute | solution.py:28
  118.0 4.9 %collective-permute-start.41 = (bf16[2,128,128]{2,1,0:T(8,128)(2,1)}, bf16[2,128,128]{2,1,0:T(8,128)(2,1)}, u32[]{:S(2)}, u32[]{:S(2)}) collective-permute-start(bf16[2,128,128]{2,1,0:T(8,128)(2,1)} %fusion.13), channel_id=1, source_target_pairs={{0,128},{1,129},{2,130},{3,131},{4,132},{5,133},{6,134},{7,135},{8... | collective-permute-start | bytes 196616 | tf_op jit(solution)/shard_map/ppermute | solution.py:28
  121.5 4.5 %collective-permute-start.42 = (bf16[2,128,128]{2,1,0:T(8,128)(2,1)}, bf16[2,128,128]{2,1,0:T(8,128)(2,1)}, u32[]{:S(2)}, u32[]{:S(2)}) collective-permute-start(bf16[2,128,128]{2,1,0:T(8,128)(2,1)} %fusion.13), channel_id=1, source_target_pairs={{0,192},{1,193},{2,194},{3,195},{4,196},{5,197},{6,198},{7,199},{8... | collective-permute-start | bytes 196616 | tf_op jit(solution)/shard_map/ppermute | solution.py:28
  122.1 8.4 %copy-start.6 = (bf16[512,512]{1,0:T(8,128)(2,1)S(1)}, bf16[512,512]{1,0:T(8,128)(2,1)}, u32[]{:S(2)}) copy-start(bf16[512,512]{1,0:T(8,128)(2,1)} %refs_0_.3) | copy-start | bytes 1572868
  122.1 8.4 %copy-start.9 = (bf16[512,512]{1,0:T(8,128)(2,1)S(1)}, bf16[512,512]{1,0:T(8,128)(2,1)}, u32[]{:S(2)}) copy-start(bf16[512,512]{1,0:T(8,128)(2,1)} %copy-done.7) | copy-start | bytes 1572868
  122.9 7.5 %collective-permute-start.22 = (bf16[2,256,256]{2,1,0:T(8,128)(2,1)S(1)}, bf16[2,256,256]{2,1,0:T(8,128)(2,1)S(1)}, u32[]{:S(2)}, u32[]{:S(2)}) collective-permute-start(bf16[2,256,256]{2,1,0:T(8,128)(2,1)S(1)} %collective-permute-done.17.refs_11_), channel_id=1, source_target_pairs={{0,8},{1,9},{2,10},{3,11},{4,12},{5,13},{6,14},{7,15},{8,0},{9,1},... | collective-permute-start | bytes 786440 | tf_op jit(solution)/shard_map/ppermute | solution.py:28
  126.0 4.5 %collective-permute-start.23 = (bf16[2,256,256]{2,1,0:T(8,128)(2,1)}, bf16[2,256,256]{2,1,0:T(8,128)(2,1)S(1)}, u32[]{:S(2)}, u32[]{:S(2)}) collective-permute-start(bf16[2,256,256]{2,1,0:T(8,128)(2,1)} %collective-permute-done.18.refs_12_), channel_id=1, source_target_pairs={{0,8},{1,9},{2,10},{3,11},{4,12},{5,13},{6,14},{7,15},{8,0},{9,1},... | collective-permute-start | bytes 786440 | tf_op jit(solution)/shard_map/ppermute | solution.py:28
  130.3 13.5 %collective-permute-start.43 = (f32[2,2,128,128]{3,2,1,0:T(8,128)S(1)}, f32[2,2,128,128]{3,2,1,0:T(8,128)S(1)}, u32[]{:S(2)}, u32[]{:S(2)}) collective-permute-start(f32[2,2,128,128]{3,2,1,0:T(8,128)S(1)} %pad_maximum_fusion.3), channel_id=1, source_target_pairs={{0,8},{1,9},{2,10},{3,11},{4,12},{5,13},{6,14},{7,15},{8,0},{9,1},... | collective-permute-start | bytes 786440 | tf_op jit(solution)/shard_map/ppermute | solution.py:28
  132.2 1.2 copy-start.28
  134.4 9.4 %copy-start.32 = (bf16[2,128,128]{2,1,0:T(8,128)(2,1)S(1)}, bf16[2,128,128]{2,1,0:T(8,128)(2,1)}, u32[]{:S(2)}) copy-start(bf16[2,128,128]{2,1,0:T(8,128)(2,1)} %copy-done.31) | copy-start | bytes 196612
  (18 other events, 16.0 us)

commit v2 on v0

v2 whole, which is shorter than its diff:
```python
import jax
import jax.numpy as jnp
from jax import lax
from jax.experimental import pallas as pl
from jax.experimental.pallas import tpu as pltpu
from jax.sharding import PartitionSpec as P

NX, NY, NC, NZ = 4, 4, 2, 8
BOTH = ("seq", "tensor")
BF, F32 = jnp.bfloat16, jnp.float32


def place(x, y, c, z):
    return (((x % NX) * NY + y % NY) * NC + c % NC) * NZ + z % NZ


def move(a, f):
    pairs = [
        (place(x, y, c, z), place(*f(x, y, c, z)))
        for x in range(NX)
        for y in range(NY)
        for c in range(NC)
        for z in range(NZ)
    ]
    return lax.ppermute(a, BOTH, pairs)


def swap(a):
    return move(a, lambda x, y, c, z: (x, y, c + 1, z))


def along_z(a):
    return move(a, lambda x, y, c, z: (x, y, c, z + (1 if c == 0 else -1)))


def first(a, k):
    return move(a, lambda x, y, c, z: (x + k, y, c, z) if c == 0 else (x, y + k, c, z))


def second(a, k):
    return move(a, lambda x, y, c, z: (x, y + k, c, z) if c == 0 else (x + k, y, c, z))


def by_x(a, k):
    return move(a, lambda x, y, c, z: (x + k, y, c, z))


def by_y(a, k):
    return move(a, lambda x, y, c, z: (x, y + k, c, z))


def scalars(pos):
    return pos[0], pos[1], pos[2], pos[3]


def slot_of(step):
    step = lax.rem(step + 4, 4)
    return jnp.where(step >= 2, 5 - step, step)


def column(c, x, y, q):
    dx, dy = slot_of(x - q // NY), slot_of(y - lax.rem(q, NY))
    return jnp.where(c == 0, dy * 4 + dx, dx * 4 + dy)


def weights_dot(x_ref, parts, lanes):
    acc = None
    at = 0
    for part, n in parts:
        d = jnp.dot(x_ref[:, at : at + n], part[:n, lanes], preferred_element_type=F32)
        acc = d if acc is None else acc + d
        at += n
    return acc


def kv_kernel(pos, own, z1, z2, z3, a4, st, right, left, far_a, far_b, got_a, got_b, got_c, *outs):
    kv_ref, r_ref, part_ref, give_ref, xa_ref, xb_ref = outs
    mine = ((st, 1024), (right, 1024), (left, 1024), (far_a, 512), (far_b, 512))
    other = ((got_a, 1024), (got_b, 2048), (got_c, 1024))
    pieces = (
        (own, 0), (z1, 0), (z2, 0), (z3, 0), (a4, 0), (got_a, 1024), (got_b, 2048), (got_c, 1024)
    )
    x, y, z, c = scalars(pos)
    sign = 1 - 2 * c
    shifts = [0] + [-k for k in range(1, 5)] + [k for k in range(1, 4)]
    total = jnp.zeros((512, 128), F32)
    for (piece, lo), k in zip(pieces, shifts):
        at = lax.rem(z + sign * k + 2 * NZ, NZ)
        for h in range(2):
            q = 2 * at + h
            block = piece[lo : lo + 512, h * 256 : (h + 1) * 256]
            xa_ref[:, pl.ds(pl.multiple_of(column(c, x, y, q) * 256, 256), 256)] = block
            xb_ref[:, pl.ds(pl.multiple_of(column(1 - c, x, y, q) * 256, 256), 256)] = block
            wide = block.astype(F32)
            wide = wide * wide
            total = total + wide[:, :128] + wide[:, 128:]
    r = lax.rsqrt(jnp.sum(total, axis=1, keepdims=True) * (1.0 / 4096) + 1e-05)
    r_ref[...] = jnp.broadcast_to(r, (512, 128))

    @pl.loop(0, 2)
    def _(i):
        lanes = pl.ds(pl.multiple_of(i * 256, 256), 256)
        kv_ref[c, :, lanes] = (weights_dot(xa_ref, mine, lanes) * r_ref[:, :1]).astype(BF)
        kv_ref[1 - c, :, lanes] = (weights_dot(xb_ref, other, lanes) * r_ref[:, :1]).astype(BF)

    @pl.loop(0, 4)
    def _(h):
        head = lax.rem(h + 2 * c, 4)
        lanes = pl.ds(pl.multiple_of(head * 128, 128), 128)
        state = lax.dot_general(
            kv_ref[0, :, lanes],
            kv_ref[1, :, lanes],
            (((0,), (0,)), ((), ())),
            preferred_element_type=F32,
        )

        @pl.when(h < 2)
        def _():
            part_ref[h] = state

        @pl.when(h >= 2)
        def _():
            give_ref[h - 2] = state.astype(BF)


def chip_kernel(pos, part_ref, sib_ref, sent_ref):
    sent_ref[...] = (part_ref[...] + sib_ref[...].astype(F32)).astype(BF)


def along(at, sent, behind, ahead, opposite):
    b, f, o = behind[...].astype(F32), ahead[...].astype(F32), opposite[...].astype(F32)
    total = (sent[...].astype(F32) + o) + (b + f)
    before = jnp.where(at >= 1, b, 0.0) + jnp.where(at >= 2, o, 0.0) + jnp.where(at == 3, f, 0.0)
    return before, total


def row_kernel(pos, sent, behind, ahead, opposite, before_ref, next_ref):
    before, total = along(pos[1], sent, behind, ahead, opposite)
    before_ref[...] = before
    next_ref[...] = total.astype(BF)


def plane_kernel(pos, sent, behind, ahead, opposite, row_ref, part_ref, sib_ref, mine_ref, both_ref):
    before, total = along(pos[0], sent, behind, ahead, opposite)
    before = before + row_ref[...]
    c = pos[3]
    mine_ref[0] = before + jnp.where(c == 1, sib_ref[...].astype(F32), 0.0)
    mine_ref[1] = total
    both_ref[0] = before + jnp.where(c == 0, part_ref[...], 0.0)
    both_ref[1] = total


def split_dot(q, m):
    hi = m.astype(BF)
    lo = (m - hi.astype(F32)).astype(BF)
    return jnp.dot(q, hi, preferred_element_type=F32) + jnp.dot(q, lo, preferred_element_type=F32)


def q_kernel(pos, xa_ref, xb_ref, *refs):
    sizes = (1024, 1024, 1024, 512, 512, 3072, 1024)
    parts = tuple(zip(refs[:7], sizes))
    mine, other = parts[:5], parts[5:]
    kv_ref, r_ref, carried_ref, q_ref, raw_ref = refs[7:]
    c = pos[3]
    for x_ref, parts, to in ((xa_ref, mine, c), (xb_ref, other, 1 - c)):
        got = weights_dot(x_ref, parts, slice(0, 256)) * r_ref[:, :1]
        q_ref[:, pl.ds(pl.multiple_of(to * 256, 256), 256)] = got.astype(BF)
    row = lax.broadcasted_iota(jnp.int32, (512, 512), 0)
    col = lax.broadcasted_iota(jnp.int32, (512, 512), 1)

    @pl.loop(0, 4)
    def _(h):
        lanes = pl.ds(pl.multiple_of(h * 128, 128), 128)
        q = q_ref[:, lanes]
        scores = lax.dot_general(
            q, kv_ref[0, :, lanes], (((1,), (1,)), ((), ())), preferred_element_type=F32
        )
        weights = jnp.where(col <= row, scores, 0.0).astype(BF)
        intra = jnp.dot(weights, kv_ref[1, :, lanes], preferred_element_type=F32)
        raw_ref[:, lanes] = intra + split_dot(q, carried_ref[h])


def out_kernel(pos, q_ref, raw_ref, mine_ref, both_ref, carried_ref, gain_ref, out_ref, final_ref):
    c = pos[3]
    for own in range(2):
        for n in range(2):
            h = 2 * (c if own else 1 - c) + n
            lanes = pl.ds(pl.multiple_of(h * 128, 128), 128)
            before = mine_ref[0, n] if own else both_ref[0, n]
            total = mine_ref[1, n] if own else both_ref[1, n]
            raw = raw_ref[:, lanes] + split_dot(q_ref[:, lanes], before)
            scale = lax.rsqrt(jnp.mean(raw * raw, axis=1, keepdims=True) + 1e-06)
            out_ref[:, lanes] = (raw * scale * gain_ref[:, lanes]).astype(BF)
            final_ref[h] = carried_ref[h] + total


SMEM = pl.BlockSpec(memory_space=pltpu.SMEM)
VMEM = pl.BlockSpec(memory_space=pltpu.VMEM)


def kernel(body, name, outs, n_in, flops, space=VMEM, scratch=(), spaces=None, size=8):
    return pl.pallas_call(
        body,
        name=name,
        out_shape=tuple(jax.ShapeDtypeStruct(*o) for o in outs),
        in_specs=[SMEM] + (space if isinstance(space, list) else [space] * n_in),
        out_specs=tuple(spaces or [VMEM] * len(outs)),
        scratch_shapes=scratch,
        compiler_params=pltpu.CompilerParams(vmem_limit_bytes=size << 20),
        cost_estimate=pl.CostEstimate(flops=flops, bytes_accessed=1 << 20, transcendentals=0),
    )


def after(a, *deps):
    return lax.optimization_barrier((a,) + deps)[0]


def shards(tokens, norm_gain, w_query, w_key, w_value, out_gain, carried):
    s = lax.axis_index("seq").astype(jnp.int32)
    z = lax.axis_index("tensor").astype(jnp.int32)
    c = lax.rem(s, 2)
    y = lax.rem(s // 2, NY)
    x = s // (2 * NY)
    pos = jnp.stack([x, y, z, c])
    tokens, pos = lax.optimization_barrier((tokens, pos))
    even = c == 0
    pick = lambda a, b: jnp.where(even, a, b)

    sib = swap(tokens)
    g = lax.dynamic_slice(norm_gain, (s * 128,), (128,))[:, None]
    scaled = lambda w: (w.astype(F32) * g).astype(BF)
    wq, wk, wv = scaled(w_query), scaled(w_key), scaled(w_value)
    qa, qb = wq[:, :256], wq[:, 256:]
    mine = jnp.concatenate([pick(wk, wv), pick(qa, qb)], 1)
    give = jnp.concatenate([pick(wv, wk), pick(qb, qa)], 1)
    got = swap(after(give, sib))
    chip = jnp.concatenate([pick(mine, got), pick(got, mine)], 0)
    cat = jnp.concatenate
    z1 = along_z(after(cat([tokens, sib]), got))
    near = [first(chip, k) for k in (1, -1, 2)]
    z1, *near = lax.optimization_barrier((z1, *near))
    near = [chip] + near
    st = cat([w[:, :512] for w in near])
    qst = cat([w[:, 512:] for w in near])
    z2 = along_z(z1)
    right, left = second(st, 1), second(st, -1)
    got_a = swap(cat([st, z1[512:]]))
    z2, right, left, got_a = lax.optimization_barrier((z2, right, left, got_a))
    z3 = along_z(z2)
    far_a, far_b = second(right[:512], 1), second(left[512:], -1)
    got_b = swap(cat([right, left, z2[512:]]))
    z3, far_a, far_b, got_b = lax.optimization_barrier((z3, far_a, far_b, got_b))
    a4 = along_z(z3[:512])
    qright, qleft = second(qst, 1), second(qst, -1)
    got_c = swap(cat([far_a, far_b, z3[512:]]))
    a4, qright, qleft, got_c = lax.optimization_barrier((a4, qright, qleft, got_c))
    qfar_a, qfar_b = second(qright[:512], 1), second(qleft[512:], -1)
    q_parts = (qst, qright, qleft, qfar_a, qfar_b)

    flops = 2 * 512 * 4096 * 1024
    kv_rows, r, part, give, xa, xb = kernel(
        kv_kernel,
        "kv",
        [
            ((2, 512, 512), BF),
            ((512, 128), F32),
            ((2, 128, 128), F32),
            ((2, 128, 128), BF),
            ((512, 4096), BF),
            ((512, 4096), BF),
        ],
        13,
        flops,
    )(pos, tokens, z1, z2, z3, a4, st, right, left, far_a, far_b, got_a, got_b, got_c)
    q_other = (
        swap(cat([qst, qright, qleft])),
        swap(after(cat([qfar_a, after(qfar_b, part)]), part)),
    )
    query, raw = kernel(q_kernel, "q", [((512, 512), BF), ((512, 512), F32)], 12, flops)(
        pos, xa, xb, *q_parts, *q_other, kv_rows, r, carried
    )

    heads = (2, 128, 128)
    from_sib = swap(give)
    (sent,) = kernel(chip_kernel, "chip", [(heads, BF)], 2, 1 << 16)(
        pos, part, from_sib
    )
    near = [by_y(sent, k) for k in (1, -1, 2)]
    before, row = kernel(row_kernel, "row", [(heads, F32), (heads, BF)], 4, 1 << 16)(
        pos, sent, *near
    )
    near = [by_x(row, k) for k in (1, -1, 2)]
    before = after(before, raw)
    both = (2,) + heads
    mine, give = kernel(plane_kernel, "plane", [(both, F32), (both, F32)], 7, 1 << 16)(
        pos, row, *near, before, part, from_sib
    )
    return kernel(out_kernel, "out", [((512, 512), BF), ((4, 128, 128), F32)], 6, 1 << 28)(
        pos, query, raw, mine, swap(give), carried, out_gain.reshape(1, 512)
    )


def solution(mesh):
    return jax.shard_map(
        shards,
        mesh=mesh,
        in_specs=(
            P("seq", "tensor"),
            P(),
            P("seq", "tensor"),
            P("seq", "tensor"),
            P("seq", "tensor"),
            P("tensor"),
            P("tensor", None, None),
        ),
        out_specs=(P("seq", "tensor"), P("tensor", None, None)),
        check_vma=False,
    )
```

time: 293 us -> 111 us (0.38)
  waiting for transfers between devices: 247 us -> 48.4 us
  starting transfers between devices: 0.19 us -> 40.8 us
  matrix products: 22.9 us -> 0 us
  Pallas kernels: 0 us -> 17 us
  between operations: 13.9 us -> 0.99 us
  other arithmetic: 7.74 us -> 2.83 us
    all_gather x5 -> x0, waiting for transfers between devices: 245 us -> none  [the longest x1 58.4 us: shards(): whole = lax.all_gather(tokens, 'tensor', axis=1, tiled=True)]
    ppermute x0 -> x30, waiting for transfers between devices: none -> 48.4 us  [move(): return lax.ppermute(a, BOTH, pairs)]
    ppermute x0 -> x30, starting transfers between devices: none -> 40.8 us  [move(): return lax.ppermute(a, BOTH, pairs)]
    dot_general x6 -> x0, matrix products: 22.9 us -> none  [the longest x3 18.6 us: add_rows(): jnp.dot(normed, piece, preferred_element_type=jnp.float32)]
    pallas_call x0 -> x6, Pallas kernels: none -> 17 us  [the longest x1 8.24 us: shards(): kernel(kv_kernel, 'kv', [((2, 512, 512), BF), ((512, 128), F32), ((2, 128...]
    reduce_sum x2 -> x0, other arithmetic: 6.72 us -> none  [the longest x1 3.64 us: shards(): total = zero_state + jnp.sum(piece, axis=0)]
  transfers between devices with their start and end apart: 5 -> 30, of which waited for: 5 -> 15; matrix products, arithmetic and copies ran while one was open for 9% -> 3% of each run, Pallas kernels for 0% -> 13%
where the time goes in v2:
time: 111 us
  waiting for transfers between devices  48.4 us (44%)
  starting transfers between devices  40.8 us (37%)
  Pallas kernels  17 us (15%)
  other arithmetic  2.83 us (3%)
  local copies, waits for them, and re-layouts  1.27 us (1%)
    ppermute x30, waiting for transfers between devices, move(): return lax.ppermute(a, BOTH, pairs)  48.4 us
    ppermute x30, starting transfers between devices, move(): return lax.ppermute(a, BOTH, pairs)  40.8 us
    pallas_call x1, Pallas kernels, shards(): kernel(kv_kernel, 'kv', [((2, 512, 512), BF), ((512, 128), F32), ((2, 128...  8.24 us
    pallas_call x1, Pallas kernels, shards(): kernel(q_kernel, 'q', [((512, 512), BF), ((512, 512), F32)], 12, flops)  4.91 us
  transfers between devices with their start and end apart: 30, of which 15 were waited for; matrix products, arithmetic and copies ran while one was open for 3% of the time, Pallas kernels for 13%

profile of v2, /device:TPU:1, one launch (start us, length us, event | category | flops | bytes accessed | tf_op | source)
XLA Modules:
  0.0 111.2 jit_solution(11743239169782909862)
XLA Ops:
  0.6 0.0 copy-start
  0.7 0.1 pad_add_fusion.pos
  0.7 3.3 %collective-permute-start = (bf16[512,512]{1,0:T(8,128)(2,1)}, bf16[512,512]{1,0:T(8,128)(2,1)S(1)}, u32[]{:S(2)}, u32[]{:S(2)}) collective-permute-start(bf16[512,512]{1,0:T(8,128)(2,1)} %own), channel_id=1, source_target_pairs={{0,8},{1,9},{2,10},{3,11},{4,12},{5,13},{6,14},{7,15},{8,0},{9,1},... | collective-permute-start | bytes 1572872 | tf_op jit(solution)/shard_map/ppermute | solution.py:25
  4.0 0.8 dynamic_slice.3
  4.8 1.0 multiply_convert_fusion
  5.8 1.1 broadcast_select_fusion.2
  6.9 0.0 collective-permute-done
  6.9 0.1 collective-permute-start.1
  7.0 0.1 pad_maximum_fusion.2
  7.1 1.3 %collective-permute-done.1 = bf16[128,768]{1,0:T(8,128)(2,1)S(1)} collective-permute-done((bf16[128,768]{1,0:T(8,128)(2,1)S(1)}, bf16[128,768]{1,0:T(8,128)(2,1)S(1)}, u32[]{:S(2)}, u32[]{:S(2)}) %collective-permute-start.1) | collective-permute-done | bytes 196640 | tf_op jit(solution)/shard_map/ppermute | solution.py:25
  8.5 3.8 %collective-permute-start.2 = (bf16[1024,512]{1,0:T(8,128)(2,1)S(1)}, bf16[1024,512]{1,0:T(8,128)(2,1)S(1)}, u32[]{:S(2)}, u32[]{:S(2)}) collective-permute-start(bf16[1024,512]{1,0:T(8,128)(2,1)S(1)} %pad_maximum_fusion.2), channel_id=1, source_target_pairs={{0,1},{1,2},{2,3},{3,4},{4,5},{5,6},{6,7},{7,0},{8,15},{9,8},{10,9... | collective-permute-start | bytes 3145736 | tf_op jit(solution)/shard_map/ppermute | solution.py:25
  12.3 0.1 broadcast_select_fusion.1
  12.4 3.0 %collective-permute-start.5 = (bf16[256,768]{1,0:T(8,128)(2,1)S(1)}, bf16[256,768]{1,0:T(8,128)(2,1)S(1)}, u32[]{:S(2)}, u32[]{:S(2)}) collective-permute-start(bf16[256,768]{1,0:T(8,128)(2,1)S(1)} %pad_maximum_fusion.6), channel_id=1, source_target_pairs={{0,128},{1,129},{2,130},{3,131},{4,132},{5,133},{6,134},{7,135},{8... | collective-permute-start | bytes 1179656 | tf_op jit(solution)/shard_map/ppermute | solution.py:25
  15.4 0.8 collective-permute-start.4
  16.2 0.7 collective-permute-start.3
  16.9 3.8 %collective-permute-done.5 = bf16[256,768]{1,0:T(8,128)(2,1)S(1)} collective-permute-done((bf16[256,768]{1,0:T(8,128)(2,1)S(1)}, bf16[256,768]{1,0:T(8,128)(2,1)S(1)}, u32[]{:S(2)}, u32[]{:S(2)}) %collective-permute-start.5) | collective-permute-done | bytes 393248 | tf_op jit(solution)/shard_map/ppermute | solution.py:25
  20.7 4.5 %collective-permute-done.4 = bf16[256,768]{1,0:T(8,128)(2,1)S(1)} collective-permute-done((bf16[256,768]{1,0:T(8,128)(2,1)S(1)}, bf16[256,768]{1,0:T(8,128)(2,1)S(1)}, u32[]{:S(2)}, u32[]{:S(2)}) %collective-permute-start.4) | collective-permute-done | bytes 393248 | tf_op jit(solution)/shard_map/ppermute | solution.py:25
  25.2 0.0 collective-permute-done.2.z1
  25.4 0.3 collective-permute-start.9
  25.8 1.8 %collective-permute-start.6 = (bf16[1024,512]{1,0:T(8,128)(2,1)S(1)}, bf16[1024,512]{1,0:T(8,128)(2,1)S(1)}, u32[]{:S(2)}, u32[]{:S(2)}) collective-permute-start(bf16[1024,512]{1,0:T(8,128)(2,1)S(1)} %collective-permute-done.2.z1), channel_id=1, source_target_pairs={{0,1},{1,2},{2,3},{3,4},{4,5},{5,6},{6,7},{7,0},{8,15},{9,8},{10,9... | collective-permute-start | bytes 3145736 | tf_op jit(solution)/shard_map/ppermute | solution.py:25
  27.5 0.1 pad_maximum_fusion.3.st
  27.6 2.6 %collective-permute-start.8 = (bf16[1024,512]{1,0:T(8,128)(2,1)S(1)}, bf16[1024,512]{1,0:T(8,128)(2,1)S(1)}, u32[]{:S(2)}, u32[]{:S(2)}) collective-permute-start(bf16[1024,512]{1,0:T(8,128)(2,1)S(1)} %pad_maximum_fusion.3.st), channel_id=1, source_target_pairs={{0,48},{1,49},{2,50},{3,51},{4,52},{5,53},{6,54},{7,55},{8,200},{9... | collective-permute-start | bytes 3145736 | tf_op jit(solution)/shard_map/ppermute | solution.py:25
  30.1 0.0 collective-permute-start.7
  30.1 9.6 %collective-permute-done.6.z2 = bf16[1024,512]{1,0:T(8,128)(2,1)S(1)} collective-permute-done((bf16[1024,512]{1,0:T(8,128)(2,1)S(1)}, bf16[1024,512]{1,0:T(8,128)(2,1)S(1)}, u32[]{:S(2)}, u32[]{:S(2)}) %collective-permute-start.6) | collective-permute-done | bytes 1048608 | tf_op jit(solution)/shard_map/ppermute | solution.py:25
  39.7 2.2 %collective-permute-done.8.left = bf16[1024,512]{1,0:T(8,128)(2,1)S(1)} collective-permute-done((bf16[1024,512]{1,0:T(8,128)(2,1)S(1)}, bf16[1024,512]{1,0:T(8,128)(2,1)S(1)}, u32[]{:S(2)}, u32[]{:S(2)}) %collective-permute-start.8) | collective-permute-done | bytes 1048608 | tf_op jit(solution)/shard_map/ppermute | solution.py:25
  41.9 3.1 %collective-permute-done.7.right = bf16[1024,512]{1,0:T(8,128)(2,1)S(1)} collective-permute-done((bf16[1024,512]{1,0:T(8,128)(2,1)S(1)}, bf16[1024,512]{1,0:T(8,128)(2,1)S(1)}, u32[]{:S(2)}, u32[]{:S(2)}) %collective-permute-start.7) | collective-permute-done | bytes 1048608 | tf_op jit(solution)/shard_map/ppermute | solution.py:25
  45.0 0.2 pad_maximum_fusion
  45.2 0.1 collective-permute-start.13
  45.4 3.0 %collective-permute-start.10 = (bf16[1024,512]{1,0:T(8,128)(2,1)S(1)}, bf16[1024,512]{1,0:T(8,128)(2,1)S(1)}, u32[]{:S(2)}, u32[]{:S(2)}) collective-permute-start(bf16[1024,512]{1,0:T(8,128)(2,1)S(1)} %collective-permute-done.6.z2), channel_id=1, source_target_pairs={{0,1},{1,2},{2,3},{3,4},{4,5},{5,6},{6,7},{7,0},{8,15},{9,8},{10,9... | collective-permute-start | bytes 3145736 | tf_op jit(solution)/shard_map/ppermute | solution.py:25
  48.4 2.6 %collective-permute-start.12 = (bf16[512,512]{1,0:T(8,128)(2,1)S(1)}, bf16[512,512]{1,0:T(8,128)(2,1)S(1)}, u32[]{:S(2)}, u32[]{:S(2)}) collective-permute-start(bf16[512,512]{1,0:T(8,128)(2,1)S(1)} %slice.62), channel_id=1, source_target_pairs={{0,48},{1,49},{2,50},{3,51},{4,52},{5,53},{6,54},{7,55},{8,200},{9... | collective-permute-start | bytes 1572872 | tf_op jit(solution)/shard_map/ppermute | solution.py:25
  51.0 6.1 %collective-permute-done.12.far_b = bf16[512,512]{1,0:T(8,128)(2,1)S(1)} collective-permute-done((bf16[512,512]{1,0:T(8,128)(2,1)S(1)}, bf16[512,512]{1,0:T(8,128)(2,1)S(1)}, u32[]{:S(2)}, u32[]{:S(2)}) %collective-permute-start.12) | collective-permute-done | bytes 524320 | tf_op jit(solution)/shard_map/ppermute | solution.py:25
  57.1 3.4 %collective-permute-done.11.far_a = bf16[512,512]{1,0:T(8,128)(2,1)S(1)} collective-permute-done((bf16[512,512]{1,0:T(8,128)(2,1)S(1)}, bf16[512,512]{1,0:T(8,128)(2,1)S(1)}, u32[]{:S(2)}, u32[]{:S(2)}) %collective-permute-start.11) | collective-permute-done | bytes 524320 | tf_op jit(solution)/shard_map/ppermute | solution.py:25
  60.5 0.1 fusion.4
  60.6 0.1 pad_maximum_fusion.1
  60.7 1.4 %collective-permute-start.17 = (bf16[1536,512]{1,0:T(8,128)(2,1)S(1)}, bf16[1536,512]{1,0:T(8,128)(2,1)S(1)}, u32[]{:S(2)}, u32[]{:S(2)}) collective-permute-start(bf16[1536,512]{1,0:T(8,128)(2,1)S(1)} %pad_maximum_fusion.1), channel_id=1, source_target_pairs={{0,8},{1,9},{2,10},{3,11},{4,12},{5,13},{6,14},{7,15},{8,0},{9,1},... | collective-permute-start | bytes 4718600 | tf_op jit(solution)/shard_map/ppermute | solution.py:25
  62.3 2.4 %collective-permute-start.16 = (bf16[1024,256]{1,0:T(8,128)(2,1)S(1)}, bf16[1024,256]{1,0:T(8,128)(2,1)S(1)}, u32[]{:S(2)}, u32[]{:S(2)}) collective-permute-start(bf16[1024,256]{1,0:T(8,128)(2,1)S(1)} %pad_maximum_fusion.4.refs_0_), channel_id=1, source_target_pairs={{0,48},{1,49},{2,50},{3,51},{4,52},{5,53},{6,54},{7,55},{8,200},{9... | collective-permute-start | bytes 1572872 | tf_op jit(solution)/shard_map/ppermute | solution.py:25
  64.6 1.7 %collective-permute-start.14 = (bf16[512,512]{1,0:T(8,128)(2,1)S(1)}, bf16[512,512]{1,0:T(8,128)(2,1)S(1)}, u32[]{:S(2)}, u32[]{:S(2)}) collective-permute-start(bf16[512,512]{1,0:T(8,128)(2,1)S(1)} %get-tuple-element.77), channel_id=1, source_target_pairs={{0,1},{1,2},{2,3},{3,4},{4,5},{5,6},{6,7},{7,0},{8,15},{9,8},{10,9... | collective-permute-start | bytes 1572872 | tf_op jit(solution)/shard_map/ppermute | solution.py:25
  66.4 4.5 %collective-permute-done.16.refs_2_ = bf16[1024,256]{1,0:T(8,128)(2,1)S(1)} collective-permute-done((bf16[1024,256]{1,0:T(8,128)(2,1)S(1)}, bf16[1024,256]{1,0:T(8,128)(2,1)S(1)}, u32[]{:S(2)}, u32[]{:S(2)}) %collective-permute-start.16) | collective-permute-done | bytes 524320 | tf_op jit(solution)/shard_map/ppermute | solution.py:25
  70.8 3.3 %collective-permute-done.15.refs_1_ = bf16[1024,256]{1,0:T(8,128)(2,1)S(1)} collective-permute-done((bf16[1024,256]{1,0:T(8,128)(2,1)S(1)}, bf16[1024,256]{1,0:T(8,128)(2,1)S(1)}, u32[]{:S(2)}, u32[]{:S(2)}) %collective-permute-start.15) | collective-permute-done | bytes 524320 | tf_op jit(solution)/shard_map/ppermute | solution.py:25
  74.3 1.9 %collective-permute-start.20 = (bf16[3072,256]{1,0:T(8,128)(2,1)S(1)}, bf16[3072,256]{1,0:T(8,128)(2,1)S(1)}, u32[]{:S(2)}, u32[]{:S(2)}) collective-permute-start(bf16[3072,256]{1,0:T(8,128)(2,1)S(1)} %constant_dynamic-update-slice_fusion.4), channel_id=1, source_target_pairs={{0,8},{1,9},{2,10},{3,11},{4,12},{5,13},{6,14},{7,15},{8,0},{9,1},... | collective-permute-start | bytes 4718600 | tf_op jit(solution)/shard_map/ppermute | solution.py:25
  76.2 1.2 %collective-permute-start.19 = (bf16[512,256]{1,0:T(8,128)(2,1)S(1)}, bf16[512,256]{1,0:T(8,128)(2,1)S(1)}, u32[]{:S(2)}, u32[]{:S(2)}) collective-permute-start(bf16[512,256]{1,0:T(8,128)(2,1)S(1)} %slice.71), channel_id=1, source_target_pairs={{0,48},{1,49},{2,50},{3,51},{4,52},{5,53},{6,54},{7,55},{8,200},{9... | collective-permute-start | bytes 786440 | tf_op jit(solution)/shard_map/ppermute | solution.py:25
  77.4 0.3 collective-permute-start.18
  77.7 8.2 %kv.1 = (bf16[2,512,512]{2,1,0:T(8,128)(2,1)S(1)}, f32[512,128]{1,0:T(8,128)S(1)}, f32[2,128,128]{2,1,0:T(8,128)S(1)}, bf16[2,128,128]{2,1,0:T(8,128)(2,1)S(1)},...) custom-call(s32[4]{0:T(128)S(1)} %pad_add_fusion.pos, bf16[512,512]{1,0:T(8,128)(2,1)S(1)} %copy-done, ...), custom_call_target="tpu_custom_call" | custom-call | flops 4294967296 | bytes 1048576 | tf_op jit(solution)/shard_map/kv/pallas_call | solution.py:261
  86.0 0.0 copy-start.1
  86.0 1.9 %collective-permute-start.21 = (bf16[1024,256]{1,0:T(8,128)(2,1)S(1)}, bf16[1024,256]{1,0:T(8,128)(2,1)S(1)}, u32[]{:S(2)}, u32[]{:S(2)}) collective-permute-start(bf16[1024,256]{1,0:T(8,128)(2,1)S(1)} %pad_maximum_fusion.5), channel_id=1, source_target_pairs={{0,8},{1,9},{2,10},{3,11},{4,12},{5,13},{6,14},{7,15},{8,0},{9,1},... | collective-permute-start | bytes 1572872 | tf_op jit(solution)/shard_map/ppermute | solution.py:25
  87.9 0.1 collective-permute-start.22
  88.0 1.5 %collective-permute-done.22.sib_ref = bf16[2,128,128]{2,1,0:T(8,128)(2,1)S(1)} collective-permute-done((bf16[2,128,128]{2,1,0:T(8,128)(2,1)S(1)}, bf16[2,128,128]{2,1,0:T(8,128)(2,1)S(1)}, u32[]{:S(2)}, u32[]{:S(2)}) %collective-permute-start.22) | collective-permute-done | bytes 65568 | tf_op jit(solution)/shard_map/ppermute | solution.py:25
  89.5 0.6 chip.1.sent
  90.1 1.4 %collective-permute-start.25 = (bf16[2,128,128]{2,1,0:T(8,128)(2,1)S(1)}, bf16[2,128,128]{2,1,0:T(8,128)(2,1)S(1)}, u32[]{:S(2)}, u32[]{:S(2)}) collective-permute-start(bf16[2,128,128]{2,1,0:T(8,128)(2,1)S(1)} %chip.1.sent), channel_id=1, source_target_pairs={{0,32},{1,33},{2,34},{3,35},{4,36},{5,37},{6,38},{7,39},{8,40},{9,... | collective-permute-start | bytes 196616 | tf_op jit(solution)/shard_map/ppermute | solution.py:25
  91.5 1.8 %collective-permute-start.24 = (bf16[2,128,128]{2,1,0:T(8,128)(2,1)S(1)}, bf16[2,128,128]{2,1,0:T(8,128)(2,1)S(1)}, u32[]{:S(2)}, u32[]{:S(2)}) collective-permute-start(bf16[2,128,128]{2,1,0:T(8,128)(2,1)S(1)} %chip.1.sent), channel_id=1, source_target_pairs={{0,48},{1,49},{2,50},{3,51},{4,52},{5,53},{6,54},{7,55},{8,56},{9,... | collective-permute-start | bytes 196616 | tf_op jit(solution)/shard_map/ppermute | solution.py:25
  93.2 0.5 collective-permute-start.23
  93.7 1.1 collective-permute-done.25.opposite
  94.8 1.9 %collective-permute-done.24.ahead = bf16[2,128,128]{2,1,0:T(8,128)(2,1)S(1)} collective-permute-done((bf16[2,128,128]{2,1,0:T(8,128)(2,1)S(1)}, bf16[2,128,128]{2,1,0:T(8,128)(2,1)S(1)}, u32[]{:S(2)}, u32[]{:S(2)}) %collective-permute-start.24) | collective-permute-done | bytes 65568 | tf_op jit(solution)/shard_map/ppermute | solution.py:25
  96.7 0.9 collective-permute-done.23.behind
  97.6 0.6 row.1
  98.2 0.1 collective-permute-start.28
  98.3 1.2 %collective-permute-start.27 = (bf16[2,128,128]{2,1,0:T(8,128)(2,1)S(1)}, bf16[2,128,128]{2,1,0:T(8,128)(2,1)S(1)}, u32[]{:S(2)}, u32[]{:S(2)}) collective-permute-start(bf16[2,128,128]{2,1,0:T(8,128)(2,1)S(1)} %get-tuple-element.67.sent), channel_id=1, source_target_pairs={{0,192},{1,193},{2,194},{3,195},{4,196},{5,197},{6,198},{7,199},{8... | collective-permute-start | bytes 196616 | tf_op jit(solution)/shard_map/ppermute | solution.py:25
  99.5 0.4 collective-permute-start.26
  99.8 0.0 copy-start.2
  99.9 4.9 %q.1 = (bf16[512,512]{1,0:T(8,128)(2,1)S(1)}, f32[512,512]{1,0:T(8,128)S(1)}) custom-call(s32[4]{0:T(128)S(1)} %pad_add_fusion.pos, bf16[512,4096]{1,0:T(8,128)(2,1)S(1)} %get-tuple-element.55.xa_ref, bf16[512,4096]{1,0:T(8,128)(2,1)S(1)} %get-tuple-element.56.xb_ref, bf16[1024,256]{1,0:T(8,128)(2,1)S(1)} %pad_maximum_fusion.4.refs_0_, ...), custom_call_target="tpu_custom_call" | custom-call | flops 4294967296 | bytes 1048576 | tf_op jit(solution)/shard_map/q/pallas_call | solution.py:279
  104.8 0.6 plane.1
  105.5 2.6 %collective-permute-start.29 = (f32[2,2,128,128]{3,2,1,0:T(8,128)S(1)}, f32[2,2,128,128]{3,2,1,0:T(8,128)S(1)}, u32[]{:S(2)}, u32[]{:S(2)}) collective-permute-start(f32[2,2,128,128]{3,2,1,0:T(8,128)S(1)} %get-tuple-element.71), channel_id=1, source_target_pairs={{0,8},{1,9},{2,10},{3,11},{4,12},{5,13},{6,14},{7,15},{8,0},{9,1},... | collective-permute-start | bytes 786440 | tf_op jit(solution)/shard_map/ppermute | solution.py:25
  108.0 1.2 %collective-permute-done.29.both_ref = f32[2,2,128,128]{3,2,1,0:T(8,128)S(1)} collective-permute-done((f32[2,2,128,128]{3,2,1,0:T(8,128)S(1)}, f32[2,2,128,128]{3,2,1,0:T(8,128)S(1)}, u32[]{:S(2)}, u32[]{:S(2)}) %collective-permute-start.29) | collective-permute-done | bytes 262176 | tf_op jit(solution)/shard_map/ppermute | solution.py:25
  109.2 2.0 %out.1 = (bf16[512,512]{1,0:T(8,128)(2,1)}, f32[4,128,128]{2,1,0:T(8,128)}) custom-call(s32[4]{0:T(128)S(1)} %pad_add_fusion.pos, bf16[512,512]{1,0:T(8,128)(2,1)S(1)} %get-tuple-element.64.q_ref, f32[512,512]{1,0:T(8,128)S(1)} %get-tuple-element.65.raw_ref, f32[2,2,128,128]{3,2,1,0:T(8,128)S(1)} %get-tuple-element.70.mine_ref, ...), custom_call_target="tpu_custom_call" | custom-call | flops 268435456 | bytes 1048576 | tf_op jit(solution)/shard_map/out/pallas_call | solution.py:298
  (39 shorter events, 0.7 us)
Async XLA Ops:
  0.6 6.4 %copy-start = (bf16[512,512]{1,0:T(8,128)(2,1)S(1)}, bf16[512,512]{1,0:T(8,128)(2,1)}, u32[]{:S(2)}) copy-start(bf16[512,512]{1,0:T(8,128)(2,1)} %own) | copy-start | bytes 1572868
  0.7 6.2 %collective-permute-start = (bf16[512,512]{1,0:T(8,128)(2,1)}, bf16[512,512]{1,0:T(8,128)(2,1)S(1)}, u32[]{:S(2)}, u32[]{:S(2)}) collective-permute-start(bf16[512,512]{1,0:T(8,128)(2,1)} %own), channel_id=1, source_target_pairs={{0,8},{1,9},{2,10},{3,11},{4,12},{5,13},{6,14},{7,15},{8,0},{9,1},... | collective-permute-start | bytes 1572872 | tf_op jit(solution)/shard_map/ppermute | solution.py:25
  6.9 1.5 %collective-permute-start.1 = (bf16[128,768]{1,0:T(8,128)(2,1)S(1)}, bf16[128,768]{1,0:T(8,128)(2,1)S(1)}, u32[]{:S(2)}, u32[]{:S(2)}) collective-permute-start(bf16[128,768]{1,0:T(8,128)(2,1)S(1)} %pad_maximum_fusion.7), channel_id=1, source_target_pairs={{0,8},{1,9},{2,10},{3,11},{4,12},{5,13},{6,14},{7,15},{8,0},{9,1},... | collective-permute-start | bytes 589832 | tf_op jit(solution)/shard_map/ppermute | solution.py:25
  8.5 16.8 %collective-permute-start.2 = (bf16[1024,512]{1,0:T(8,128)(2,1)S(1)}, bf16[1024,512]{1,0:T(8,128)(2,1)S(1)}, u32[]{:S(2)}, u32[]{:S(2)}) collective-permute-start(bf16[1024,512]{1,0:T(8,128)(2,1)S(1)} %pad_maximum_fusion.2), channel_id=1, source_target_pairs={{0,1},{1,2},{2,3},{3,4},{4,5},{5,6},{6,7},{7,0},{8,15},{9,8},{10,9... | collective-permute-start | bytes 3145736 | tf_op jit(solution)/shard_map/ppermute | solution.py:25
  12.4 8.3 %collective-permute-start.5 = (bf16[256,768]{1,0:T(8,128)(2,1)S(1)}, bf16[256,768]{1,0:T(8,128)(2,1)S(1)}, u32[]{:S(2)}, u32[]{:S(2)}) collective-permute-start(bf16[256,768]{1,0:T(8,128)(2,1)S(1)} %pad_maximum_fusion.6), channel_id=1, source_target_pairs={{0,128},{1,129},{2,130},{3,131},{4,132},{5,133},{6,134},{7,135},{8... | collective-permute-start | bytes 1179656 | tf_op jit(solution)/shard_map/ppermute | solution.py:25
  15.4 9.8 %collective-permute-start.4 = (bf16[256,768]{1,0:T(8,128)(2,1)S(1)}, bf16[256,768]{1,0:T(8,128)(2,1)S(1)}, u32[]{:S(2)}, u32[]{:S(2)}) collective-permute-start(bf16[256,768]{1,0:T(8,128)(2,1)S(1)} %pad_maximum_fusion.6), channel_id=1, source_target_pairs={{0,192},{1,193},{2,194},{3,195},{4,196},{5,197},{6,198},{7,199},{8... | collective-permute-start | bytes 1179656 | tf_op jit(solution)/shard_map/ppermute | solution.py:25
  16.2 9.0 %collective-permute-start.3 = (bf16[256,768]{1,0:T(8,128)(2,1)S(1)}, bf16[256,768]{1,0:T(8,128)(2,1)S(1)}, u32[]{:S(2)}, u32[]{:S(2)}) collective-permute-start(bf16[256,768]{1,0:T(8,128)(2,1)S(1)} %pad_maximum_fusion.6), channel_id=1, source_target_pairs={{0,64},{1,65},{2,66},{3,67},{4,68},{5,69},{6,70},{7,71},{8,24},{9,... | collective-permute-start | bytes 1179656 | tf_op jit(solution)/shard_map/ppermute | solution.py:25
  25.4 19.6 %collective-permute-start.9 = (bf16[1536,512]{1,0:T(8,128)(2,1)S(1)}, bf16[1536,512]{1,0:T(8,128)(2,1)S(1)}, u32[]{:S(2)}, u32[]{:S(2)}) collective-permute-start(bf16[1536,512]{1,0:T(8,128)(2,1)S(1)} %slice_dynamic-update-slice_fusion), channel_id=1, source_target_pairs={{0,8},{1,9},{2,10},{3,11},{4,12},{5,13},{6,14},{7,15},{8,0},{9,1},... | collective-permute-start | bytes 4718600 | tf_op jit(solution)/shard_map/ppermute | solution.py:25
  25.8 13.9 %collective-permute-start.6 = (bf16[1024,512]{1,0:T(8,128)(2,1)S(1)}, bf16[1024,512]{1,0:T(8,128)(2,1)S(1)}, u32[]{:S(2)}, u32[]{:S(2)}) collective-permute-start(bf16[1024,512]{1,0:T(8,128)(2,1)S(1)} %collective-permute-done.2.z1), channel_id=1, source_target_pairs={{0,1},{1,2},{2,3},{3,4},{4,5},{5,6},{6,7},{7,0},{8,15},{9,8},{10,9... | collective-permute-start | bytes 3145736 | tf_op jit(solution)/shard_map/ppermute | solution.py:25
  27.6 14.3 %collective-permute-start.8 = (bf16[1024,512]{1,0:T(8,128)(2,1)S(1)}, bf16[1024,512]{1,0:T(8,128)(2,1)S(1)}, u32[]{:S(2)}, u32[]{:S(2)}) collective-permute-start(bf16[1024,512]{1,0:T(8,128)(2,1)S(1)} %pad_maximum_fusion.3.st), channel_id=1, source_target_pairs={{0,48},{1,49},{2,50},{3,51},{4,52},{5,53},{6,54},{7,55},{8,200},{9... | collective-permute-start | bytes 3145736 | tf_op jit(solution)/shard_map/ppermute | solution.py:25
  30.1 14.9 %collective-permute-start.7 = (bf16[1024,512]{1,0:T(8,128)(2,1)S(1)}, bf16[1024,512]{1,0:T(8,128)(2,1)S(1)}, u32[]{:S(2)}, u32[]{:S(2)}) collective-permute-start(bf16[1024,512]{1,0:T(8,128)(2,1)S(1)} %pad_maximum_fusion.3.st), channel_id=1, source_target_pairs={{0,16},{1,17},{2,18},{3,19},{4,20},{5,21},{6,22},{7,23},{8,72},{9,... | collective-permute-start | bytes 3145736 | tf_op jit(solution)/shard_map/ppermute | solution.py:25
  45.2 15.3 %collective-permute-start.13 = (bf16[2560,512]{1,0:T(8,128)(2,1)S(1)}, bf16[2560,512]{1,0:T(8,128)(2,1)S(1)}, u32[]{:S(2)}, u32[]{:S(2)}) collective-permute-start(bf16[2560,512]{1,0:T(8,128)(2,1)S(1)} %pad_maximum_fusion), channel_id=1, source_target_pairs={{0,8},{1,9},{2,10},{3,11},{4,12},{5,13},{6,14},{7,15},{8,0},{9,1},... | collective-permute-start | bytes 7864328 | tf_op jit(solution)/shard_map/ppermute | solution.py:25
  45.4 15.1 %collective-permute-start.10 = (bf16[1024,512]{1,0:T(8,128)(2,1)S(1)}, bf16[1024,512]{1,0:T(8,128)(2,1)S(1)}, u32[]{:S(2)}, u32[]{:S(2)}) collective-permute-start(bf16[1024,512]{1,0:T(8,128)(2,1)S(1)} %collective-permute-done.6.z2), channel_id=1, source_target_pairs={{0,1},{1,2},{2,3},{3,4},{4,5},{5,6},{6,7},{7,0},{8,15},{9,8},{10,9... | collective-permute-start | bytes 3145736 | tf_op jit(solution)/shard_map/ppermute | solution.py:25
  48.4 8.7 %collective-permute-start.12 = (bf16[512,512]{1,0:T(8,128)(2,1)S(1)}, bf16[512,512]{1,0:T(8,128)(2,1)S(1)}, u32[]{:S(2)}, u32[]{:S(2)}) collective-permute-start(bf16[512,512]{1,0:T(8,128)(2,1)S(1)} %slice.62), channel_id=1, source_target_pairs={{0,48},{1,49},{2,50},{3,51},{4,52},{5,53},{6,54},{7,55},{8,200},{9... | collective-permute-start | bytes 1572872 | tf_op jit(solution)/shard_map/ppermute | solution.py:25
  51.0 9.5 %collective-permute-start.11 = (bf16[512,512]{1,0:T(8,128)(2,1)S(1)}, bf16[512,512]{1,0:T(8,128)(2,1)S(1)}, u32[]{:S(2)}, u32[]{:S(2)}) collective-permute-start(bf16[512,512]{1,0:T(8,128)(2,1)S(1)} %slice.61), channel_id=1, source_target_pairs={{0,16},{1,17},{2,18},{3,19},{4,20},{5,21},{6,22},{7,23},{8,72},{9,... | collective-permute-start | bytes 1572872 | tf_op jit(solution)/shard_map/ppermute | solution.py:25
  60.7 13.5 %collective-permute-start.17 = (bf16[1536,512]{1,0:T(8,128)(2,1)S(1)}, bf16[1536,512]{1,0:T(8,128)(2,1)S(1)}, u32[]{:S(2)}, u32[]{:S(2)}) collective-permute-start(bf16[1536,512]{1,0:T(8,128)(2,1)S(1)} %pad_maximum_fusion.1), channel_id=1, source_target_pairs={{0,8},{1,9},{2,10},{3,11},{4,12},{5,13},{6,14},{7,15},{8,0},{9,1},... | collective-permute-start | bytes 4718600 | tf_op jit(solution)/shard_map/ppermute | solution.py:25
  62.3 8.6 %collective-permute-start.16 = (bf16[1024,256]{1,0:T(8,128)(2,1)S(1)}, bf16[1024,256]{1,0:T(8,128)(2,1)S(1)}, u32[]{:S(2)}, u32[]{:S(2)}) collective-permute-start(bf16[1024,256]{1,0:T(8,128)(2,1)S(1)} %pad_maximum_fusion.4.refs_0_), channel_id=1, source_target_pairs={{0,48},{1,49},{2,50},{3,51},{4,52},{5,53},{6,54},{7,55},{8,200},{9... | collective-permute-start | bytes 1572872 | tf_op jit(solution)/shard_map/ppermute | solution.py:25
  64.6 9.5 %collective-permute-start.15 = (bf16[1024,256]{1,0:T(8,128)(2,1)S(1)}, bf16[1024,256]{1,0:T(8,128)(2,1)S(1)}, u32[]{:S(2)}, u32[]{:S(2)}) collective-permute-start(bf16[1024,256]{1,0:T(8,128)(2,1)S(1)} %pad_maximum_fusion.4.refs_0_), channel_id=1, source_target_pairs={{0,16},{1,17},{2,18},{3,19},{4,20},{5,21},{6,22},{7,23},{8,72},{9,... | collective-permute-start | bytes 1572872 | tf_op jit(solution)/shard_map/ppermute | solution.py:25
  64.6 9.5 %collective-permute-start.14 = (bf16[512,512]{1,0:T(8,128)(2,1)S(1)}, bf16[512,512]{1,0:T(8,128)(2,1)S(1)}, u32[]{:S(2)}, u32[]{:S(2)}) collective-permute-start(bf16[512,512]{1,0:T(8,128)(2,1)S(1)} %get-tuple-element.77), channel_id=1, source_target_pairs={{0,1},{1,2},{2,3},{3,4},{4,5},{5,6},{6,7},{7,0},{8,15},{9,8},{10,9... | collective-permute-start | bytes 1572872 | tf_op jit(solution)/shard_map/ppermute | solution.py:25
  74.3 25.6 %collective-permute-start.20 = (bf16[3072,256]{1,0:T(8,128)(2,1)S(1)}, bf16[3072,256]{1,0:T(8,128)(2,1)S(1)}, u32[]{:S(2)}, u32[]{:S(2)}) collective-permute-start(bf16[3072,256]{1,0:T(8,128)(2,1)S(1)} %constant_dynamic-update-slice_fusion.4), channel_id=1, source_target_pairs={{0,8},{1,9},{2,10},{3,11},{4,12},{5,13},{6,14},{7,15},{8,0},{9,1},... | collective-permute-start | bytes 4718600 | tf_op jit(solution)/shard_map/ppermute | solution.py:25
  76.2 9.8 %collective-permute-start.19 = (bf16[512,256]{1,0:T(8,128)(2,1)S(1)}, bf16[512,256]{1,0:T(8,128)(2,1)S(1)}, u32[]{:S(2)}, u32[]{:S(2)}) collective-permute-start(bf16[512,256]{1,0:T(8,128)(2,1)S(1)} %slice.71), channel_id=1, source_target_pairs={{0,48},{1,49},{2,50},{3,51},{4,52},{5,53},{6,54},{7,55},{8,200},{9... | collective-permute-start | bytes 786440 | tf_op jit(solution)/shard_map/ppermute | solution.py:25
  77.4 8.6 %collective-permute-start.18 = (bf16[512,256]{1,0:T(8,128)(2,1)S(1)}, bf16[512,256]{1,0:T(8,128)(2,1)S(1)}, u32[]{:S(2)}, u32[]{:S(2)}) collective-permute-start(bf16[512,256]{1,0:T(8,128)(2,1)S(1)} %slice.70), channel_id=1, source_target_pairs={{0,16},{1,17},{2,18},{3,19},{4,20},{5,21},{6,22},{7,23},{8,72},{9,... | collective-permute-start | bytes 786440 | tf_op jit(solution)/shard_map/ppermute | solution.py:25
  86.0 13.9 %copy-start.1 = (f32[4,128,128]{2,1,0:T(8,128)S(1)}, f32[4,128,128]{2,1,0:T(8,128)}, u32[]{:S(2)}) copy-start(f32[4,128,128]{2,1,0:T(8,128)} %carried_ref.1) | copy-start | bytes 786436
  86.0 13.8 %collective-permute-start.21 = (bf16[1024,256]{1,0:T(8,128)(2,1)S(1)}, bf16[1024,256]{1,0:T(8,128)(2,1)S(1)}, u32[]{:S(2)}, u32[]{:S(2)}) collective-permute-start(bf16[1024,256]{1,0:T(8,128)(2,1)S(1)} %pad_maximum_fusion.5), channel_id=1, source_target_pairs={{0,8},{1,9},{2,10},{3,11},{4,12},{5,13},{6,14},{7,15},{8,0},{9,1},... | collective-permute-start | bytes 1572872 | tf_op jit(solution)/shard_map/ppermute | solution.py:25
  87.9 1.6 %collective-permute-start.22 = (bf16[2,128,128]{2,1,0:T(8,128)(2,1)S(1)}, bf16[2,128,128]{2,1,0:T(8,128)(2,1)S(1)}, u32[]{:S(2)}, u32[]{:S(2)}) collective-permute-start(bf16[2,128,128]{2,1,0:T(8,128)(2,1)S(1)} %get-tuple-element.66), channel_id=1, source_target_pairs={{0,8},{1,9},{2,10},{3,11},{4,12},{5,13},{6,14},{7,15},{8,0},{9,1},... | collective-permute-start | bytes 196616 | tf_op jit(solution)/shard_map/ppermute | solution.py:25
  90.1 4.7 %collective-permute-start.25 = (bf16[2,128,128]{2,1,0:T(8,128)(2,1)S(1)}, bf16[2,128,128]{2,1,0:T(8,128)(2,1)S(1)}, u32[]{:S(2)}, u32[]{:S(2)}) collective-permute-start(bf16[2,128,128]{2,1,0:T(8,128)(2,1)S(1)} %chip.1.sent), channel_id=1, source_target_pairs={{0,32},{1,33},{2,34},{3,35},{4,36},{5,37},{6,38},{7,39},{8,40},{9,... | collective-permute-start | bytes 196616 | tf_op jit(solution)/shard_map/ppermute | solution.py:25
  91.5 5.2 %collective-permute-start.24 = (bf16[2,128,128]{2,1,0:T(8,128)(2,1)S(1)}, bf16[2,128,128]{2,1,0:T(8,128)(2,1)S(1)}, u32[]{:S(2)}, u32[]{:S(2)}) collective-permute-start(bf16[2,128,128]{2,1,0:T(8,128)(2,1)S(1)} %chip.1.sent), channel_id=1, source_target_pairs={{0,48},{1,49},{2,50},{3,51},{4,52},{5,53},{6,54},{7,55},{8,56},{9,... | collective-permute-start | bytes 196616 | tf_op jit(solution)/shard_map/ppermute | solution.py:25
  93.2 4.3 %collective-permute-start.23 = (bf16[2,128,128]{2,1,0:T(8,128)(2,1)S(1)}, bf16[2,128,128]{2,1,0:T(8,128)(2,1)S(1)}, u32[]{:S(2)}, u32[]{:S(2)}) collective-permute-start(bf16[2,128,128]{2,1,0:T(8,128)(2,1)S(1)} %chip.1.sent), channel_id=1, source_target_pairs={{0,16},{1,17},{2,18},{3,19},{4,20},{5,21},{6,22},{7,23},{8,24},{9,... | collective-permute-start | bytes 196616 | tf_op jit(solution)/shard_map/ppermute | solution.py:25
  98.2 6.6 %collective-permute-start.28 = (bf16[2,128,128]{2,1,0:T(8,128)(2,1)S(1)}, bf16[2,128,128]{2,1,0:T(8,128)(2,1)S(1)}, u32[]{:S(2)}, u32[]{:S(2)}) collective-permute-start(bf16[2,128,128]{2,1,0:T(8,128)(2,1)S(1)} %get-tuple-element.67.sent), channel_id=1, source_target_pairs={{0,128},{1,129},{2,130},{3,131},{4,132},{5,133},{6,134},{7,135},{8... | collective-permute-start | bytes 196616 | tf_op jit(solution)/shard_map/ppermute | solution.py:25
  98.3 6.5 %collective-permute-start.27 = (bf16[2,128,128]{2,1,0:T(8,128)(2,1)S(1)}, bf16[2,128,128]{2,1,0:T(8,128)(2,1)S(1)}, u32[]{:S(2)}, u32[]{:S(2)}) collective-permute-start(bf16[2,128,128]{2,1,0:T(8,128)(2,1)S(1)} %get-tuple-element.67.sent), channel_id=1, source_target_pairs={{0,192},{1,193},{2,194},{3,195},{4,196},{5,197},{6,198},{7,199},{8... | collective-permute-start | bytes 196616 | tf_op jit(solution)/shard_map/ppermute | solution.py:25
  99.5 5.3 %collective-permute-start.26 = (bf16[2,128,128]{2,1,0:T(8,128)(2,1)S(1)}, bf16[2,128,128]{2,1,0:T(8,128)(2,1)S(1)}, u32[]{:S(2)}, u32[]{:S(2)}) collective-permute-start(bf16[2,128,128]{2,1,0:T(8,128)(2,1)S(1)} %get-tuple-element.67.sent), channel_id=1, source_target_pairs={{0,64},{1,65},{2,66},{3,67},{4,68},{5,69},{6,70},{7,71},{8,72},{9,... | collective-permute-start | bytes 196616 | tf_op jit(solution)/shard_map/ppermute | solution.py:25
  99.8 9.3 %copy-start.2 = (f32[512]{0:T(512)S(1)}, f32[512]{0:T(512)}, u32[]{:S(2)}) copy-start(f32[512]{0:T(512)} %param.12) | copy-start | bytes 6148
  105.5 3.7 %collective-permute-start.29 = (f32[2,2,128,128]{3,2,1,0:T(8,128)S(1)}, f32[2,2,128,128]{3,2,1,0:T(8,128)S(1)}, u32[]{:S(2)}, u32[]{:S(2)}) collective-permute-start(f32[2,2,128,128]{3,2,1,0:T(8,128)S(1)} %get-tuple-element.71), channel_id=1, source_target_pairs={{0,8},{1,9},{2,10},{3,11},{4,12},{5,13},{6,14},{7,15},{8,0},{9,1},... | collective-permute-start | bytes 786440 | tf_op jit(solution)/shard_map/ppermute | solution.py:25

commit v3 on v2

--- a/solution.py
+++ b/solution.py
@@ -73,19 +73,10 @@
     return acc
 
 
-def kv_kernel(pos, own, z1, z2, z3, a4, st, right, left, far_a, far_b, got_a, got_b, got_c, *outs):
-    kv_ref, r_ref, part_ref, give_ref, xa_ref, xb_ref = outs
-    mine = ((st, 1024), (right, 1024), (left, 1024), (far_a, 512), (far_b, 512))
-    other = ((got_a, 1024), (got_b, 2048), (got_c, 1024))
-    pieces = (
-        (own, 0), (z1, 0), (z2, 0), (z3, 0), (a4, 0), (got_a, 1024), (got_b, 2048), (got_c, 1024)
-    )
+def x_pass(pos, pieces, xa_ref, xb_ref, total):
     x, y, z, c = scalars(pos)
-    sign = 1 - 2 * c
-    shifts = [0] + [-k for k in range(1, 5)] + [k for k in range(1, 4)]
-    total = jnp.zeros((512, 128), F32)
-    for (piece, lo), k in zip(pieces, shifts):
-        at = lax.rem(z + sign * k + 2 * NZ, NZ)
+    for piece, lo, k in pieces:
+        at = lax.rem(z + (1 - 2 * c) * k + 2 * NZ, NZ)
         for h in range(2):
             q = 2 * at + h
             block = piece[lo : lo + 512, h * 256 : (h + 1) * 256]
@@ -94,6 +85,21 @@
             wide = block.astype(F32)
             wide = wide * wide
             total = total + wide[:, :128] + wide[:, 128:]
+    return total
+
+
+def x_kernel(pos, own, z1, z2, z3, got_a, xa_ref, xb_ref, squares_ref):
+    pieces = ((own, 0, 0), (z1, 0, -1), (z2, 0, -2), (z3, 0, -3), (got_a, 1024, 1))
+    squares_ref[...] = x_pass(pos, pieces, xa_ref, xb_ref, jnp.zeros((512, 128), F32))
+
+
+def kv_kernel(pos, xa_in, xb_in, squares, a4, st, right, left, far_a, far_b, got_a, got_b, *outs):
+    kv_ref, r_ref, part_ref, give_ref, xa_ref, xb_ref = outs
+    c = pos[3]
+    mine = ((st, 1024), (right, 1024), (left, 1024), (far_a, 512), (far_b, 512))
+    other = ((got_a, 1024), (got_b, 3072))
+    pieces = ((a4, 0, -4), (got_b, 3072, 2), (got_b, 3584, 3))
+    total = x_pass(pos, pieces, xa_ref, xb_ref, squares[...])
     r = lax.rsqrt(jnp.sum(total, axis=1, keepdims=True) * (1.0 / 4096) + 1e-05)
     r_ref[...] = jnp.broadcast_to(r, (512, 128))
 
@@ -160,11 +166,14 @@
     sizes = (1024, 1024, 1024, 512, 512, 3072, 1024)
     parts = tuple(zip(refs[:7], sizes))
     mine, other = parts[:5], parts[5:]
-    kv_ref, r_ref, carried_ref, q_ref, raw_ref = refs[7:]
+    r_ref, q_ref = refs[7:]
     c = pos[3]
     for x_ref, parts, to in ((xa_ref, mine, c), (xb_ref, other, 1 - c)):
         got = weights_dot(x_ref, parts, slice(0, 256)) * r_ref[:, :1]
         q_ref[:, pl.ds(pl.multiple_of(to * 256, 256), 256)] = got.astype(BF)
+
+
+def block_kernel(pos, q_ref, kv_ref, carried_ref, raw_ref):
     row = lax.broadcasted_iota(jnp.int32, (512, 512), 0)
     col = lax.broadcasted_iota(jnp.int32, (512, 512), 1)
 
@@ -198,13 +207,14 @@
 VMEM = pl.BlockSpec(memory_space=pltpu.VMEM)
 
 
-def kernel(body, name, outs, n_in, flops, space=VMEM, scratch=(), spaces=None, size=8):
+def kernel(body, name, outs, n_in, flops, space=VMEM, scratch=(), aliases=None, size=8):
     return pl.pallas_call(
         body,
         name=name,
         out_shape=tuple(jax.ShapeDtypeStruct(*o) for o in outs),
         in_specs=[SMEM] + (space if isinstance(space, list) else [space] * n_in),
-        out_specs=tuple(spaces or [VMEM] * len(outs)),
+        out_specs=(VMEM,) * len(outs),
+        input_output_aliases=aliases or {},
         scratch_shapes=scratch,
         compiler_params=pltpu.CompilerParams(vmem_limit_bytes=size << 20),
         cost_estimate=pl.CostEstimate(flops=flops, bytes_accessed=1 << 20, transcendentals=0),
@@ -227,14 +237,12 @@
     pick = lambda a, b: jnp.where(even, a, b)
 
     sib = swap(tokens)
-    g = lax.dynamic_slice(norm_gain, (s * 128,), (128,))[:, None]
-    scaled = lambda w: (w.astype(F32) * g).astype(BF)
-    wq, wk, wv = scaled(w_query), scaled(w_key), scaled(w_value)
-    qa, qb = wq[:, :256], wq[:, 256:]
-    mine = jnp.concatenate([pick(wk, wv), pick(qa, qb)], 1)
-    give = jnp.concatenate([pick(wv, wk), pick(qb, qa)], 1)
+    mine = jnp.concatenate([pick(w_key, w_value), pick(w_query[:, :256], w_query[:, 256:])], 1)
+    give = jnp.concatenate([pick(w_value, w_key), pick(w_query[:, 256:], w_query[:, :256])], 1)
     got = swap(after(give, sib))
+    g = lax.dynamic_slice(norm_gain, ((s // 2) * 256,), (256,))[:, None]
     chip = jnp.concatenate([pick(mine, got), pick(got, mine)], 0)
+    chip = (chip.astype(F32) * g).astype(BF)
     cat = jnp.concatenate
     z1 = along_z(after(cat([tokens, sib]), got))
     near = [first(chip, k) for k in (1, -1, 2)]
@@ -248,13 +256,19 @@
     z2, right, left, got_a = lax.optimization_barrier((z2, right, left, got_a))
     z3 = along_z(z2)
     far_a, far_b = second(right[:512], 1), second(left[512:], -1)
-    got_b = swap(cat([right, left, z2[512:]]))
-    z3, far_a, far_b, got_b = lax.optimization_barrier((z3, far_a, far_b, got_b))
+    qright, qleft = second(qst, 1), second(qst, -1)
+    z3, far_a, far_b, qright, qleft = lax.optimization_barrier((z3, far_a, far_b, qright, qleft))
     a4 = along_z(z3[:512])
-    qright, qleft = second(qst, 1), second(qst, -1)
-    got_c = swap(cat([far_a, far_b, z3[512:]]))
-    a4, qright, qleft, got_c = lax.optimization_barrier((a4, qright, qleft, got_c))
     qfar_a, qfar_b = second(qright[:512], 1), second(qleft[512:], -1)
+    got_b = swap(cat([right, left, far_a, far_b, z2[512:], z3[512:]]))
+    got_q = swap(cat([qst, qright, qleft]))
+    orders = [((512, 4096), BF), ((512, 4096), BF)]
+    xa, xb, squares = kernel(x_kernel, "x", orders + [((512, 128), F32)], 5, 1 << 31)(
+        pos, tokens, z1, z2, z3, got_a
+    )
+    a4, qfar_a, qfar_b, got_b, got_q, xa, xb, squares = lax.optimization_barrier(
+        (a4, qfar_a, qfar_b, got_b, got_q, xa, xb, squares)
+    )
     q_parts = (qst, qright, qleft, qfar_a, qfar_b)
 
     flops = 2 * 512 * 4096 * 1024
@@ -266,18 +280,18 @@
             ((512, 128), F32),
             ((2, 128, 128), F32),
             ((2, 128, 128), BF),
-            ((512, 4096), BF),
-            ((512, 4096), BF),
-        ],
-        13,
+        ]
+        + orders,
+        11,
         flops,
-    )(pos, tokens, z1, z2, z3, a4, st, right, left, far_a, far_b, got_a, got_b, got_c)
-    q_other = (
-        swap(cat([qst, qright, qleft])),
-        swap(after(cat([qfar_a, after(qfar_b, part)]), part)),
-    )
-    query, raw = kernel(q_kernel, "q", [((512, 512), BF), ((512, 512), F32)], 12, flops)(
-        pos, xa, xb, *q_parts, *q_other, kv_rows, r, carried
+        aliases={1: 4, 2: 5},
+    )(pos, xa, xb, squares, a4, st, right, left, far_a, far_b, got_a, got_b)
+    q_other = (got_q, swap(cat([qfar_a, qfar_b])))
+    (query,) = kernel(q_kernel, "q", [((512, 512), BF)], 10, flops // 2)(
+        pos, xa, xb, *q_parts, *q_other, r
+    )
+    (raw,) = kernel(block_kernel, "block", [((512, 512), F32)], 3, flops // 2)(
+        pos, query, kv_rows, carried
     )
 
     heads = (2, 128, 128)
@@ -286,6 +300,7 @@
         pos, part, from_sib
     )
     near = [by_y(sent, k) for k in (1, -1, 2)]
+    near[0] = after(near[0], query)
     before, row = kernel(row_kernel, "row", [(heads, F32), (heads, BF)], 4, 1 << 16)(
         pos, sent, *near
     )

time: 111 us -> 107 us (0.964)
  starting transfers between devices: 40.8 us -> 37.3 us
  waiting for transfers between devices: 48.4 us -> 46.5 us
    ppermute x30 -> x29, starting transfers between devices: 40.8 us -> 37.3 us  [move(): return lax.ppermute(a, BOTH, pairs)]
    pallas_call x1 -> x3, Pallas kernels: 4.91 us -> 7.1 us  [the longest x1 2.9 us: shards(): kernel(q_kernel, 'q', [((512, 512), BF)], 10, flops // 2)]
    ppermute x30 -> x29, waiting for transfers between devices: 48.4 us -> 46.5 us  [move(): return lax.ppermute(a, BOTH, pairs)]
    pallas_call x1, Pallas kernels: 8.24 us -> 7.02 us  [shards(): kernel(kv_kernel, 'kv', [((2, 512, 512), BF), ((512, 128), F32), ((2, 128...]
  transfers between devices with their start and end apart: 30 -> 29, of which waited for: 15 -> 16; matrix products, arithmetic and copies ran while one was open for 3% -> 3% of each run, Pallas kernels for 13% -> 14%
where the time goes in v3:
time: 107 us
  waiting for transfers between devices  46.5 us (43%)
  starting transfers between devices  37.3 us (35%)
  Pallas kernels  17.9 us (17%)
  other arithmetic  2.38 us (2%)
  local copies, waits for them, and re-layouts  1.52 us (1%)
    ppermute x29, waiting for transfers between devices, move(): return lax.ppermute(a, BOTH, pairs)  46.5 us
    ppermute x29, starting transfers between devices, move(): return lax.ppermute(a, BOTH, pairs)  37.3 us
    pallas_call x1, Pallas kernels, shards(): kernel(kv_kernel, 'kv', [((2, 512, 512), BF), ((512, 128), F32), ((2, 128...  7.02 us
    pallas_call x1, Pallas kernels, shards(): kernel(q_kernel, 'q', [((512, 512), BF)], 10, flops // 2)  2.9 us
    pallas_call x1, Pallas kernels, shards(): kernel(block_kernel, 'block', [((512, 512), F32)], 3, flops // 2)  2.56 us
  transfers between devices with their start and end apart: 29, of which 16 were waited for; matrix products, arithmetic and copies ran while one was open for 3% of the time, Pallas kernels for 14%

profile of v3, /device:TPU:1, one launch (start us, length us, event | category | flops | bytes accessed | tf_op | source)
XLA Modules:
  0.0 106.6 jit_solution(5854807035814930341)
XLA Ops:
  0.6 0.0 copy-start
  0.7 0.1 pad_add_fusion.pos
  0.7 3.3 %collective-permute-start = (bf16[512,512]{1,0:T(8,128)(2,1)}, bf16[512,512]{1,0:T(8,128)(2,1)S(1)}, u32[]{:S(2)}, u32[]{:S(2)}) collective-permute-start(bf16[512,512]{1,0:T(8,128)(2,1)} %own), channel_id=1, source_target_pairs={{0,8},{1,9},{2,10},{3,11},{4,12},{5,13},{6,14},{7,15},{8,0},{9,1},... | collective-permute-start | bytes 1572872 | tf_op jit(solution)/shard_map/ppermute | solution.py:25
  4.0 0.9 broadcast_select_fusion.4
  4.9 1.0 broadcast_select_fusion.2
  5.9 0.0 collective-permute-done
  5.9 0.2 collective-permute-start.1
  6.1 0.1 pad_maximum_fusion
  6.2 1.2 %collective-permute-done.1 = bf16[128,768]{1,0:T(8,128)(2,1)S(1)} collective-permute-done((bf16[128,768]{1,0:T(8,128)(2,1)S(1)}, bf16[128,768]{1,0:T(8,128)(2,1)S(1)}, u32[]{:S(2)}, u32[]{:S(2)}) %collective-permute-start.1) | collective-permute-done | bytes 196640 | tf_op jit(solution)/shard_map/ppermute | solution.py:25
  7.5 3.8 %collective-permute-start.2 = (bf16[1024,512]{1,0:T(8,128)(2,1)S(1)}, bf16[1024,512]{1,0:T(8,128)(2,1)S(1)}, u32[]{:S(2)}, u32[]{:S(2)}) collective-permute-start(bf16[1024,512]{1,0:T(8,128)(2,1)S(1)} %pad_maximum_fusion), channel_id=1, source_target_pairs={{0,1},{1,2},{2,3},{3,4},{4,5},{5,6},{6,7},{7,0},{8,15},{9,8},{10,9... | collective-permute-start | bytes 3145736 | tf_op jit(solution)/shard_map/ppermute | solution.py:25
  11.3 0.8 dynamic_slice.3
  12.1 0.1 broadcast_select_fusion.1
  12.1 0.1 multiply_convert_fusion
  12.3 3.0 %collective-permute-start.5 = (bf16[256,768]{1,0:T(8,128)(2,1)S(1)}, bf16[256,768]{1,0:T(8,128)(2,1)S(1)}, u32[]{:S(2)}, u32[]{:S(2)}) collective-permute-start(bf16[256,768]{1,0:T(8,128)(2,1)S(1)} %multiply_convert_fusion), channel_id=1, source_target_pairs={{0,128},{1,129},{2,130},{3,131},{4,132},{5,133},{6,134},{7,135},{8... | collective-permute-start | bytes 1179656 | tf_op jit(solution)/shard_map/ppermute | solution.py:25
  15.3 0.8 collective-permute-start.4
  16.0 0.7 collective-permute-start.3
  16.8 3.8 %collective-permute-done.5 = bf16[256,768]{1,0:T(8,128)(2,1)S(1)} collective-permute-done((bf16[256,768]{1,0:T(8,128)(2,1)S(1)}, bf16[256,768]{1,0:T(8,128)(2,1)S(1)}, u32[]{:S(2)}, u32[]{:S(2)}) %collective-permute-start.5) | collective-permute-done | bytes 393248 | tf_op jit(solution)/shard_map/ppermute | solution.py:25
  20.6 4.5 %collective-permute-done.4 = bf16[256,768]{1,0:T(8,128)(2,1)S(1)} collective-permute-done((bf16[256,768]{1,0:T(8,128)(2,1)S(1)}, bf16[256,768]{1,0:T(8,128)(2,1)S(1)}, u32[]{:S(2)}, u32[]{:S(2)}) %collective-permute-start.4) | collective-permute-done | bytes 393248 | tf_op jit(solution)/shard_map/ppermute | solution.py:25
  25.3 0.1 collective-permute-start.9
  25.4 1.1 %collective-permute-start.6 = (bf16[1024,512]{1,0:T(8,128)(2,1)S(1)}, bf16[1024,512]{1,0:T(8,128)(2,1)S(1)}, u32[]{:S(2)}, u32[]{:S(2)}) collective-permute-start(bf16[1024,512]{1,0:T(8,128)(2,1)S(1)} %collective-permute-done.2.z1), channel_id=1, source_target_pairs={{0,1},{1,2},{2,3},{3,4},{4,5},{5,6},{6,7},{7,0},{8,15},{9,8},{10,9... | collective-permute-start | bytes 3145736 | tf_op jit(solution)/shard_map/ppermute | solution.py:25
  26.5 0.1 pad_maximum_fusion.1.st
  26.6 2.6 %collective-permute-start.8 = (bf16[1024,512]{1,0:T(8,128)(2,1)S(1)}, bf16[1024,512]{1,0:T(8,128)(2,1)S(1)}, u32[]{:S(2)}, u32[]{:S(2)}) collective-permute-start(bf16[1024,512]{1,0:T(8,128)(2,1)S(1)} %pad_maximum_fusion.1.st), channel_id=1, source_target_pairs={{0,48},{1,49},{2,50},{3,51},{4,52},{5,53},{6,54},{7,55},{8,200},{9... | collective-permute-start | bytes 3145736 | tf_op jit(solution)/shard_map/ppermute | solution.py:25
  29.2 10.2 %collective-permute-done.6.z2 = bf16[1024,512]{1,0:T(8,128)(2,1)S(1)} collective-permute-done((bf16[1024,512]{1,0:T(8,128)(2,1)S(1)}, bf16[1024,512]{1,0:T(8,128)(2,1)S(1)}, u32[]{:S(2)}, u32[]{:S(2)}) %collective-permute-start.6) | collective-permute-done | bytes 1048608 | tf_op jit(solution)/shard_map/ppermute | solution.py:25
  39.4 1.5 %collective-permute-done.8.left = bf16[1024,512]{1,0:T(8,128)(2,1)S(1)} collective-permute-done((bf16[1024,512]{1,0:T(8,128)(2,1)S(1)}, bf16[1024,512]{1,0:T(8,128)(2,1)S(1)}, u32[]{:S(2)}, u32[]{:S(2)}) %collective-permute-start.8) | collective-permute-done | bytes 1048608 | tf_op jit(solution)/shard_map/ppermute | solution.py:25
  40.9 3.4 %collective-permute-done.7.right = bf16[1024,512]{1,0:T(8,128)(2,1)S(1)} collective-permute-done((bf16[1024,512]{1,0:T(8,128)(2,1)S(1)}, bf16[1024,512]{1,0:T(8,128)(2,1)S(1)}, u32[]{:S(2)}, u32[]{:S(2)}) %collective-permute-start.7) | collective-permute-done | bytes 1048608 | tf_op jit(solution)/shard_map/ppermute | solution.py:25
  44.3 1.5 %collective-permute-start.10 = (bf16[1024,512]{1,0:T(8,128)(2,1)S(1)}, bf16[1024,512]{1,0:T(8,128)(2,1)S(1)}, u32[]{:S(2)}, u32[]{:S(2)}) collective-permute-start(bf16[1024,512]{1,0:T(8,128)(2,1)S(1)} %collective-permute-done.6.z2), channel_id=1, source_target_pairs={{0,1},{1,2},{2,3},{3,4},{4,5},{5,6},{6,7},{7,0},{8,15},{9,8},{10,9... | collective-permute-start | bytes 3145736 | tf_op jit(solution)/shard_map/ppermute | solution.py:25
  45.9 0.1 collective-permute-start.14
  46.0 1.5 %collective-permute-start.13 = (bf16[1024,256]{1,0:T(8,128)(2,1)S(1)}, bf16[1024,256]{1,0:T(8,128)(2,1)S(1)}, u32[]{:S(2)}, u32[]{:S(2)}) collective-permute-start(bf16[1024,256]{1,0:T(8,128)(2,1)S(1)} %pad_maximum_fusion.2.refs_0_), channel_id=1, source_target_pairs={{0,16},{1,17},{2,18},{3,19},{4,20},{5,21},{6,22},{7,23},{8,72},{9,... | collective-permute-start | bytes 1572872 | tf_op jit(solution)/shard_map/ppermute | solution.py:25
  47.5 1.4 %collective-permute-start.12 = (bf16[512,512]{1,0:T(8,128)(2,1)S(1)}, bf16[512,512]{1,0:T(8,128)(2,1)S(1)}, u32[]{:S(2)}, u32[]{:S(2)}) collective-permute-start(bf16[512,512]{1,0:T(8,128)(2,1)S(1)} %slice.64), channel_id=1, source_target_pairs={{0,48},{1,49},{2,50},{3,51},{4,52},{5,53},{6,54},{7,55},{8,200},{9... | collective-permute-start | bytes 1572872 | tf_op jit(solution)/shard_map/ppermute | solution.py:25
  48.9 0.2 collective-permute-start.11
  49.1 0.1 constant_dynamic-update-slice_fusion.7
  49.1 0.1 constant_dynamic-update-slice_fusion.6
  49.2 5.1 %collective-permute-done.14.refs_2_ = bf16[1024,256]{1,0:T(8,128)(2,1)S(1)} collective-permute-done((bf16[1024,256]{1,0:T(8,128)(2,1)S(1)}, bf16[1024,256]{1,0:T(8,128)(2,1)S(1)}, u32[]{:S(2)}, u32[]{:S(2)}) %collective-permute-start.14) | collective-permute-done | bytes 524320 | tf_op jit(solution)/shard_map/ppermute | solution.py:25
  54.3 1.3 %collective-permute-done.13.refs_1_ = bf16[1024,256]{1,0:T(8,128)(2,1)S(1)} collective-permute-done((bf16[1024,256]{1,0:T(8,128)(2,1)S(1)}, bf16[1024,256]{1,0:T(8,128)(2,1)S(1)}, u32[]{:S(2)}, u32[]{:S(2)}) %collective-permute-start.13) | collective-permute-done | bytes 524320 | tf_op jit(solution)/shard_map/ppermute | solution.py:25
  55.6 4.3 %collective-permute-done.12.far_b = bf16[512,512]{1,0:T(8,128)(2,1)S(1)} collective-permute-done((bf16[512,512]{1,0:T(8,128)(2,1)S(1)}, bf16[512,512]{1,0:T(8,128)(2,1)S(1)}, u32[]{:S(2)}, u32[]{:S(2)}) %collective-permute-start.12) | collective-permute-done | bytes 524320 | tf_op jit(solution)/shard_map/ppermute | solution.py:25
  59.9 1.3 %collective-permute-done.11.far_a = bf16[512,512]{1,0:T(8,128)(2,1)S(1)} collective-permute-done((bf16[512,512]{1,0:T(8,128)(2,1)S(1)}, bf16[512,512]{1,0:T(8,128)(2,1)S(1)}, u32[]{:S(2)}, u32[]{:S(2)}) %collective-permute-start.11) | collective-permute-done | bytes 524320 | tf_op jit(solution)/shard_map/ppermute | solution.py:25
  61.3 0.1 slice_dynamic-update-slice_fusion
  61.4 1.2 %collective-permute-start.18 = (bf16[4096,512]{1,0:T(8,128)(2,1)S(1)}, bf16[4096,512]{1,0:T(8,128)(2,1)S(1)}, u32[]{:S(2)}, u32[]{:S(2)}) collective-permute-start(bf16[4096,512]{1,0:T(8,128)(2,1)S(1)} %get-tuple-element.82), channel_id=1, source_target_pairs={{0,8},{1,9},{2,10},{3,11},{4,12},{5,13},{6,14},{7,15},{8,0},{9,1},... | collective-permute-start | bytes 12582920 | tf_op jit(solution)/shard_map/ppermute | solution.py:25
  62.7 0.1 collective-permute-start.19
  62.8 1.9 %collective-permute-start.15 = (bf16[512,512]{1,0:T(8,128)(2,1)S(1)}, bf16[512,512]{1,0:T(8,128)(2,1)S(1)}, u32[]{:S(2)}, u32[]{:S(2)}) collective-permute-start(bf16[512,512]{1,0:T(8,128)(2,1)S(1)} %get-tuple-element.83), channel_id=1, source_target_pairs={{0,1},{1,2},{2,3},{3,4},{4,5},{5,6},{6,7},{7,0},{8,15},{9,8},{10,9... | collective-permute-start | bytes 1572872 | tf_op jit(solution)/shard_map/ppermute | solution.py:25
  64.7 2.6 %collective-permute-start.17 = (bf16[512,256]{1,0:T(8,128)(2,1)S(1)}, bf16[512,256]{1,0:T(8,128)(2,1)S(1)}, u32[]{:S(2)}, u32[]{:S(2)}) collective-permute-start(bf16[512,256]{1,0:T(8,128)(2,1)S(1)} %slice.71), channel_id=1, source_target_pairs={{0,48},{1,49},{2,50},{3,51},{4,52},{5,53},{6,54},{7,55},{8,200},{9... | collective-permute-start | bytes 786440 | tf_op jit(solution)/shard_map/ppermute | solution.py:25
  67.2 0.0 collective-permute-start.16
  67.2 1.6 %x.1 = (bf16[512,4096]{1,0:T(8,128)(2,1)S(1)}, bf16[512,4096]{1,0:T(8,128)(2,1)S(1)}, f32[512,128]{1,0:T(8,128)S(1)}) custom-call(s32[4]{0:T(128)S(1)} %pad_add_fusion.pos, bf16[512,512]{1,0:T(8,128)(2,1)S(1)} %copy-done, bf16[1024,512]{1,0:T(8,128)(2,1)S(1)} %collective-permute-done.2.z1, bf16[1024,512]{1,0:T(8,128)(2,1)S(1)} %collective-permute-done.6.z2, ...), custom_call_target="tpu_custom_call" | custom-call | flops 2147483648 | bytes 1048576 | tf_op jit(solution)/shard_map/x/pallas_call | solution.py:266
  68.9 1.7 %collective-permute-done.17.refs_4_ = bf16[512,256]{1,0:T(8,128)(2,1)S(1)} collective-permute-done((bf16[512,256]{1,0:T(8,128)(2,1)S(1)}, bf16[512,256]{1,0:T(8,128)(2,1)S(1)}, u32[]{:S(2)}, u32[]{:S(2)}) %collective-permute-start.17) | collective-permute-done | bytes 262176 | tf_op jit(solution)/shard_map/ppermute | solution.py:25
  70.5 3.2 %collective-permute-done.16.refs_3_ = bf16[512,256]{1,0:T(8,128)(2,1)S(1)} collective-permute-done((bf16[512,256]{1,0:T(8,128)(2,1)S(1)}, bf16[512,256]{1,0:T(8,128)(2,1)S(1)}, u32[]{:S(2)}, u32[]{:S(2)}) %collective-permute-start.16) | collective-permute-done | bytes 262176 | tf_op jit(solution)/shard_map/ppermute | solution.py:25
  73.9 0.5 collective-permute-start.20
  74.3 7.0 %kv.1 = (bf16[2,512,512]{2,1,0:T(8,128)(2,1)S(1)}, f32[512,128]{1,0:T(8,128)S(1)}, f32[2,128,128]{2,1,0:T(8,128)S(1)}, bf16[2,128,128]{2,1,0:T(8,128)(2,1)S(1)},...) custom-call(s32[4]{0:T(128)S(1)} %pad_add_fusion.pos, ...), custom_call_target="tpu_custom_call", output_to_operand_aliasing={{4}: (1, {}), {5}: (2, {})} | custom-call | flops 4294967296 | bytes 1048576 | tf_op jit(solution)/shard_map/kv/pallas_call | solution.py:275
  81.4 0.2 collective-permute-start.21
  81.6 1.1 %collective-permute-done.21.sib_ref = bf16[2,128,128]{2,1,0:T(8,128)(2,1)S(1)} collective-permute-done((bf16[2,128,128]{2,1,0:T(8,128)(2,1)S(1)}, bf16[2,128,128]{2,1,0:T(8,128)(2,1)S(1)}, u32[]{:S(2)}, u32[]{:S(2)}) %collective-permute-start.21) | collective-permute-done | bytes 65568 | tf_op jit(solution)/shard_map/ppermute | solution.py:25
  82.7 0.6 chip.1.sent
  83.3 1.3 %collective-permute-start.24 = (bf16[2,128,128]{2,1,0:T(8,128)(2,1)S(1)}, bf16[2,128,128]{2,1,0:T(8,128)(2,1)S(1)}, u32[]{:S(2)}, u32[]{:S(2)}) collective-permute-start(bf16[2,128,128]{2,1,0:T(8,128)(2,1)S(1)} %chip.1.sent), channel_id=1, source_target_pairs={{0,32},{1,33},{2,34},{3,35},{4,36},{5,37},{6,38},{7,39},{8,40},{9,... | collective-permute-start | bytes 196616 | tf_op jit(solution)/shard_map/ppermute | solution.py:25
  84.6 1.6 %collective-permute-start.23 = (bf16[2,128,128]{2,1,0:T(8,128)(2,1)S(1)}, bf16[2,128,128]{2,1,0:T(8,128)(2,1)S(1)}, u32[]{:S(2)}, u32[]{:S(2)}) collective-permute-start(bf16[2,128,128]{2,1,0:T(8,128)(2,1)S(1)} %chip.1.sent), channel_id=1, source_target_pairs={{0,48},{1,49},{2,50},{3,51},{4,52},{5,53},{6,54},{7,55},{8,56},{9,... | collective-permute-start | bytes 196616 | tf_op jit(solution)/shard_map/ppermute | solution.py:25
  86.2 2.9 %q.1.q_ref = bf16[512,512]{1,0:T(8,128)(2,1)S(1)} custom-call(s32[4]{0:T(128)S(1)} %pad_add_fusion.pos, bf16[512,4096]{1,0:T(8,128)(2,1)S(1)} %get-tuple-element.67.xa_ref, bf16[512,4096]{1,0:T(8,128)(2,1)S(1)} %get-tuple-element.68.xb_ref, bf16[1024,256]{1,0:T(8,128)(2,1)S(1)} %pad_maximum_fusion.2.refs_0_, ...), custom_call_target="tpu_custom_call" | custom-call | flops 2147483648 | bytes 1048576 | tf_op jit(solution)/shard_map/q/pallas_call | solution.py:290
  89.1 1.4 %collective-permute-done.22.behind = bf16[2,128,128]{2,1,0:T(8,128)(2,1)S(1)} collective-permute-done((bf16[2,128,128]{2,1,0:T(8,128)(2,1)S(1)}, bf16[2,128,128]{2,1,0:T(8,128)(2,1)S(1)}, u32[]{:S(2)}, u32[]{:S(2)}) %collective-permute-start.22) | collective-permute-done | bytes 65568 | tf_op jit(solution)/shard_map/ppermute | solution.py:25
  90.5 0.6 row.1
  91.2 2.7 %collective-permute-start.27 = (bf16[2,128,128]{2,1,0:T(8,128)(2,1)S(1)}, bf16[2,128,128]{2,1,0:T(8,128)(2,1)S(1)}, u32[]{:S(2)}, u32[]{:S(2)}) collective-permute-start(bf16[2,128,128]{2,1,0:T(8,128)(2,1)S(1)} %get-tuple-element.77.sent), channel_id=1, source_target_pairs={{0,128},{1,129},{2,130},{3,131},{4,132},{5,133},{6,134},{7,135},{8... | collective-permute-start | bytes 196616 | tf_op jit(solution)/shard_map/ppermute | solution.py:25
  93.9 0.9 collective-permute-start.26
  94.8 0.5 collective-permute-start.25
  95.3 2.6 %block.1.raw_ref = f32[512,512]{1,0:T(8,128)S(1)} custom-call(s32[4]{0:T(128)S(1)} %pad_add_fusion.pos, bf16[512,512]{1,0:T(8,128)(2,1)S(1)} %q.1.q_ref, bf16[2,512,512]{2,1,0:T(8,128)(2,1)S(1)} %get-tuple-element.73.kv_ref, f32[4,128,128]{2,1,0:T(8,128)S(1)} %copy-done.1), custom_call_target="tpu_custom_call" | custom-call | flops 2147483648 | bytes 1048576 | tf_op jit(solution)/shard_map/block/pallas_call | solution.py:293
  97.9 1.2 %collective-permute-done.25.behind = bf16[2,128,128]{2,1,0:T(8,128)(2,1)S(1)} collective-permute-done((bf16[2,128,128]{2,1,0:T(8,128)(2,1)S(1)}, bf16[2,128,128]{2,1,0:T(8,128)(2,1)S(1)}, u32[]{:S(2)}, u32[]{:S(2)}) %collective-permute-start.25) | collective-permute-done | bytes 65568 | tf_op jit(solution)/shard_map/ppermute | solution.py:25
  99.1 0.6 plane.1
  99.8 3.7 %collective-permute-start.28 = (f32[2,2,128,128]{3,2,1,0:T(8,128)S(1)}, f32[2,2,128,128]{3,2,1,0:T(8,128)S(1)}, u32[]{:S(2)}, u32[]{:S(2)}) collective-permute-start(f32[2,2,128,128]{3,2,1,0:T(8,128)S(1)} %get-tuple-element.81), channel_id=1, source_target_pairs={{0,8},{1,9},{2,10},{3,11},{4,12},{5,13},{6,14},{7,15},{8,0},{9,1},... | collective-permute-start | bytes 786440 | tf_op jit(solution)/shard_map/ppermute | solution.py:25
  103.4 1.2 %collective-permute-done.28.both_ref = f32[2,2,128,128]{3,2,1,0:T(8,128)S(1)} collective-permute-done((f32[2,2,128,128]{3,2,1,0:T(8,128)S(1)}, f32[2,2,128,128]{3,2,1,0:T(8,128)S(1)}, u32[]{:S(2)}, u32[]{:S(2)}) %collective-permute-start.28) | collective-permute-done | bytes 262176 | tf_op jit(solution)/shard_map/ppermute | solution.py:25
  104.6 2.0 %out.1 = (bf16[512,512]{1,0:T(8,128)(2,1)}, f32[4,128,128]{2,1,0:T(8,128)}) custom-call(s32[4]{0:T(128)S(1)} %pad_add_fusion.pos, bf16[512,512]{1,0:T(8,128)(2,1)S(1)} %q.1.q_ref, f32[512,512]{1,0:T(8,128)S(1)} %block.1.raw_ref, f32[2,2,128,128]{3,2,1,0:T(8,128)S(1)} %get-tuple-element.80.mine_ref, f32[2,2,128,128]{3,2,1,0:T(8,128)S(1)} %collective-permute-done.28.both_ref, ...), custom_call_target="tpu_custom_call" | custom-call | flops 268435456 | bytes 1048576 | tf_op jit(solution)/shard_map/out/pallas_call | solution.py:313
  (40 shorter events, 0.7 us)
Async XLA Ops:
  0.6 5.5 %copy-start = (bf16[512,512]{1,0:T(8,128)(2,1)S(1)}, bf16[512,512]{1,0:T(8,128)(2,1)}, u32[]{:S(2)}) copy-start(bf16[512,512]{1,0:T(8,128)(2,1)} %own) | copy-start | bytes 1572868
  0.7 5.2 %collective-permute-start = (bf16[512,512]{1,0:T(8,128)(2,1)}, bf16[512,512]{1,0:T(8,128)(2,1)S(1)}, u32[]{:S(2)}, u32[]{:S(2)}) collective-permute-start(bf16[512,512]{1,0:T(8,128)(2,1)} %own), channel_id=1, source_target_pairs={{0,8},{1,9},{2,10},{3,11},{4,12},{5,13},{6,14},{7,15},{8,0},{9,1},... | collective-permute-start | bytes 1572872 | tf_op jit(solution)/shard_map/ppermute | solution.py:25
  5.9 1.5 %collective-permute-start.1 = (bf16[128,768]{1,0:T(8,128)(2,1)S(1)}, bf16[128,768]{1,0:T(8,128)(2,1)S(1)}, u32[]{:S(2)}, u32[]{:S(2)}) collective-permute-start(bf16[128,768]{1,0:T(8,128)(2,1)S(1)} %pad_maximum_fusion.4), channel_id=1, source_target_pairs={{0,8},{1,9},{2,10},{3,11},{4,12},{5,13},{6,14},{7,15},{8,0},{9,1},... | collective-permute-start | bytes 589832 | tf_op jit(solution)/shard_map/ppermute | solution.py:25
  7.5 17.6 %collective-permute-start.2 = (bf16[1024,512]{1,0:T(8,128)(2,1)S(1)}, bf16[1024,512]{1,0:T(8,128)(2,1)S(1)}, u32[]{:S(2)}, u32[]{:S(2)}) collective-permute-start(bf16[1024,512]{1,0:T(8,128)(2,1)S(1)} %pad_maximum_fusion), channel_id=1, source_target_pairs={{0,1},{1,2},{2,3},{3,4},{4,5},{5,6},{6,7},{7,0},{8,15},{9,8},{10,9... | collective-permute-start | bytes 3145736 | tf_op jit(solution)/shard_map/ppermute | solution.py:25
  12.3 8.3 %collective-permute-start.5 = (bf16[256,768]{1,0:T(8,128)(2,1)S(1)}, bf16[256,768]{1,0:T(8,128)(2,1)S(1)}, u32[]{:S(2)}, u32[]{:S(2)}) collective-permute-start(bf16[256,768]{1,0:T(8,128)(2,1)S(1)} %multiply_convert_fusion), channel_id=1, source_target_pairs={{0,128},{1,129},{2,130},{3,131},{4,132},{5,133},{6,134},{7,135},{8... | collective-permute-start | bytes 1179656 | tf_op jit(solution)/shard_map/ppermute | solution.py:25
  15.3 9.8 %collective-permute-start.4 = (bf16[256,768]{1,0:T(8,128)(2,1)S(1)}, bf16[256,768]{1,0:T(8,128)(2,1)S(1)}, u32[]{:S(2)}, u32[]{:S(2)}) collective-permute-start(bf16[256,768]{1,0:T(8,128)(2,1)S(1)} %multiply_convert_fusion), channel_id=1, source_target_pairs={{0,192},{1,193},{2,194},{3,195},{4,196},{5,197},{6,198},{7,199},{8... | collective-permute-start | bytes 1179656 | tf_op jit(solution)/shard_map/ppermute | solution.py:25
  16.0 9.0 %collective-permute-start.3 = (bf16[256,768]{1,0:T(8,128)(2,1)S(1)}, bf16[256,768]{1,0:T(8,128)(2,1)S(1)}, u32[]{:S(2)}, u32[]{:S(2)}) collective-permute-start(bf16[256,768]{1,0:T(8,128)(2,1)S(1)} %multiply_convert_fusion), channel_id=1, source_target_pairs={{0,64},{1,65},{2,66},{3,67},{4,68},{5,69},{6,70},{7,71},{8,24},{9,... | collective-permute-start | bytes 1179656 | tf_op jit(solution)/shard_map/ppermute | solution.py:25
  25.3 19.0 %collective-permute-start.9 = (bf16[1536,512]{1,0:T(8,128)(2,1)S(1)}, bf16[1536,512]{1,0:T(8,128)(2,1)S(1)}, u32[]{:S(2)}, u32[]{:S(2)}) collective-permute-start(bf16[1536,512]{1,0:T(8,128)(2,1)S(1)} %slice_dynamic-update-slice_fusion.2), channel_id=1, source_target_pairs={{0,8},{1,9},{2,10},{3,11},{4,12},{5,13},{6,14},{7,15},{8,0},{9,1},... | collective-permute-start | bytes 4718600 | tf_op jit(solution)/shard_map/ppermute | solution.py:25
  25.4 14.0 %collective-permute-start.6 = (bf16[1024,512]{1,0:T(8,128)(2,1)S(1)}, bf16[1024,512]{1,0:T(8,128)(2,1)S(1)}, u32[]{:S(2)}, u32[]{:S(2)}) collective-permute-start(bf16[1024,512]{1,0:T(8,128)(2,1)S(1)} %collective-permute-done.2.z1), channel_id=1, source_target_pairs={{0,1},{1,2},{2,3},{3,4},{4,5},{5,6},{6,7},{7,0},{8,15},{9,8},{10,9... | collective-permute-start | bytes 3145736 | tf_op jit(solution)/shard_map/ppermute | solution.py:25
  26.6 14.3 %collective-permute-start.8 = (bf16[1024,512]{1,0:T(8,128)(2,1)S(1)}, bf16[1024,512]{1,0:T(8,128)(2,1)S(1)}, u32[]{:S(2)}, u32[]{:S(2)}) collective-permute-start(bf16[1024,512]{1,0:T(8,128)(2,1)S(1)} %pad_maximum_fusion.1.st), channel_id=1, source_target_pairs={{0,48},{1,49},{2,50},{3,51},{4,52},{5,53},{6,54},{7,55},{8,200},{9... | collective-permute-start | bytes 3145736 | tf_op jit(solution)/shard_map/ppermute | solution.py:25
  29.1 15.1 %collective-permute-start.7 = (bf16[1024,512]{1,0:T(8,128)(2,1)S(1)}, bf16[1024,512]{1,0:T(8,128)(2,1)S(1)}, u32[]{:S(2)}, u32[]{:S(2)}) collective-permute-start(bf16[1024,512]{1,0:T(8,128)(2,1)S(1)} %pad_maximum_fusion.1.st), channel_id=1, source_target_pairs={{0,16},{1,17},{2,18},{3,19},{4,20},{5,21},{6,22},{7,23},{8,72},{9,... | collective-permute-start | bytes 3145736 | tf_op jit(solution)/shard_map/ppermute | solution.py:25
  44.3 16.9 %collective-permute-start.10 = (bf16[1024,512]{1,0:T(8,128)(2,1)S(1)}, bf16[1024,512]{1,0:T(8,128)(2,1)S(1)}, u32[]{:S(2)}, u32[]{:S(2)}) collective-permute-start(bf16[1024,512]{1,0:T(8,128)(2,1)S(1)} %collective-permute-done.6.z2), channel_id=1, source_target_pairs={{0,1},{1,2},{2,3},{3,4},{4,5},{5,6},{6,7},{7,0},{8,15},{9,8},{10,9... | collective-permute-start | bytes 3145736 | tf_op jit(solution)/shard_map/ppermute | solution.py:25
  45.9 8.4 %collective-permute-start.14 = (bf16[1024,256]{1,0:T(8,128)(2,1)S(1)}, bf16[1024,256]{1,0:T(8,128)(2,1)S(1)}, u32[]{:S(2)}, u32[]{:S(2)}) collective-permute-start(bf16[1024,256]{1,0:T(8,128)(2,1)S(1)} %pad_maximum_fusion.2.refs_0_), channel_id=1, source_target_pairs={{0,48},{1,49},{2,50},{3,51},{4,52},{5,53},{6,54},{7,55},{8,200},{9... | collective-permute-start | bytes 1572872 | tf_op jit(solution)/shard_map/ppermute | solution.py:25
  46.0 9.6 %collective-permute-start.13 = (bf16[1024,256]{1,0:T(8,128)(2,1)S(1)}, bf16[1024,256]{1,0:T(8,128)(2,1)S(1)}, u32[]{:S(2)}, u32[]{:S(2)}) collective-permute-start(bf16[1024,256]{1,0:T(8,128)(2,1)S(1)} %pad_maximum_fusion.2.refs_0_), channel_id=1, source_target_pairs={{0,16},{1,17},{2,18},{3,19},{4,20},{5,21},{6,22},{7,23},{8,72},{9,... | collective-permute-start | bytes 1572872 | tf_op jit(solution)/shard_map/ppermute | solution.py:25
  47.5 12.4 %collective-permute-start.12 = (bf16[512,512]{1,0:T(8,128)(2,1)S(1)}, bf16[512,512]{1,0:T(8,128)(2,1)S(1)}, u32[]{:S(2)}, u32[]{:S(2)}) collective-permute-start(bf16[512,512]{1,0:T(8,128)(2,1)S(1)} %slice.64), channel_id=1, source_target_pairs={{0,48},{1,49},{2,50},{3,51},{4,52},{5,53},{6,54},{7,55},{8,200},{9... | collective-permute-start | bytes 1572872 | tf_op jit(solution)/shard_map/ppermute | solution.py:25
  48.9 12.3 %collective-permute-start.11 = (bf16[512,512]{1,0:T(8,128)(2,1)S(1)}, bf16[512,512]{1,0:T(8,128)(2,1)S(1)}, u32[]{:S(2)}, u32[]{:S(2)}) collective-permute-start(bf16[512,512]{1,0:T(8,128)(2,1)S(1)} %slice.63), channel_id=1, source_target_pairs={{0,16},{1,17},{2,18},{3,19},{4,20},{5,21},{6,22},{7,23},{8,72},{9,... | collective-permute-start | bytes 1572872 | tf_op jit(solution)/shard_map/ppermute | solution.py:25
  61.4 12.4 %collective-permute-start.18 = (bf16[4096,512]{1,0:T(8,128)(2,1)S(1)}, bf16[4096,512]{1,0:T(8,128)(2,1)S(1)}, u32[]{:S(2)}, u32[]{:S(2)}) collective-permute-start(bf16[4096,512]{1,0:T(8,128)(2,1)S(1)} %get-tuple-element.82), channel_id=1, source_target_pairs={{0,8},{1,9},{2,10},{3,11},{4,12},{5,13},{6,14},{7,15},{8,0},{9,1},... | collective-permute-start | bytes 12582920 | tf_op jit(solution)/shard_map/ppermute | solution.py:25
  62.7 11.1 %collective-permute-start.19 = (bf16[3072,256]{1,0:T(8,128)(2,1)S(1)}, bf16[3072,256]{1,0:T(8,128)(2,1)S(1)}, u32[]{:S(2)}, u32[]{:S(2)}) collective-permute-start(bf16[3072,256]{1,0:T(8,128)(2,1)S(1)} %constant_dynamic-update-slice_fusion.8), channel_id=1, source_target_pairs={{0,8},{1,9},{2,10},{3,11},{4,12},{5,13},{6,14},{7,15},{8,0},{9,1},... | collective-permute-start | bytes 4718600 | tf_op jit(solution)/shard_map/ppermute | solution.py:25
  62.8 11.0 %collective-permute-start.15 = (bf16[512,512]{1,0:T(8,128)(2,1)S(1)}, bf16[512,512]{1,0:T(8,128)(2,1)S(1)}, u32[]{:S(2)}, u32[]{:S(2)}) collective-permute-start(bf16[512,512]{1,0:T(8,128)(2,1)S(1)} %get-tuple-element.83), channel_id=1, source_target_pairs={{0,1},{1,2},{2,3},{3,4},{4,5},{5,6},{6,7},{7,0},{8,15},{9,8},{10,9... | collective-permute-start | bytes 1572872 | tf_op jit(solution)/shard_map/ppermute | solution.py:25
  64.7 5.9 %collective-permute-start.17 = (bf16[512,256]{1,0:T(8,128)(2,1)S(1)}, bf16[512,256]{1,0:T(8,128)(2,1)S(1)}, u32[]{:S(2)}, u32[]{:S(2)}) collective-permute-start(bf16[512,256]{1,0:T(8,128)(2,1)S(1)} %slice.71), channel_id=1, source_target_pairs={{0,48},{1,49},{2,50},{3,51},{4,52},{5,53},{6,54},{7,55},{8,200},{9... | collective-permute-start | bytes 786440 | tf_op jit(solution)/shard_map/ppermute | solution.py:25
  67.2 6.6 %collective-permute-start.16 = (bf16[512,256]{1,0:T(8,128)(2,1)S(1)}, bf16[512,256]{1,0:T(8,128)(2,1)S(1)}, u32[]{:S(2)}, u32[]{:S(2)}) collective-permute-start(bf16[512,256]{1,0:T(8,128)(2,1)S(1)} %slice.70), channel_id=1, source_target_pairs={{0,16},{1,17},{2,18},{3,19},{4,20},{5,21},{6,22},{7,23},{8,72},{9,... | collective-permute-start | bytes 786440 | tf_op jit(solution)/shard_map/ppermute | solution.py:25
  73.9 12.4 %collective-permute-start.20 = (bf16[1024,256]{1,0:T(8,128)(2,1)S(1)}, bf16[1024,256]{1,0:T(8,128)(2,1)S(1)}, u32[]{:S(2)}, u32[]{:S(2)}) collective-permute-start(bf16[1024,256]{1,0:T(8,128)(2,1)S(1)} %pad_maximum_fusion.3), channel_id=1, source_target_pairs={{0,8},{1,9},{2,10},{3,11},{4,12},{5,13},{6,14},{7,15},{8,0},{9,1},... | collective-permute-start | bytes 1572872 | tf_op jit(solution)/shard_map/ppermute | solution.py:25
  81.4 1.3 %collective-permute-start.21 = (bf16[2,128,128]{2,1,0:T(8,128)(2,1)S(1)}, bf16[2,128,128]{2,1,0:T(8,128)(2,1)S(1)}, u32[]{:S(2)}, u32[]{:S(2)}) collective-permute-start(bf16[2,128,128]{2,1,0:T(8,128)(2,1)S(1)} %get-tuple-element.75), channel_id=1, source_target_pairs={{0,8},{1,9},{2,10},{3,11},{4,12},{5,13},{6,14},{7,15},{8,0},{9,1},... | collective-permute-start | bytes 196616 | tf_op jit(solution)/shard_map/ppermute | solution.py:25
  83.3 7.3 %collective-permute-start.24 = (bf16[2,128,128]{2,1,0:T(8,128)(2,1)S(1)}, bf16[2,128,128]{2,1,0:T(8,128)(2,1)S(1)}, u32[]{:S(2)}, u32[]{:S(2)}) collective-permute-start(bf16[2,128,128]{2,1,0:T(8,128)(2,1)S(1)} %chip.1.sent), channel_id=1, source_target_pairs={{0,32},{1,33},{2,34},{3,35},{4,36},{5,37},{6,38},{7,39},{8,40},{9,... | collective-permute-start | bytes 196616 | tf_op jit(solution)/shard_map/ppermute | solution.py:25
  84.6 6.0 %collective-permute-start.23 = (bf16[2,128,128]{2,1,0:T(8,128)(2,1)S(1)}, bf16[2,128,128]{2,1,0:T(8,128)(2,1)S(1)}, u32[]{:S(2)}, u32[]{:S(2)}) collective-permute-start(bf16[2,128,128]{2,1,0:T(8,128)(2,1)S(1)} %chip.1.sent), channel_id=1, source_target_pairs={{0,48},{1,49},{2,50},{3,51},{4,52},{5,53},{6,54},{7,55},{8,56},{9,... | collective-permute-start | bytes 196616 | tf_op jit(solution)/shard_map/ppermute | solution.py:25
  86.2 4.3 %collective-permute-start.22 = (bf16[2,128,128]{2,1,0:T(8,128)(2,1)S(1)}, bf16[2,128,128]{2,1,0:T(8,128)(2,1)S(1)}, u32[]{:S(2)}, u32[]{:S(2)}) collective-permute-start(bf16[2,128,128]{2,1,0:T(8,128)(2,1)S(1)} %chip.1.sent), channel_id=1, source_target_pairs={{0,16},{1,17},{2,18},{3,19},{4,20},{5,21},{6,22},{7,23},{8,24},{9,... | collective-permute-start | bytes 196616 | tf_op jit(solution)/shard_map/ppermute | solution.py:25
  86.2 9.1 %copy-start.1 = (f32[4,128,128]{2,1,0:T(8,128)S(1)}, f32[4,128,128]{2,1,0:T(8,128)}, u32[]{:S(2)}) copy-start(f32[4,128,128]{2,1,0:T(8,128)} %carried_ref.3) | copy-start | bytes 786436
  91.2 6.7 %collective-permute-start.27 = (bf16[2,128,128]{2,1,0:T(8,128)(2,1)S(1)}, bf16[2,128,128]{2,1,0:T(8,128)(2,1)S(1)}, u32[]{:S(2)}, u32[]{:S(2)}) collective-permute-start(bf16[2,128,128]{2,1,0:T(8,128)(2,1)S(1)} %get-tuple-element.77.sent), channel_id=1, source_target_pairs={{0,128},{1,129},{2,130},{3,131},{4,132},{5,133},{6,134},{7,135},{8... | collective-permute-start | bytes 196616 | tf_op jit(solution)/shard_map/ppermute | solution.py:25
  93.9 4.1 %collective-permute-start.26 = (bf16[2,128,128]{2,1,0:T(8,128)(2,1)S(1)}, bf16[2,128,128]{2,1,0:T(8,128)(2,1)S(1)}, u32[]{:S(2)}, u32[]{:S(2)}) collective-permute-start(bf16[2,128,128]{2,1,0:T(8,128)(2,1)S(1)} %get-tuple-element.77.sent), channel_id=1, source_target_pairs={{0,192},{1,193},{2,194},{3,195},{4,196},{5,197},{6,198},{7,199},{8... | collective-permute-start | bytes 196616 | tf_op jit(solution)/shard_map/ppermute | solution.py:25
  94.8 4.3 %collective-permute-start.25 = (bf16[2,128,128]{2,1,0:T(8,128)(2,1)S(1)}, bf16[2,128,128]{2,1,0:T(8,128)(2,1)S(1)}, u32[]{:S(2)}, u32[]{:S(2)}) collective-permute-start(bf16[2,128,128]{2,1,0:T(8,128)(2,1)S(1)} %get-tuple-element.77.sent), channel_id=1, source_target_pairs={{0,64},{1,65},{2,66},{3,67},{4,68},{5,69},{6,70},{7,71},{8,72},{9,... | collective-permute-start | bytes 196616 | tf_op jit(solution)/shard_map/ppermute | solution.py:25
  95.3 9.3 %copy-start.2 = (f32[512]{0:T(512)S(1)}, f32[512]{0:T(512)}, u32[]{:S(2)}) copy-start(f32[512]{0:T(512)} %param.12) | copy-start | bytes 6148
  99.8 4.8 %collective-permute-start.28 = (f32[2,2,128,128]{3,2,1,0:T(8,128)S(1)}, f32[2,2,128,128]{3,2,1,0:T(8,128)S(1)}, u32[]{:S(2)}, u32[]{:S(2)}) collective-permute-start(f32[2,2,128,128]{3,2,1,0:T(8,128)S(1)} %get-tuple-element.81), channel_id=1, source_target_pairs={{0,8},{1,9},{2,10},{3,11},{4,12},{5,13},{6,14},{7,15},{8,0},{9,1},... | collective-permute-start | bytes 786440 | tf_op jit(solution)/shard_map/ppermute | solution.py:25

commit v4 on v3

--- a/solution.py
+++ b/solution.py
@@ -266,9 +266,7 @@
     xa, xb, squares = kernel(x_kernel, "x", orders + [((512, 128), F32)], 5, 1 << 31)(
         pos, tokens, z1, z2, z3, got_a
     )
-    a4, qfar_a, qfar_b, got_b, got_q, xa, xb, squares = lax.optimization_barrier(
-        (a4, qfar_a, qfar_b, got_b, got_q, xa, xb, squares)
-    )
+    a4, got_b, xa, xb, squares = lax.optimization_barrier((a4, got_b, xa, xb, squares))
     q_parts = (qst, qright, qleft, qfar_a, qfar_b)
 
     flops = 2 * 512 * 4096 * 1024
@@ -286,7 +284,7 @@
         flops,
         aliases={1: 4, 2: 5},
     )(pos, xa, xb, squares, a4, st, right, left, far_a, far_b, got_a, got_b)
-    q_other = (got_q, swap(cat([qfar_a, qfar_b])))
+    q_other = (got_q, swap(cat([after(qfar_a, part), after(qfar_b, part)])))
     (query,) = kernel(q_kernel, "q", [((512, 512), BF)], 10, flops // 2)(
         pos, xa, xb, *q_parts, *q_other, r
     )

time: 107 us -> 106 us (level)
  waiting for transfers between devices: 46.5 us -> 38.1 us
  starting transfers between devices: 37.3 us -> 44.7 us
    ppermute x29, waiting for transfers between devices: 46.5 us -> 38.1 us  [move(): return lax.ppermute(a, BOTH, pairs)]
    ppermute x29, starting transfers between devices: 37.3 us -> 44.7 us  [move(): return lax.ppermute(a, BOTH, pairs)]
  transfers between devices with their start and end apart: 29 -> 29, of which waited for: 16 -> 13; matrix products, arithmetic and copies ran while one was open for 3% -> 3% of each run, Pallas kernels for 14% -> 14%
where the time goes in v4:
time: 106 us
  starting transfers between devices  44.7 us (42%)
  waiting for transfers between devices  38.1 us (36%)
  Pallas kernels  17.9 us (17%)
  other arithmetic  2.38 us (2%)
  local copies, waits for them, and re-layouts  1.52 us (1%)
    ppermute x29, starting transfers between devices, move(): return lax.ppermute(a, BOTH, pairs)  44.7 us
    ppermute x29, waiting for transfers between devices, move(): return lax.ppermute(a, BOTH, pairs)  38.1 us
    pallas_call x1, Pallas kernels, shards(): kernel(kv_kernel, 'kv', [((2, 512, 512), BF), ((512, 128), F32), ((2, 128...  7.02 us
    pallas_call x1, Pallas kernels, shards(): kernel(q_kernel, 'q', [((512, 512), BF)], 10, flops // 2)  2.91 us
    pallas_call x1, Pallas kernels, shards(): kernel(block_kernel, 'block', [((512, 512), F32)], 3, flops // 2)  2.56 us
  transfers between devices with their start and end apart: 29, of which 13 were waited for; matrix products, arithmetic and copies ran while one was open for 3% of the time, Pallas kernels for 14%

profile of v4, /device:TPU:1, one launch (start us, length us, event | category | flops | bytes accessed | tf_op | source)
XLA Modules:
  0.0 105.7 jit_solution(8454035035576546381)
XLA Ops:
  0.6 0.0 copy-start
  0.7 0.1 pad_add_fusion.pos
  0.7 3.3 %collective-permute-start = (bf16[512,512]{1,0:T(8,128)(2,1)}, bf16[512,512]{1,0:T(8,128)(2,1)S(1)}, u32[]{:S(2)}, u32[]{:S(2)}) collective-permute-start(bf16[512,512]{1,0:T(8,128)(2,1)} %own), channel_id=1, source_target_pairs={{0,8},{1,9},{2,10},{3,11},{4,12},{5,13},{6,14},{7,15},{8,0},{9,1},... | collective-permute-start | bytes 1572872 | tf_op jit(solution)/shard_map/ppermute | solution.py:25
  4.0 0.9 broadcast_select_fusion.4
  4.9 1.0 broadcast_select_fusion.2
  5.9 0.2 collective-permute-start.1
  6.1 0.1 pad_maximum_fusion
  6.2 1.2 %collective-permute-done.1 = bf16[128,768]{1,0:T(8,128)(2,1)S(1)} collective-permute-done((bf16[128,768]{1,0:T(8,128)(2,1)S(1)}, bf16[128,768]{1,0:T(8,128)(2,1)S(1)}, u32[]{:S(2)}, u32[]{:S(2)}) %collective-permute-start.1) | collective-permute-done | bytes 196640 | tf_op jit(solution)/shard_map/ppermute | solution.py:25
  7.5 3.8 %collective-permute-start.2 = (bf16[1024,512]{1,0:T(8,128)(2,1)S(1)}, bf16[1024,512]{1,0:T(8,128)(2,1)S(1)}, u32[]{:S(2)}, u32[]{:S(2)}) collective-permute-start(bf16[1024,512]{1,0:T(8,128)(2,1)S(1)} %pad_maximum_fusion), channel_id=1, source_target_pairs={{0,1},{1,2},{2,3},{3,4},{4,5},{5,6},{6,7},{7,0},{8,15},{9,8},{10,9... | collective-permute-start | bytes 3145736 | tf_op jit(solution)/shard_map/ppermute | solution.py:25
  11.3 0.8 dynamic_slice.3
  12.1 0.1 broadcast_select_fusion.1
  12.1 0.1 multiply_convert_fusion
  12.3 1.4 %collective-permute-start.3 = (bf16[256,768]{1,0:T(8,128)(2,1)S(1)}, bf16[256,768]{1,0:T(8,128)(2,1)S(1)}, u32[]{:S(2)}, u32[]{:S(2)}) collective-permute-start(bf16[256,768]{1,0:T(8,128)(2,1)S(1)} %multiply_convert_fusion), channel_id=1, source_target_pairs={{0,64},{1,65},{2,66},{3,67},{4,68},{5,69},{6,70},{7,71},{8,24},{9,... | collective-permute-start | bytes 1179656 | tf_op jit(solution)/shard_map/ppermute | solution.py:25
  13.6 1.5 %collective-permute-start.4 = (bf16[256,768]{1,0:T(8,128)(2,1)S(1)}, bf16[256,768]{1,0:T(8,128)(2,1)S(1)}, u32[]{:S(2)}, u32[]{:S(2)}) collective-permute-start(bf16[256,768]{1,0:T(8,128)(2,1)S(1)} %multiply_convert_fusion), channel_id=1, source_target_pairs={{0,192},{1,193},{2,194},{3,195},{4,196},{5,197},{6,198},{7,199},{8... | collective-permute-start | bytes 1179656 | tf_op jit(solution)/shard_map/ppermute | solution.py:25
  15.2 1.6 %collective-permute-start.5 = (bf16[256,768]{1,0:T(8,128)(2,1)S(1)}, bf16[256,768]{1,0:T(8,128)(2,1)S(1)}, u32[]{:S(2)}, u32[]{:S(2)}) collective-permute-start(bf16[256,768]{1,0:T(8,128)(2,1)S(1)} %multiply_convert_fusion), channel_id=1, source_target_pairs={{0,128},{1,129},{2,130},{3,131},{4,132},{5,133},{6,134},{7,135},{8... | collective-permute-start | bytes 1179656 | tf_op jit(solution)/shard_map/ppermute | solution.py:25
  16.8 3.8 %collective-permute-done.3 = bf16[256,768]{1,0:T(8,128)(2,1)S(1)} collective-permute-done((bf16[256,768]{1,0:T(8,128)(2,1)S(1)}, bf16[256,768]{1,0:T(8,128)(2,1)S(1)}, u32[]{:S(2)}, u32[]{:S(2)}) %collective-permute-start.3) | collective-permute-done | bytes 393248 | tf_op jit(solution)/shard_map/ppermute | solution.py:25
  20.5 3.6 %collective-permute-done.4 = bf16[256,768]{1,0:T(8,128)(2,1)S(1)} collective-permute-done((bf16[256,768]{1,0:T(8,128)(2,1)S(1)}, bf16[256,768]{1,0:T(8,128)(2,1)S(1)}, u32[]{:S(2)}, u32[]{:S(2)}) %collective-permute-start.4) | collective-permute-done | bytes 393248 | tf_op jit(solution)/shard_map/ppermute | solution.py:25
  24.1 1.5 %collective-permute-done.5 = bf16[256,768]{1,0:T(8,128)(2,1)S(1)} collective-permute-done((bf16[256,768]{1,0:T(8,128)(2,1)S(1)}, bf16[256,768]{1,0:T(8,128)(2,1)S(1)}, u32[]{:S(2)}, u32[]{:S(2)}) %collective-permute-start.5) | collective-permute-done | bytes 393248 | tf_op jit(solution)/shard_map/ppermute | solution.py:25
  25.6 0.0 collective-permute-done.2.z1
  25.8 0.1 collective-permute-start.9
  25.9 0.1 pad_maximum_fusion.1.st
  26.0 1.3 %collective-permute-start.7 = (bf16[1024,512]{1,0:T(8,128)(2,1)S(1)}, bf16[1024,512]{1,0:T(8,128)(2,1)S(1)}, u32[]{:S(2)}, u32[]{:S(2)}) collective-permute-start(bf16[1024,512]{1,0:T(8,128)(2,1)S(1)} %pad_maximum_fusion.1.st), channel_id=1, source_target_pairs={{0,16},{1,17},{2,18},{3,19},{4,20},{5,21},{6,22},{7,23},{8,72},{9,... | collective-permute-start | bytes 3145736 | tf_op jit(solution)/shard_map/ppermute | solution.py:25
  27.3 1.5 %collective-permute-start.8 = (bf16[1024,512]{1,0:T(8,128)(2,1)S(1)}, bf16[1024,512]{1,0:T(8,128)(2,1)S(1)}, u32[]{:S(2)}, u32[]{:S(2)}) collective-permute-start(bf16[1024,512]{1,0:T(8,128)(2,1)S(1)} %pad_maximum_fusion.1.st), channel_id=1, source_target_pairs={{0,48},{1,49},{2,50},{3,51},{4,52},{5,53},{6,54},{7,55},{8,200},{9... | collective-permute-start | bytes 3145736 | tf_op jit(solution)/shard_map/ppermute | solution.py:25
  28.8 1.0 collective-permute-start.6
  29.8 11.4 %collective-permute-done.7.right = bf16[1024,512]{1,0:T(8,128)(2,1)S(1)} collective-permute-done((bf16[1024,512]{1,0:T(8,128)(2,1)S(1)}, bf16[1024,512]{1,0:T(8,128)(2,1)S(1)}, u32[]{:S(2)}, u32[]{:S(2)}) %collective-permute-start.7) | collective-permute-done | bytes 1048608 | tf_op jit(solution)/shard_map/ppermute | solution.py:25
  41.2 0.0 collective-permute-done.8.left
  41.2 1.5 %collective-permute-done.6.z2 = bf16[1024,512]{1,0:T(8,128)(2,1)S(1)} collective-permute-done((bf16[1024,512]{1,0:T(8,128)(2,1)S(1)}, bf16[1024,512]{1,0:T(8,128)(2,1)S(1)}, u32[]{:S(2)}, u32[]{:S(2)}) %collective-permute-start.6) | collective-permute-done | bytes 1048608 | tf_op jit(solution)/shard_map/ppermute | solution.py:25
  42.7 1.9 %collective-permute-start.10 = (bf16[1024,512]{1,0:T(8,128)(2,1)S(1)}, bf16[1024,512]{1,0:T(8,128)(2,1)S(1)}, u32[]{:S(2)}, u32[]{:S(2)}) collective-permute-start(bf16[1024,512]{1,0:T(8,128)(2,1)S(1)} %collective-permute-done.6.z2), channel_id=1, source_target_pairs={{0,1},{1,2},{2,3},{3,4},{4,5},{5,6},{6,7},{7,0},{8,15},{9,8},{10,9... | collective-permute-start | bytes 3145736 | tf_op jit(solution)/shard_map/ppermute | solution.py:25
  44.7 0.1 collective-permute-start.13
  44.8 2.7 %collective-permute-start.14 = (bf16[1024,256]{1,0:T(8,128)(2,1)S(1)}, bf16[1024,256]{1,0:T(8,128)(2,1)S(1)}, u32[]{:S(2)}, u32[]{:S(2)}) collective-permute-start(bf16[1024,256]{1,0:T(8,128)(2,1)S(1)} %pad_maximum_fusion.2.refs_0_), channel_id=1, source_target_pairs={{0,48},{1,49},{2,50},{3,51},{4,52},{5,53},{6,54},{7,55},{8,200},{9... | collective-permute-start | bytes 1572872 | tf_op jit(solution)/shard_map/ppermute | solution.py:25
  47.5 0.1 collective-permute-start.11
  47.7 2.7 %collective-permute-start.12 = (bf16[512,512]{1,0:T(8,128)(2,1)S(1)}, bf16[512,512]{1,0:T(8,128)(2,1)S(1)}, u32[]{:S(2)}, u32[]{:S(2)}) collective-permute-start(bf16[512,512]{1,0:T(8,128)(2,1)S(1)} %slice.64), channel_id=1, source_target_pairs={{0,48},{1,49},{2,50},{3,51},{4,52},{5,53},{6,54},{7,55},{8,200},{9... | collective-permute-start | bytes 1572872 | tf_op jit(solution)/shard_map/ppermute | solution.py:25
  50.4 0.1 constant_dynamic-update-slice_fusion.7
  50.5 0.1 constant_dynamic-update-slice_fusion.6
  50.5 3.8 %collective-permute-done.13.refs_1_ = bf16[1024,256]{1,0:T(8,128)(2,1)S(1)} collective-permute-done((bf16[1024,256]{1,0:T(8,128)(2,1)S(1)}, bf16[1024,256]{1,0:T(8,128)(2,1)S(1)}, u32[]{:S(2)}, u32[]{:S(2)}) %collective-permute-start.13) | collective-permute-done | bytes 524320 | tf_op jit(solution)/shard_map/ppermute | solution.py:25
  54.3 5.6 %collective-permute-done.11.far_a = bf16[512,512]{1,0:T(8,128)(2,1)S(1)} collective-permute-done((bf16[512,512]{1,0:T(8,128)(2,1)S(1)}, bf16[512,512]{1,0:T(8,128)(2,1)S(1)}, u32[]{:S(2)}, u32[]{:S(2)}) %collective-permute-start.11) | collective-permute-done | bytes 524320 | tf_op jit(solution)/shard_map/ppermute | solution.py:25
  60.1 0.1 slice_dynamic-update-slice_fusion
  60.2 2.3 %collective-permute-start.16 = (bf16[4096,512]{1,0:T(8,128)(2,1)S(1)}, bf16[4096,512]{1,0:T(8,128)(2,1)S(1)}, u32[]{:S(2)}, u32[]{:S(2)}) collective-permute-start(bf16[4096,512]{1,0:T(8,128)(2,1)S(1)} %get-tuple-element.80), channel_id=1, source_target_pairs={{0,8},{1,9},{2,10},{3,11},{4,12},{5,13},{6,14},{7,15},{8,0},{9,1},... | collective-permute-start | bytes 12582920 | tf_op jit(solution)/shard_map/ppermute | solution.py:25
  62.5 3.0 %collective-permute-start.15 = (bf16[512,512]{1,0:T(8,128)(2,1)S(1)}, bf16[512,512]{1,0:T(8,128)(2,1)S(1)}, u32[]{:S(2)}, u32[]{:S(2)}) collective-permute-start(bf16[512,512]{1,0:T(8,128)(2,1)S(1)} %get-tuple-element.81), channel_id=1, source_target_pairs={{0,1},{1,2},{2,3},{3,4},{4,5},{5,6},{6,7},{7,0},{8,15},{9,8},{10,9... | collective-permute-start | bytes 1572872 | tf_op jit(solution)/shard_map/ppermute | solution.py:25
  65.5 0.1 collective-permute-start.19
  65.7 1.3 %collective-permute-start.17 = (bf16[512,256]{1,0:T(8,128)(2,1)S(1)}, bf16[512,256]{1,0:T(8,128)(2,1)S(1)}, u32[]{:S(2)}, u32[]{:S(2)}) collective-permute-start(bf16[512,256]{1,0:T(8,128)(2,1)S(1)} %slice.72), channel_id=1, source_target_pairs={{0,16},{1,17},{2,18},{3,19},{4,20},{5,21},{6,22},{7,23},{8,72},{9,... | collective-permute-start | bytes 786440 | tf_op jit(solution)/shard_map/ppermute | solution.py:25
  67.0 1.5 %collective-permute-start.18 = (bf16[512,256]{1,0:T(8,128)(2,1)S(1)}, bf16[512,256]{1,0:T(8,128)(2,1)S(1)}, u32[]{:S(2)}, u32[]{:S(2)}) collective-permute-start(bf16[512,256]{1,0:T(8,128)(2,1)S(1)} %slice.73), channel_id=1, source_target_pairs={{0,48},{1,49},{2,50},{3,51},{4,52},{5,53},{6,54},{7,55},{8,200},{9... | collective-permute-start | bytes 786440 | tf_op jit(solution)/shard_map/ppermute | solution.py:25
  68.4 1.6 %x.1 = (bf16[512,4096]{1,0:T(8,128)(2,1)S(1)}, bf16[512,4096]{1,0:T(8,128)(2,1)S(1)}, f32[512,128]{1,0:T(8,128)S(1)}) custom-call(s32[4]{0:T(128)S(1)} %pad_add_fusion.pos, bf16[512,512]{1,0:T(8,128)(2,1)S(1)} %copy-done, bf16[1024,512]{1,0:T(8,128)(2,1)S(1)} %collective-permute-done.2.z1, bf16[1024,512]{1,0:T(8,128)(2,1)S(1)} %collective-permute-done.6.z2, ...), custom_call_target="tpu_custom_call" | custom-call | flops 2147483648 | bytes 1048576 | tf_op jit(solution)/shard_map/x/pallas_call | solution.py:266
  70.1 1.5 %collective-permute-done.15.a4 = bf16[512,512]{1,0:T(8,128)(2,1)S(1)} collective-permute-done((bf16[512,512]{1,0:T(8,128)(2,1)S(1)}, bf16[512,512]{1,0:T(8,128)(2,1)S(1)}, u32[]{:S(2)}, u32[]{:S(2)}) %collective-permute-start.15) | collective-permute-done | bytes 524320 | tf_op jit(solution)/shard_map/ppermute | solution.py:25
  71.6 7.0 %kv.1 = (bf16[2,512,512]{2,1,0:T(8,128)(2,1)S(1)}, f32[512,128]{1,0:T(8,128)S(1)}, f32[2,128,128]{2,1,0:T(8,128)S(1)}, bf16[2,128,128]{2,1,0:T(8,128)(2,1)S(1)},...) custom-call(s32[4]{0:T(128)S(1)} %pad_add_fusion.pos, ...), custom_call_target="tpu_custom_call", output_to_operand_aliasing={{4}: (1, {}), {5}: (2, {})} | custom-call | flops 4294967296 | bytes 1048576 | tf_op jit(solution)/shard_map/kv/pallas_call | solution.py:273
  78.7 1.5 %collective-permute-start.20 = (bf16[1024,256]{1,0:T(8,128)(2,1)S(1)}, bf16[1024,256]{1,0:T(8,128)(2,1)S(1)}, u32[]{:S(2)}, u32[]{:S(2)}) collective-permute-start(bf16[1024,256]{1,0:T(8,128)(2,1)S(1)} %pad_maximum_fusion.3), channel_id=1, source_target_pairs={{0,8},{1,9},{2,10},{3,11},{4,12},{5,13},{6,14},{7,15},{8,0},{9,1},... | collective-permute-start | bytes 1572872 | tf_op jit(solution)/shard_map/ppermute | solution.py:25
  80.2 0.1 collective-permute-start.21
  80.3 1.5 %collective-permute-done.21.sib_ref = bf16[2,128,128]{2,1,0:T(8,128)(2,1)S(1)} collective-permute-done((bf16[2,128,128]{2,1,0:T(8,128)(2,1)S(1)}, bf16[2,128,128]{2,1,0:T(8,128)(2,1)S(1)}, u32[]{:S(2)}, u32[]{:S(2)}) %collective-permute-start.21) | collective-permute-done | bytes 65568 | tf_op jit(solution)/shard_map/ppermute | solution.py:25
  81.8 0.6 chip.1.sent
  82.4 0.1 collective-permute-start.22
  82.4 3.0 %collective-permute-start.23 = (bf16[2,128,128]{2,1,0:T(8,128)(2,1)S(1)}, bf16[2,128,128]{2,1,0:T(8,128)(2,1)S(1)}, u32[]{:S(2)}, u32[]{:S(2)}) collective-permute-start(bf16[2,128,128]{2,1,0:T(8,128)(2,1)S(1)} %chip.1.sent), channel_id=1, source_target_pairs={{0,48},{1,49},{2,50},{3,51},{4,52},{5,53},{6,54},{7,55},{8,56},{9,... | collective-permute-start | bytes 196616 | tf_op jit(solution)/shard_map/ppermute | solution.py:25
  85.5 1.1 %collective-permute-start.24 = (bf16[2,128,128]{2,1,0:T(8,128)(2,1)S(1)}, bf16[2,128,128]{2,1,0:T(8,128)(2,1)S(1)}, u32[]{:S(2)}, u32[]{:S(2)}) collective-permute-start(bf16[2,128,128]{2,1,0:T(8,128)(2,1)S(1)} %chip.1.sent), channel_id=1, source_target_pairs={{0,32},{1,33},{2,34},{3,35},{4,36},{5,37},{6,38},{7,39},{8,40},{9,... | collective-permute-start | bytes 196616 | tf_op jit(solution)/shard_map/ppermute | solution.py:25
  86.6 2.9 %q.1.q_ref = bf16[512,512]{1,0:T(8,128)(2,1)S(1)} custom-call(s32[4]{0:T(128)S(1)} %pad_add_fusion.pos, bf16[512,4096]{1,0:T(8,128)(2,1)S(1)} %get-tuple-element.64.xa_ref, bf16[512,4096]{1,0:T(8,128)(2,1)S(1)} %get-tuple-element.65.xb_ref, bf16[1024,256]{1,0:T(8,128)(2,1)S(1)} %pad_maximum_fusion.2.refs_0_, ...), custom_call_target="tpu_custom_call" | custom-call | flops 2147483648 | bytes 1048576 | tf_op jit(solution)/shard_map/q/pallas_call | solution.py:288
  89.5 0.6 collective-permute-done.24.opposite
  90.1 0.6 row.1
  90.7 1.5 %collective-permute-start.25 = (bf16[2,128,128]{2,1,0:T(8,128)(2,1)S(1)}, bf16[2,128,128]{2,1,0:T(8,128)(2,1)S(1)}, u32[]{:S(2)}, u32[]{:S(2)}) collective-permute-start(bf16[2,128,128]{2,1,0:T(8,128)(2,1)S(1)} %get-tuple-element.75.sent), channel_id=1, source_target_pairs={{0,64},{1,65},{2,66},{3,67},{4,68},{5,69},{6,70},{7,71},{8,72},{9,... | collective-permute-start | bytes 196616 | tf_op jit(solution)/shard_map/ppermute | solution.py:25
  92.2 1.5 %collective-permute-start.26 = (bf16[2,128,128]{2,1,0:T(8,128)(2,1)S(1)}, bf16[2,128,128]{2,1,0:T(8,128)(2,1)S(1)}, u32[]{:S(2)}, u32[]{:S(2)}) collective-permute-start(bf16[2,128,128]{2,1,0:T(8,128)(2,1)S(1)} %get-tuple-element.75.sent), channel_id=1, source_target_pairs={{0,192},{1,193},{2,194},{3,195},{4,196},{5,197},{6,198},{7,199},{8... | collective-permute-start | bytes 196616 | tf_op jit(solution)/shard_map/ppermute | solution.py:25
  93.7 1.5 %collective-permute-start.27 = (bf16[2,128,128]{2,1,0:T(8,128)(2,1)S(1)}, bf16[2,128,128]{2,1,0:T(8,128)(2,1)S(1)}, u32[]{:S(2)}, u32[]{:S(2)}) collective-permute-start(bf16[2,128,128]{2,1,0:T(8,128)(2,1)S(1)} %get-tuple-element.75.sent), channel_id=1, source_target_pairs={{0,128},{1,129},{2,130},{3,131},{4,132},{5,133},{6,134},{7,135},{8... | collective-permute-start | bytes 196616 | tf_op jit(solution)/shard_map/ppermute | solution.py:25
  95.2 2.6 %block.1.raw_ref = f32[512,512]{1,0:T(8,128)S(1)} custom-call(s32[4]{0:T(128)S(1)} %pad_add_fusion.pos, bf16[512,512]{1,0:T(8,128)(2,1)S(1)} %q.1.q_ref, bf16[2,512,512]{2,1,0:T(8,128)(2,1)S(1)} %get-tuple-element.72.kv_ref, f32[4,128,128]{2,1,0:T(8,128)S(1)} %copy-done.1), custom_call_target="tpu_custom_call" | custom-call | flops 2147483648 | bytes 1048576 | tf_op jit(solution)/shard_map/block/pallas_call | solution.py:291
  97.8 0.9 collective-permute-done.27.opposite
  98.7 0.6 plane.1
  99.4 3.2 %collective-permute-start.28 = (f32[2,2,128,128]{3,2,1,0:T(8,128)S(1)}, f32[2,2,128,128]{3,2,1,0:T(8,128)S(1)}, u32[]{:S(2)}, u32[]{:S(2)}) collective-permute-start(f32[2,2,128,128]{3,2,1,0:T(8,128)S(1)} %get-tuple-element.79), channel_id=1, source_target_pairs={{0,8},{1,9},{2,10},{3,11},{4,12},{5,13},{6,14},{7,15},{8,0},{9,1},... | collective-permute-start | bytes 786440 | tf_op jit(solution)/shard_map/ppermute | solution.py:25
  102.5 1.2 %collective-permute-done.28.both_ref = f32[2,2,128,128]{3,2,1,0:T(8,128)S(1)} collective-permute-done((f32[2,2,128,128]{3,2,1,0:T(8,128)S(1)}, f32[2,2,128,128]{3,2,1,0:T(8,128)S(1)}, u32[]{:S(2)}, u32[]{:S(2)}) %collective-permute-start.28) | collective-permute-done | bytes 262176 | tf_op jit(solution)/shard_map/ppermute | solution.py:25
  103.7 2.0 %out.1 = (bf16[512,512]{1,0:T(8,128)(2,1)}, f32[4,128,128]{2,1,0:T(8,128)}) custom-call(s32[4]{0:T(128)S(1)} %pad_add_fusion.pos, bf16[512,512]{1,0:T(8,128)(2,1)S(1)} %q.1.q_ref, f32[512,512]{1,0:T(8,128)S(1)} %block.1.raw_ref, f32[2,2,128,128]{3,2,1,0:T(8,128)S(1)} %get-tuple-element.78.mine_ref, f32[2,2,128,128]{3,2,1,0:T(8,128)S(1)} %collective-permute-done.28.both_ref, ...), custom_call_target="tpu_custom_call" | custom-call | flops 268435456 | bytes 1048576 | tf_op jit(solution)/shard_map/out/pallas_call | solution.py:311
  (40 shorter events, 0.7 us)
Async XLA Ops:
  0.6 5.5 %copy-start = (bf16[512,512]{1,0:T(8,128)(2,1)S(1)}, bf16[512,512]{1,0:T(8,128)(2,1)}, u32[]{:S(2)}) copy-start(bf16[512,512]{1,0:T(8,128)(2,1)} %own) | copy-start | bytes 1572868
  0.7 5.2 %collective-permute-start = (bf16[512,512]{1,0:T(8,128)(2,1)}, bf16[512,512]{1,0:T(8,128)(2,1)S(1)}, u32[]{:S(2)}, u32[]{:S(2)}) collective-permute-start(bf16[512,512]{1,0:T(8,128)(2,1)} %own), channel_id=1, source_target_pairs={{0,8},{1,9},{2,10},{3,11},{4,12},{5,13},{6,14},{7,15},{8,0},{9,1},... | collective-permute-start | bytes 1572872 | tf_op jit(solution)/shard_map/ppermute | solution.py:25
  5.9 1.5 %collective-permute-start.1 = (bf16[128,768]{1,0:T(8,128)(2,1)S(1)}, bf16[128,768]{1,0:T(8,128)(2,1)S(1)}, u32[]{:S(2)}, u32[]{:S(2)}) collective-permute-start(bf16[128,768]{1,0:T(8,128)(2,1)S(1)} %pad_maximum_fusion.4), channel_id=1, source_target_pairs={{0,8},{1,9},{2,10},{3,11},{4,12},{5,13},{6,14},{7,15},{8,0},{9,1},... | collective-permute-start | bytes 589832 | tf_op jit(solution)/shard_map/ppermute | solution.py:25
  7.5 18.2 %collective-permute-start.2 = (bf16[1024,512]{1,0:T(8,128)(2,1)S(1)}, bf16[1024,512]{1,0:T(8,128)(2,1)S(1)}, u32[]{:S(2)}, u32[]{:S(2)}) collective-permute-start(bf16[1024,512]{1,0:T(8,128)(2,1)S(1)} %pad_maximum_fusion), channel_id=1, source_target_pairs={{0,1},{1,2},{2,3},{3,4},{4,5},{5,6},{6,7},{7,0},{8,15},{9,8},{10,9... | collective-permute-start | bytes 3145736 | tf_op jit(solution)/shard_map/ppermute | solution.py:25
  12.3 8.3 %collective-permute-start.3 = (bf16[256,768]{1,0:T(8,128)(2,1)S(1)}, bf16[256,768]{1,0:T(8,128)(2,1)S(1)}, u32[]{:S(2)}, u32[]{:S(2)}) collective-permute-start(bf16[256,768]{1,0:T(8,128)(2,1)S(1)} %multiply_convert_fusion), channel_id=1, source_target_pairs={{0,64},{1,65},{2,66},{3,67},{4,68},{5,69},{6,70},{7,71},{8,24},{9,... | collective-permute-start | bytes 1179656 | tf_op jit(solution)/shard_map/ppermute | solution.py:25
  13.6 10.5 %collective-permute-start.4 = (bf16[256,768]{1,0:T(8,128)(2,1)S(1)}, bf16[256,768]{1,0:T(8,128)(2,1)S(1)}, u32[]{:S(2)}, u32[]{:S(2)}) collective-permute-start(bf16[256,768]{1,0:T(8,128)(2,1)S(1)} %multiply_convert_fusion), channel_id=1, source_target_pairs={{0,192},{1,193},{2,194},{3,195},{4,196},{5,197},{6,198},{7,199},{8... | collective-permute-start | bytes 1179656 | tf_op jit(solution)/shard_map/ppermute | solution.py:25
  15.2 10.5 %collective-permute-start.5 = (bf16[256,768]{1,0:T(8,128)(2,1)S(1)}, bf16[256,768]{1,0:T(8,128)(2,1)S(1)}, u32[]{:S(2)}, u32[]{:S(2)}) collective-permute-start(bf16[256,768]{1,0:T(8,128)(2,1)S(1)} %multiply_convert_fusion), channel_id=1, source_target_pairs={{0,128},{1,129},{2,130},{3,131},{4,132},{5,133},{6,134},{7,135},{8... | collective-permute-start | bytes 1179656 | tf_op jit(solution)/shard_map/ppermute | solution.py:25
  25.8 16.9 %collective-permute-start.9 = (bf16[1536,512]{1,0:T(8,128)(2,1)S(1)}, bf16[1536,512]{1,0:T(8,128)(2,1)S(1)}, u32[]{:S(2)}, u32[]{:S(2)}) collective-permute-start(bf16[1536,512]{1,0:T(8,128)(2,1)S(1)} %slice_dynamic-update-slice_fusion.2), channel_id=1, source_target_pairs={{0,8},{1,9},{2,10},{3,11},{4,12},{5,13},{6,14},{7,15},{8,0},{9,1},... | collective-permute-start | bytes 4718600 | tf_op jit(solution)/shard_map/ppermute | solution.py:25
  26.0 15.2 %collective-permute-start.7 = (bf16[1024,512]{1,0:T(8,128)(2,1)S(1)}, bf16[1024,512]{1,0:T(8,128)(2,1)S(1)}, u32[]{:S(2)}, u32[]{:S(2)}) collective-permute-start(bf16[1024,512]{1,0:T(8,128)(2,1)S(1)} %pad_maximum_fusion.1.st), channel_id=1, source_target_pairs={{0,16},{1,17},{2,18},{3,19},{4,20},{5,21},{6,22},{7,23},{8,72},{9,... | collective-permute-start | bytes 3145736 | tf_op jit(solution)/shard_map/ppermute | solution.py:25
  27.3 13.9 %collective-permute-start.8 = (bf16[1024,512]{1,0:T(8,128)(2,1)S(1)}, bf16[1024,512]{1,0:T(8,128)(2,1)S(1)}, u32[]{:S(2)}, u32[]{:S(2)}) collective-permute-start(bf16[1024,512]{1,0:T(8,128)(2,1)S(1)} %pad_maximum_fusion.1.st), channel_id=1, source_target_pairs={{0,48},{1,49},{2,50},{3,51},{4,52},{5,53},{6,54},{7,55},{8,200},{9... | collective-permute-start | bytes 3145736 | tf_op jit(solution)/shard_map/ppermute | solution.py:25
  28.8 13.9 %collective-permute-start.6 = (bf16[1024,512]{1,0:T(8,128)(2,1)S(1)}, bf16[1024,512]{1,0:T(8,128)(2,1)S(1)}, u32[]{:S(2)}, u32[]{:S(2)}) collective-permute-start(bf16[1024,512]{1,0:T(8,128)(2,1)S(1)} %collective-permute-done.2.z1), channel_id=1, source_target_pairs={{0,1},{1,2},{2,3},{3,4},{4,5},{5,6},{6,7},{7,0},{8,15},{9,8},{10,9... | collective-permute-start | bytes 3145736 | tf_op jit(solution)/shard_map/ppermute | solution.py:25
  42.7 17.3 %collective-permute-start.10 = (bf16[1024,512]{1,0:T(8,128)(2,1)S(1)}, bf16[1024,512]{1,0:T(8,128)(2,1)S(1)}, u32[]{:S(2)}, u32[]{:S(2)}) collective-permute-start(bf16[1024,512]{1,0:T(8,128)(2,1)S(1)} %collective-permute-done.6.z2), channel_id=1, source_target_pairs={{0,1},{1,2},{2,3},{3,4},{4,5},{5,6},{6,7},{7,0},{8,15},{9,8},{10,9... | collective-permute-start | bytes 3145736 | tf_op jit(solution)/shard_map/ppermute | solution.py:25
  44.7 9.6 %collective-permute-start.13 = (bf16[1024,256]{1,0:T(8,128)(2,1)S(1)}, bf16[1024,256]{1,0:T(8,128)(2,1)S(1)}, u32[]{:S(2)}, u32[]{:S(2)}) collective-permute-start(bf16[1024,256]{1,0:T(8,128)(2,1)S(1)} %pad_maximum_fusion.2.refs_0_), channel_id=1, source_target_pairs={{0,16},{1,17},{2,18},{3,19},{4,20},{5,21},{6,22},{7,23},{8,72},{9,... | collective-permute-start | bytes 1572872 | tf_op jit(solution)/shard_map/ppermute | solution.py:25
  44.8 9.5 %collective-permute-start.14 = (bf16[1024,256]{1,0:T(8,128)(2,1)S(1)}, bf16[1024,256]{1,0:T(8,128)(2,1)S(1)}, u32[]{:S(2)}, u32[]{:S(2)}) collective-permute-start(bf16[1024,256]{1,0:T(8,128)(2,1)S(1)} %pad_maximum_fusion.2.refs_0_), channel_id=1, source_target_pairs={{0,48},{1,49},{2,50},{3,51},{4,52},{5,53},{6,54},{7,55},{8,200},{9... | collective-permute-start | bytes 1572872 | tf_op jit(solution)/shard_map/ppermute | solution.py:25
  47.5 12.4 %collective-permute-start.11 = (bf16[512,512]{1,0:T(8,128)(2,1)S(1)}, bf16[512,512]{1,0:T(8,128)(2,1)S(1)}, u32[]{:S(2)}, u32[]{:S(2)}) collective-permute-start(bf16[512,512]{1,0:T(8,128)(2,1)S(1)} %slice.63), channel_id=1, source_target_pairs={{0,16},{1,17},{2,18},{3,19},{4,20},{5,21},{6,22},{7,23},{8,72},{9,... | collective-permute-start | bytes 1572872 | tf_op jit(solution)/shard_map/ppermute | solution.py:25
  47.7 12.3 %collective-permute-start.12 = (bf16[512,512]{1,0:T(8,128)(2,1)S(1)}, bf16[512,512]{1,0:T(8,128)(2,1)S(1)}, u32[]{:S(2)}, u32[]{:S(2)}) collective-permute-start(bf16[512,512]{1,0:T(8,128)(2,1)S(1)} %slice.64), channel_id=1, source_target_pairs={{0,48},{1,49},{2,50},{3,51},{4,52},{5,53},{6,54},{7,55},{8,200},{9... | collective-permute-start | bytes 1572872 | tf_op jit(solution)/shard_map/ppermute | solution.py:25
  60.2 11.4 %collective-permute-start.16 = (bf16[4096,512]{1,0:T(8,128)(2,1)S(1)}, bf16[4096,512]{1,0:T(8,128)(2,1)S(1)}, u32[]{:S(2)}, u32[]{:S(2)}) collective-permute-start(bf16[4096,512]{1,0:T(8,128)(2,1)S(1)} %get-tuple-element.80), channel_id=1, source_target_pairs={{0,8},{1,9},{2,10},{3,11},{4,12},{5,13},{6,14},{7,15},{8,0},{9,1},... | collective-permute-start | bytes 12582920 | tf_op jit(solution)/shard_map/ppermute | solution.py:25
  62.5 9.1 %collective-permute-start.15 = (bf16[512,512]{1,0:T(8,128)(2,1)S(1)}, bf16[512,512]{1,0:T(8,128)(2,1)S(1)}, u32[]{:S(2)}, u32[]{:S(2)}) collective-permute-start(bf16[512,512]{1,0:T(8,128)(2,1)S(1)} %get-tuple-element.81), channel_id=1, source_target_pairs={{0,1},{1,2},{2,3},{3,4},{4,5},{5,6},{6,7},{7,0},{8,15},{9,8},{10,9... | collective-permute-start | bytes 1572872 | tf_op jit(solution)/shard_map/ppermute | solution.py:25
  65.5 21.1 %collective-permute-start.19 = (bf16[3072,256]{1,0:T(8,128)(2,1)S(1)}, bf16[3072,256]{1,0:T(8,128)(2,1)S(1)}, u32[]{:S(2)}, u32[]{:S(2)}) collective-permute-start(bf16[3072,256]{1,0:T(8,128)(2,1)S(1)} %constant_dynamic-update-slice_fusion.8), channel_id=1, source_target_pairs={{0,8},{1,9},{2,10},{3,11},{4,12},{5,13},{6,14},{7,15},{8,0},{9,1},... | collective-permute-start | bytes 4718600 | tf_op jit(solution)/shard_map/ppermute | solution.py:25
  65.7 12.9 %collective-permute-start.17 = (bf16[512,256]{1,0:T(8,128)(2,1)S(1)}, bf16[512,256]{1,0:T(8,128)(2,1)S(1)}, u32[]{:S(2)}, u32[]{:S(2)}) collective-permute-start(bf16[512,256]{1,0:T(8,128)(2,1)S(1)} %slice.72), channel_id=1, source_target_pairs={{0,16},{1,17},{2,18},{3,19},{4,20},{5,21},{6,22},{7,23},{8,72},{9,... | collective-permute-start | bytes 786440 | tf_op jit(solution)/shard_map/ppermute | solution.py:25
  67.0 11.6 %collective-permute-start.18 = (bf16[512,256]{1,0:T(8,128)(2,1)S(1)}, bf16[512,256]{1,0:T(8,128)(2,1)S(1)}, u32[]{:S(2)}, u32[]{:S(2)}) collective-permute-start(bf16[512,256]{1,0:T(8,128)(2,1)S(1)} %slice.73), channel_id=1, source_target_pairs={{0,48},{1,49},{2,50},{3,51},{4,52},{5,53},{6,54},{7,55},{8,200},{9... | collective-permute-start | bytes 786440 | tf_op jit(solution)/shard_map/ppermute | solution.py:25
  78.7 7.9 %collective-permute-start.20 = (bf16[1024,256]{1,0:T(8,128)(2,1)S(1)}, bf16[1024,256]{1,0:T(8,128)(2,1)S(1)}, u32[]{:S(2)}, u32[]{:S(2)}) collective-permute-start(bf16[1024,256]{1,0:T(8,128)(2,1)S(1)} %pad_maximum_fusion.3), channel_id=1, source_target_pairs={{0,8},{1,9},{2,10},{3,11},{4,12},{5,13},{6,14},{7,15},{8,0},{9,1},... | collective-permute-start | bytes 1572872 | tf_op jit(solution)/shard_map/ppermute | solution.py:25
  80.2 1.6 %collective-permute-start.21 = (bf16[2,128,128]{2,1,0:T(8,128)(2,1)S(1)}, bf16[2,128,128]{2,1,0:T(8,128)(2,1)S(1)}, u32[]{:S(2)}, u32[]{:S(2)}) collective-permute-start(bf16[2,128,128]{2,1,0:T(8,128)(2,1)S(1)} %get-tuple-element.73), channel_id=1, source_target_pairs={{0,8},{1,9},{2,10},{3,11},{4,12},{5,13},{6,14},{7,15},{8,0},{9,1},... | collective-permute-start | bytes 196616 | tf_op jit(solution)/shard_map/ppermute | solution.py:25
  82.4 7.1 %collective-permute-start.22 = (bf16[2,128,128]{2,1,0:T(8,128)(2,1)S(1)}, bf16[2,128,128]{2,1,0:T(8,128)(2,1)S(1)}, u32[]{:S(2)}, u32[]{:S(2)}) collective-permute-start(bf16[2,128,128]{2,1,0:T(8,128)(2,1)S(1)} %chip.1.sent), channel_id=1, source_target_pairs={{0,16},{1,17},{2,18},{3,19},{4,20},{5,21},{6,22},{7,23},{8,24},{9,... | collective-permute-start | bytes 196616 | tf_op jit(solution)/shard_map/ppermute | solution.py:25
  82.4 7.1 %collective-permute-start.23 = (bf16[2,128,128]{2,1,0:T(8,128)(2,1)S(1)}, bf16[2,128,128]{2,1,0:T(8,128)(2,1)S(1)}, u32[]{:S(2)}, u32[]{:S(2)}) collective-permute-start(bf16[2,128,128]{2,1,0:T(8,128)(2,1)S(1)} %chip.1.sent), channel_id=1, source_target_pairs={{0,48},{1,49},{2,50},{3,51},{4,52},{5,53},{6,54},{7,55},{8,56},{9,... | collective-permute-start | bytes 196616 | tf_op jit(solution)/shard_map/ppermute | solution.py:25
  85.5 4.6 %collective-permute-start.24 = (bf16[2,128,128]{2,1,0:T(8,128)(2,1)S(1)}, bf16[2,128,128]{2,1,0:T(8,128)(2,1)S(1)}, u32[]{:S(2)}, u32[]{:S(2)}) collective-permute-start(bf16[2,128,128]{2,1,0:T(8,128)(2,1)S(1)} %chip.1.sent), channel_id=1, source_target_pairs={{0,32},{1,33},{2,34},{3,35},{4,36},{5,37},{6,38},{7,39},{8,40},{9,... | collective-permute-start | bytes 196616 | tf_op jit(solution)/shard_map/ppermute | solution.py:25
  86.6 8.6 %copy-start.1 = (f32[4,128,128]{2,1,0:T(8,128)S(1)}, f32[4,128,128]{2,1,0:T(8,128)}, u32[]{:S(2)}) copy-start(f32[4,128,128]{2,1,0:T(8,128)} %carried_ref.3) | copy-start | bytes 786436
  90.7 7.1 %collective-permute-start.25 = (bf16[2,128,128]{2,1,0:T(8,128)(2,1)S(1)}, bf16[2,128,128]{2,1,0:T(8,128)(2,1)S(1)}, u32[]{:S(2)}, u32[]{:S(2)}) collective-permute-start(bf16[2,128,128]{2,1,0:T(8,128)(2,1)S(1)} %get-tuple-element.75.sent), channel_id=1, source_target_pairs={{0,64},{1,65},{2,66},{3,67},{4,68},{5,69},{6,70},{7,71},{8,72},{9,... | collective-permute-start | bytes 196616 | tf_op jit(solution)/shard_map/ppermute | solution.py:25
  92.2 5.6 %collective-permute-start.26 = (bf16[2,128,128]{2,1,0:T(8,128)(2,1)S(1)}, bf16[2,128,128]{2,1,0:T(8,128)(2,1)S(1)}, u32[]{:S(2)}, u32[]{:S(2)}) collective-permute-start(bf16[2,128,128]{2,1,0:T(8,128)(2,1)S(1)} %get-tuple-element.75.sent), channel_id=1, source_target_pairs={{0,192},{1,193},{2,194},{3,195},{4,196},{5,197},{6,198},{7,199},{8... | collective-permute-start | bytes 196616 | tf_op jit(solution)/shard_map/ppermute | solution.py:25
  93.7 5.0 %collective-permute-start.27 = (bf16[2,128,128]{2,1,0:T(8,128)(2,1)S(1)}, bf16[2,128,128]{2,1,0:T(8,128)(2,1)S(1)}, u32[]{:S(2)}, u32[]{:S(2)}) collective-permute-start(bf16[2,128,128]{2,1,0:T(8,128)(2,1)S(1)} %get-tuple-element.75.sent), channel_id=1, source_target_pairs={{0,128},{1,129},{2,130},{3,131},{4,132},{5,133},{6,134},{7,135},{8... | collective-permute-start | bytes 196616 | tf_op jit(solution)/shard_map/ppermute | solution.py:25
  95.2 8.5 %copy-start.2 = (f32[512]{0:T(512)S(1)}, f32[512]{0:T(512)}, u32[]{:S(2)}) copy-start(f32[512]{0:T(512)} %param.12) | copy-start | bytes 6148
  99.4 4.3 %collective-permute-start.28 = (f32[2,2,128,128]{3,2,1,0:T(8,128)S(1)}, f32[2,2,128,128]{3,2,1,0:T(8,128)S(1)}, u32[]{:S(2)}, u32[]{:S(2)}) collective-permute-start(f32[2,2,128,128]{3,2,1,0:T(8,128)S(1)} %get-tuple-element.79), channel_id=1, source_target_pairs={{0,8},{1,9},{2,10},{3,11},{4,12},{5,13},{6,14},{7,15},{8,0},{9,1},... | collective-permute-start | bytes 786440 | tf_op jit(solution)/shard_map/ppermute | solution.py:25
